TPU v7x, 128 devices: a whole 4x4x4 slice. The times are simulated.
128 devices in a mesh: angle: 16 (over y, x), block: 8 (over z, core).
Axes of the slice: x: 4, y: 4, z: 4, core: 2. Of those that a mesh axis runs over, the one named last changes fastest.
Arguments:
- object_field: float32 [32, 2, 512, 512], P(None, None, 'block'), may hold values from -1.5 to 1.5
- shears: int32 [16, 32], P('angle'), may hold values from -16 to 16, as said below
- positions: int32 [16, 8, 2], P('angle', 'block'), may hold values from 0 to 511
- measured: bfloat16 [16, 8, 512, 512], P('angle', 'block'), may hold values from 0 to 2
- probe_field: float32 [2, 512, 512], replicated
- kappa_field: float32 [16, 512, 512], P('angle'), may hold values from 0.01 to 0.1
Outputs:
- updated_object: float32 [32, 2, 512, 512], P(None, None, 'block')
Inputs may be any that keep to these rules, and one draw needn't show every extreme that they name: `shears`: each angle's row offset of each slice; the values -16 and 16 occur in every draw.
All inputs are finite; a program needn't handle non-finite values.
Results may differ from a plain program's by a relative error of at most 0.0003.
Values sent between devices are 32-bit elements; how exact they have to be, the bound alone decides.
No kernel may reach another device: no remote copies, remote signals or barrier semaphores. Data moves between devices by JAX's collectives and lax.ppermute only.
A program may use at most 192 MiB of HBM per device.

v0:
```python
import jax
import jax.numpy as jnp
from jax import lax
from jax.sharding import PartitionSpec as P

NX = 512
NY = 512
STEPS = 2
SH = 16


def with_halo(x, sides, width):
    for axis, dim in sides:
        count, length = (lax.axis_size(axis), x.shape[dim])
        up = [(i, (i + 1) % count) for i in range(count)]
        down = [(j, i) for i, j in up]
        last = lax.slice_in_dim(x, length - width, length, axis=dim)
        first = lax.slice_in_dim(x, 0, width, axis=dim)
        before = lax.ppermute(last, axis, up)
        after = lax.ppermute(first, axis, down)
        x = jnp.concatenate([before, x, after], axis=dim)
    return x


def laplace(field):
    return (
        jnp.roll(field, 1, -2)
        + jnp.roll(field, -1, -2)
        + jnp.roll(field, 1, -1)
        + jnp.roll(field, -1, -1)
        - 4.0 * field
    )


def frame_loss(projected, probe_field, kappa_row, offset, observed):
    window = jnp.roll(projected, (-offset[0], -offset[1]), axis=(1, 2))
    real_part = probe_field[0] * window[0] - probe_field[1] * window[1]
    imag_part = probe_field[0] * window[1] + probe_field[1] * window[0]
    for step in range(STEPS):
        real_part, imag_part = (
            real_part - kappa_row * laplace(imag_part),
            imag_part + kappa_row * laplace(real_part),
        )
    misfit = real_part * real_part + imag_part * imag_part - observed.astype(jnp.float32)
    return 0.5 * jnp.sum(misfit * misfit)


def per_device(object_field, shears, positions, measured, probe_field, kappa_field):
    strip_rows = object_field.shape[2]
    shear_row = shears[0]
    extended = with_halo(object_field, (("block", 2),), SH)

    def slice_rows(slab, amount):
        return lax.dynamic_slice_in_dim(slab, SH + amount, strip_rows, 1)

    own_strip = jnp.sum(jax.vmap(slice_rows)(extended, shear_row), axis=0)
    projected = lax.all_gather(own_strip, "block", axis=1, tiled=True)
    intensity = probe_field[0] * probe_field[0] + probe_field[1] * probe_field[1]
    kappa_row = kappa_field[0]

    def per_frame(totals, frame_in):
        offset, observed = frame_in
        grads = jax.grad(frame_loss)(projected, probe_field, kappa_row, offset, observed)
        weight = jnp.roll(intensity, (offset[0], offset[1]), axis=(0, 1))
        return (totals + jnp.concatenate([grads, weight[None]], 0), None)

    totals, _ = lax.scan(
        per_frame, jnp.zeros((3, NX, NY), jnp.float32), (positions[0], measured[0])
    )
    strip_totals = lax.psum_scatter(totals, "block", scatter_dimension=1, tiled=True)
    gradient_rim = with_halo(strip_totals, (("block", 1),), SH)

    def unshear_rows(rim_block, amount):
        return lax.dynamic_slice_in_dim(rim_block, SH - amount, strip_rows, 1)

    unsheared = jax.vmap(lambda amount: unshear_rows(gradient_rim, amount))(shear_row)
    summed = lax.psum(unsheared, "angle")
    return object_field - summed[:, :2] / (summed[:, 2:3] + 1.0)


def solution(mesh):
    placed = (
        P(None, None, "block", None),
        P("angle", None),
        P("angle", "block", None),
        P("angle", "block", None, None),
        P(),
        P("angle", None, None),
    )
    return jax.shard_map(
        per_device,
        mesh=mesh,
        in_specs=placed,
        out_specs=P(None, None, "block", None),
        check_vma=False,
    )
```

profile of v0, /device:TPU:1, one launch (start us, length us, event | category | flops | bytes accessed | tf_op | source)
XLA Modules:
  0.0 588.5 jit_solution(2454463777330651448)
XLA Ops:
  6.5 14.3 %copy.27 = f32[32,2,64,512]{3,1,0,2:T(2,128)S(1)} copy(f32[32,2,64,512]{3,2,1,0:T(8,128)} %param.6) | data formatting | bytes 16777216 | tf_op args[0]
  20.9 2.3 fusion.41
  23.2 3.0 collective-permute-start
  26.2 23.0 %collective-permute-done = f32[32,2,16,512]{3,1,0,2:T(2,128)S(1)} collective-permute-done((f32[32,2,16,512]{3,1,0,2:T(2,128)S(1)}, f32[32,2,16,512]{3,1,0,2:T(2,128)S(1)}, u32[]{:S(2)}, u32[]{:S(2)}) %collective-permute-start) | collective-permute-done | bytes 2097184 | tf_op jit(solution)/shard_map/ppermute | solution.py:19
  49.2 2.5 collective-permute-done.1
  51.7 26.0 %pad_maximum_fusion = f32[32,2,96,512]{3,1,0,2:T(2,128)} fusion(f32[32,2,16,512]{3,1,0,2:T(2,128)S(1)} %collective-permute-done.1, f32[32,2,64,512]{3,1,0,2:T(2,128)S(1)} %copy.27, f32[32,2,16,512]{3,1,0,2:T(2,128)S(1)} %collective-permute-done), kind=kLoop, calls=%fused_computation.2 | loop fusion | flops 6291456 | bytes 25165824 | tf_op jit(solution)/shard_map/concatenate | solution.py:21
  77.7 16.2 %gather_fusion.1 = f32[32,2,64,512]{3,1,2,0:T(2,128)} fusion(f32[32,2,96,512]{3,1,0,2:T(2,128)} %pad_maximum_fusion, s32[32]{0:T(128)S(1)} %get-tuple-element.115), kind=kCustom, calls=%fused_computation.1 | custom fusion | bytes 16777728 | tf_op jit(solution)/shard_map/vmap()/gather | solution.py:54
  94.0 6.8 %reduce_sum.9 = f32[2,64,512]{2,0,1:T(2,128)} reduce(f32[32,2,64,512]{3,1,2,0:T(2,128)} %gather_fusion.1, f32[]{:T(128)} %constant.99.clone.1), dimensions={0}, to_apply=%region_0.0 | reduce | flops 2031616 | bytes 8650756 | tf_op jit(solution)/shard_map/reduce_sum | solution.py:56
  100.8 0.3 all-reduce.42.cloned.1.call-start
  101.1 0.6 fusion.75
  106.7 21.5 %all-gather.2.cloned.1.call-done = f32[2,512,512]{2,0,1:T(2,128)} async-done(((f32[2,64,512]{2,0,1:T(2,128)}), f32[2,512,512]{2,0,1:T(2,128)}) %all-gather.2.cloned.1.call-update) | async-done | bytes 2097168 | tf_op jit(solution)/shard_map/all_gather | solution.py:57
  128.2 5.6 fusion.3
  133.8 4.5 fusion.2
  138.3 1.6 fusion.42
  139.9 0.5 fusion.27
  140.4 0.4 fusion.71
  140.8 0.2 fusion.73
  141.2 0.4 copy-done
  141.6 12.8 %fusion.16 = (f32[512,512]{1,0:T(8,128)S(1)}, f32[512,512]{1,0:T(8,128)S(1)}) fusion(f32[511,512]{1,0:T(8,128)S(1)} %get-tuple-element.111, f32[1,512]{1,0:T(1,128)S(1)} %get-tuple-element.113, f32[1,512]{1,0:T(1,128)S(1)} %get-tuple-element.112, f32[511,512]{1,0:T(8,128)S(1)} %get-tuple-element.110, f32[512,511]{1,0:T(8,128)S(1)} %get-tuple-element.107, ...), kind=kLoop, calls=%fused_computation.35 | loop fusion | flops 3670016 | bytes 12582912 | tf_op jit(solution)/shard_map/while/body/eval_jaxpr/jvp()/sub | solution.py:41
  154.7 0.7 fusion.62
  155.4 0.3 fusion.60
  155.8 1.0 fusion.11
  156.8 0.2 fusion.64
  157.0 0.4 fusion.66
  157.6 0.2 copy-done.3
  157.8 2.3 bitcast_multiply_fusion.5
  160.1 0.4 bitcast_multiply_fusion.4
  160.6 0.4 fusion.56
  160.9 0.2 fusion.58
  161.3 1.2 bitcast_multiply_fusion.3
  162.5 0.4 fusion.52
  162.9 0.2 fusion.54
  163.3 0.4 fusion.48
  163.6 0.2 fusion.50
  164.0 2.4 fusion.34
  166.4 0.2 bitcast_multiply_fusion.2
  166.6 0.4 fusion.44
  167.0 0.2 fusion.46
  167.4 1.0 fusion.35
  168.4 0.5 fusion.31
  168.9 0.5 pad_add_fusion
  169.4 1.6 copy.31
  171.0 3.1 broadcast_in_dim.37
  174.1 96.8 %dynamic_update_slice.10 = f32[2,512,1024]{2,0,1:T(2,128)} dynamic-update-slice(f32[2,512,1024]{2,0,1:T(2,128)} %broadcast_in_dim.37, f32[2,512,512]{2,0,1:T(2,128)S(1)} %copy.31, s32[]{:T(128)} %constant.100.clone.1, s32[]{:T(128)} %constant.100.clone.1, s32[]{:T(128)S(6)} %select_n.79) | dynamic-update-slice | bytes 4194308 | tf_op jit(solution)/shard_map/while/body/eval_jaxpr/transpose(jvp(jit(_roll_dynamic)))/dynamic_update_slice | solution.py:36
  271.0 1.1 broadcast_in_dim.36
  272.1 1.1 copy-done.2
  273.1 1.2 fusion.4
  274.4 1.1 slice_add_fusion.1
  275.4 0.5 fusion.6
  275.9 0.6 fusion.5
  276.6 0.7 broadcast_in_dim.42
  277.3 3.9 pad_maximum_fusion.1
  281.3 0.6 dynamic-slice
  282.4 70.2 %all-reduce.42.cloned.1.call-done = f32[3,512,512]{2,0,1:T(4,128)} async-done(((f32[3,512,512]{2,0,1:T(4,128)}), f32[3,512,512]{2,0,1:T(4,128)}) %all-reduce.42.cloned.1.call-update) | async-done | bytes 3145744
  352.6 1.0 constant_dynamic-slice_fusion.1
  353.6 0.9 collective-permute-start.2
  354.5 1.6 collective-permute-start.3
  356.1 1.1 constant_dynamic-slice_fusion.2
  357.2 1.7 collective-permute-done.3
  359.1 12.4 %gather_fusion = f32[32,3,64,512]{3,1,2,0:T(4,128)} fusion(f32[3,96,512]{2,0,1:T(4,128)S(1)} %pad_maximum_fusion.2, s32[32]{0:T(128)S(1)} %get-tuple-element.114), kind=kCustom, calls=%fused_computation | custom fusion | bytes 25166208 | tf_op jit(solution)/shard_map/vmap()/gather | solution.py:74
  371.5 15.5 %copy.32 = f32[32,3,64,512]{3,2,1,0:T(8,128)} copy(f32[32,3,64,512]{3,1,2,0:T(4,128)} %gather_fusion) | data formatting | bytes 25165824 | tf_op jit(solution)/shard_map/vmap()/gather | solution.py:74
  387.0 182.1 %all-reduce.40.cloned.1.call-done = f32[32,3,64,512]{3,2,1,0:T(8,128)} async-done(((f32[32,3,64,512]{3,2,1,0:T(8,128)}), f32[32,3,64,512]{3,2,1,0:T(8,128)}) %all-reduce.40.cloned.1.call-update) | async-done | bytes 12582928 | tf_op jit(solution)/shard_map/psum | solution.py:77
  569.1 2.9 fusion.1
  572.0 9.6 %fusion = f32[32,2,64,512]{3,2,1,0:T(8,128)} fusion(f32[32,2,64,512]{3,2,1,0:T(8,128)} %param.6, f32[32,3,64,512]{3,2,1,0:T(8,128)} %all-reduce.40.cloned.1.call-done, f32[32,64,512]{2,1,0:T(8,128)S(1)} %fusion.1), kind=kLoop, calls=%fused_computation.4 | loop fusion | flops 4194304 | bytes 29360128 | tf_op jit(solution)/shard_map/sub | solution.py:78
  (34 shorter events, 1.4 us)
Async XLA Ops:
  6.5 121.6 %all-gather.2.cloned.1.call-start = ((), (), s32[]{:S(2)}) async-start(), calls=%async_computation | async-start | bytes 2359296 | tf_op jit(solution)/shard_map/all_gather | solution.py:57
  20.9 5.4 copy-start.5
  23.2 26.0 %collective-permute-start = (f32[32,2,16,512]{3,1,0,2:T(2,128)S(1)}, f32[32,2,16,512]{3,1,0,2:T(2,128)S(1)}, u32[]{:S(2)}, u32[]{:S(2)}) collective-permute-start(f32[32,2,16,512]{3,1,0,2:T(2,128)S(1)} %get-tuple-element.41), channel_id=1, source_target_pairs={{0,1},{1,2},{2,3},{3,4},{4,5},{5,6},{6,7},{7,0},{8,9},{9,10},{10,1... | collective-permute-start | bytes 6291464 | tf_op jit(solution)/shard_map/ppermute | solution.py:19
  26.2 25.5 %collective-permute-start.1 = (f32[32,2,16,512]{3,1,0,2:T(2,128)S(1)}, f32[32,2,16,512]{3,1,0,2:T(2,128)S(1)}, u32[]{:S(2)}, u32[]{:S(2)}) collective-permute-start(f32[32,2,16,512]{3,1,0,2:T(2,128)S(1)} %get-tuple-element.42), channel_id=1, source_target_pairs={{1,0},{2,1},{3,2},{4,3},{5,4},{6,5},{7,6},{0,7},{9,8},{10,9},{11,1... | collective-permute-start | bytes 6291464 | tf_op jit(solution)/shard_map/ppermute | solution.py:20
  94.0 7.2 %copy-start.4 = (s32[1,1,2]{2,1,0:T(1,128)S(1)}, s32[1,1,2]{2,1,0:T(1,128)}, u32[]{:S(2)}) copy-start(s32[1,1,2]{2,1,0:T(1,128)} %param.8) | copy-start | bytes 28
  100.8 251.8 %all-reduce.42.cloned.1.call-start = ((), (), s32[]{:S(2)}) async-start(), calls=%async_computation.2 | async-start | bytes 8388608
  133.8 6.1 %copy-start.1 = (f32[2,512,512]{2,1,0:T(8,128)S(1)}, f32[2,512,512]{2,1,0:T(8,128)}, u32[]{:S(2)}) copy-start(f32[2,512,512]{2,1,0:T(8,128)} %param.10) | copy-start | bytes 6291460
  140.4 1.2 copy-start
  156.8 1.0 copy-start.3
  271.0 2.2 copy-start.2
  277.3 4.0 copy-start.6
  281.2 287.9 %all-reduce.40.cloned.1.call-start = ((), (), s32[]{:S(2)}) async-start(), calls=%async_computation.1 | async-start | bytes 25165824 | tf_op jit(solution)/shard_map/psum | solution.py:77
  353.6 3.6 collective-permute-start.2
  354.5 4.4 collective-permute-start.3
Sparse Core Ops, SparseCore 0:
  100.9 27.1 all-gather.1
  281.4 71.2 all-reduce.41
  387.1 181.8 all-reduce.39
where the time goes:
time: 600 us; the launch traced here: 589 us
  waiting for transfers between devices  301 us (50%)
  local copies, waits for them, and re-layouts  177 us (30%)
  other arithmetic  85.6 us (14%)
  between operations  19.5 us (3%)
    psum x1, waiting for transfers between devices, per_device(): summed = lax.psum(unsheared, 'angle')  182 us
    dynamic_update_slice x1, local copies, waits for them, and re-layouts, frame_loss(): window = jnp.roll(projected, (-offset[0], -offset[1]), axis=(1, 2))  96.8 us
    unnamed x4, waiting for transfers between devices  70.2 us
    gather x2, local copies, waits for them, and re-layouts, unshear_rows(): return lax.dynamic_slice_in_dim(rim_block, SH - amount, strip_rows, 1)  27.9 us
    concatenate x2, other arithmetic, with_halo(): x = jnp.concatenate([before, x, after], axis=dim)  26.2 us
    ppermute x2, waiting for transfers between devices, with_halo(): before = lax.ppermute(last, axis, up)  23 us
    all_gather x1, waiting for transfers between devices, per_device(): projected = lax.all_gather(own_strip, 'block', axis=1, tiled=True)  21.5 us
    unnamed x17, local copies, waits for them, and re-layouts  17.8 us
  transfers between devices with their start and end apart: 7, of which 6 were waited for; matrix products, arithmetic and copies ran while one was open for 0% of the time, Pallas kernels for 0%

commit v1 on v0

v1 whole, which is shorter than its diff:
```python
import jax
import jax.numpy as jnp
from jax import lax
from jax.experimental import pallas as pl
from jax.experimental.pallas import tpu as pltpu
from jax.sharding import PartitionSpec as P

NX = 512
NY = 512
Z = 32
SH = 16
ANGLES = 16
FRAMES = 8
STRIP = 64
LANES = 128
COLS = NY // LANES
BASE = 24
ROWS = STRIP + 2 * BASE
RIM_ROWS = STRIP + 2 * SH
SENT = BASE + SH
WRAP = NX + ROWS
F32 = jnp.float32

SMEM = pl.BlockSpec(memory_space=pltpu.SMEM)
VMEM = pl.BlockSpec(memory_space=pltpu.VMEM)


def lane_block(c):
    return slice(c * LANES, (c + 1) * LANES)


def lane_ids(rows):
    return lax.broadcasted_iota(jnp.int32, (rows, LANES), 1)


def load_wrapped(scratch, index, image):
    for c in range(COLS):
        scratch[index + (c, pl.ds(0, NX))] = image[:, lane_block(c)]
        scratch[index + (c, pl.ds(NX, ROWS))] = image[:ROWS, lane_block(c)]


def rolled_blocks(scratch, index, first_row, rows, amount):
    whole, part = amount // LANES, amount % LANES
    turned = [
        pltpu.roll(scratch[index + ((c - whole) & (COLS - 1), pl.ds(first_row, rows))], part, 1)
        for c in range(COLS)
    ]
    keep = lane_ids(rows) >= part
    return [jnp.where(keep, turned[c], turned[c - 1]) for c in range(COLS)]


def measured_kernel(position, measured, out, wrapped):
    load_wrapped(wrapped, (), measured[...].astype(F32))
    for strip in range(FRAMES):
        first_row = (strip * STRIP - BASE - position[0]) & (NX - 1)
        for c, block in enumerate(rolled_blocks(wrapped, (), first_row, ROWS, position[1])):
            out[strip, c] = block


def project_kernel(shears, slices, out):
    step = pl.program_id(0)

    @pl.when(step == 0)
    def _():
        out[...] = jnp.zeros_like(out)

    count = slices.shape[0]
    for k in range(count):
        rows = pl.ds(SH - shears[step * count + k], STRIP)
        for part in range(2):
            for c in range(COLS):
                out[part, c, rows] += slices[k, part, :, lane_block(c)]


def frames_kernel(
    strip_index,
    positions,
    partial,
    before,
    after,
    measured,
    probe,
    kappa,
    out,
    wrapped,
    window,
    local,
    field_a,
    field_b,
    field_c,
):
    pad = 8
    load_wrapped(wrapped, (0,), probe[0])
    load_wrapped(wrapped, (1,), probe[1])
    load_wrapped(wrapped, (2,), kappa[...])
    window[:, :, pl.ds(BASE - SH, RIM_ROWS)] = partial[...]
    window[:, :, pl.ds(0, BASE - SH)] = jnp.zeros((2, COLS, BASE - SH, LANES), F32)
    window[:, :, pl.ds(ROWS - BASE + SH, BASE - SH)] = jnp.zeros((2, COLS, BASE - SH, LANES), F32)
    window[:, :, pl.ds(0, SENT)] += before[...]
    window[:, :, pl.ds(ROWS - SENT, SENT)] += after[...]
    out[...] = jnp.zeros_like(out)
    for field in (field_a, field_b, field_c):
        field[...] = jnp.zeros_like(field)
    tile = 16
    lanes = lane_ids(tile)
    first_lane = lanes == 0
    last_lane = lanes == LANES - 1

    def laplace(field, part, row):
        centre = [field[part, c, pl.ds(row, tile)] for c in range(COLS)]
        right = [pltpu.roll(v, 1, 1) for v in centre]
        left = [pltpu.roll(v, LANES - 1, 1) for v in centre]
        result = []
        for c in range(COLS):
            around = field[part, c, pl.ds(row - 1, tile)] + field[part, c, pl.ds(row + 1, tile)]
            around += jnp.where(first_lane, right[c - 1], right[c])
            around += jnp.where(last_lane, left[(c + 1) % COLS], left[c])
            result.append(around - 4.0 * centre[c])
        return centre, result

    def per_frame(frame, _):
        first_row = (strip_index[0] * STRIP - BASE - positions[frame, 0]) & (NX - 1)
        for k in range(3):
            for c, block in enumerate(
                rolled_blocks(wrapped, (k,), first_row, ROWS, positions[frame, 1])
            ):
                local[k, c] = block

        def over_rows(body):
            def one(i, _):
                row = pl.multiple_of(i * tile, tile)
                body(row, pl.multiple_of(row + pad, pad))
                return 0

            lax.fori_loop(0, ROWS // tile, one, 0)

        def leave(row, padded):
            for c in range(COLS):
                probe_re, probe_im = (local[k, c, pl.ds(row, tile)] for k in range(2))
                re, im = (window[k, c, pl.ds(row, tile)] for k in range(2))
                field_a[0, c, pl.ds(padded, tile)] = probe_re * re - probe_im * im
                field_a[1, c, pl.ds(padded, tile)] = probe_re * im + probe_im * re

        def forward(row, padded):
            re, lap_re = laplace(field_a, 0, padded)
            im, lap_im = laplace(field_a, 1, padded)
            for c in range(COLS):
                kappa_row = local[2, c, pl.ds(row, tile)]
                field_b[0, c, pl.ds(padded, tile)] = re[c] - kappa_row * lap_im[c]
                field_b[1, c, pl.ds(padded, tile)] = im[c] + kappa_row * lap_re[c]

        def turn(row, padded):
            re, lap_re = laplace(field_b, 0, padded)
            im, lap_im = laplace(field_b, 1, padded)
            for c in range(COLS):
                kappa_row = local[2, c, pl.ds(row, tile)]
                wave_re = re[c] - kappa_row * lap_im[c]
                wave_im = im[c] + kappa_row * lap_re[c]
                observed = measured[frame, c, pl.ds(row, tile)]
                twice = 2.0 * (wave_re * wave_re + wave_im * wave_im - observed)
                grad_re, grad_im = twice * wave_re, twice * wave_im
                field_a[0, c, pl.ds(padded, tile)] = grad_re
                field_a[1, c, pl.ds(padded, tile)] = grad_im
                field_c[0, c, pl.ds(padded, tile)] = kappa_row * grad_re
                field_c[1, c, pl.ds(padded, tile)] = kappa_row * grad_im

        def backward(row, padded):
            _, lap_re = laplace(field_c, 0, padded)
            _, lap_im = laplace(field_c, 1, padded)
            for c in range(COLS):
                kappa_row = local[2, c, pl.ds(row, tile)]
                grad_re = field_a[0, c, pl.ds(padded, tile)] + lap_im[c]
                grad_im = field_a[1, c, pl.ds(padded, tile)] - lap_re[c]
                field_a[0, c, pl.ds(padded, tile)] = grad_re
                field_a[1, c, pl.ds(padded, tile)] = grad_im
                field_b[0, c, pl.ds(padded, tile)] = kappa_row * grad_re
                field_b[1, c, pl.ds(padded, tile)] = kappa_row * grad_im

        def collect(i, _):
            row = pl.multiple_of(i * tile, tile)
            inner = pl.multiple_of(row + BASE - SH, pad)
            padded = pl.multiple_of(inner + pad, pad)
            _, lap_re = laplace(field_b, 0, padded)
            _, lap_im = laplace(field_b, 1, padded)
            for c in range(COLS):
                grad_re = field_a[0, c, pl.ds(padded, tile)] + lap_im[c]
                grad_im = field_a[1, c, pl.ds(padded, tile)] - lap_re[c]
                probe_re, probe_im = (local[k, c, pl.ds(inner, tile)] for k in range(2))
                out[0, c, pl.ds(row, tile)] += probe_re * grad_re + probe_im * grad_im
                out[1, c, pl.ds(row, tile)] += probe_re * grad_im - probe_im * grad_re
            return 0

        over_rows(leave)
        over_rows(forward)
        over_rows(turn)
        over_rows(backward)
        lax.fori_loop(0, RIM_ROWS // tile, collect, 0)
        return 0

    lax.fori_loop(0, FRAMES, per_frame, 0)


def weight_kernel(strip_index, positions, probe, out, wrapped):
    load_wrapped(wrapped, (), probe[0] * probe[0] + probe[1] * probe[1])

    def per_angle(angle, _):
        total = [jnp.zeros((RIM_ROWS, LANES), F32)] * COLS
        for frame in range(FRAMES):
            first_row = (strip_index[0] * STRIP - SH - positions[angle, frame, 0]) & (NX - 1)
            blocks = rolled_blocks(wrapped, (), first_row, RIM_ROWS, positions[angle, frame, 1])
            total = [a + b for a, b in zip(total, blocks)]
        for c in range(COLS):
            out[angle, c] = total[c]
        return 0

    lax.fori_loop(0, ANGLES, per_angle, 0)


def divisor_kernel(shears, weights, out):
    base = pl.program_id(0) * out.shape[0]

    def per_slice(k, _):
        starts = [SH - shears[a, base + k] for a in range(ANGLES)]
        for c in range(COLS):
            total = jnp.ones((STRIP, LANES), F32)
            for a in range(ANGLES):
                total += weights[a, c, pl.ds(starts[a], STRIP)]
            out[k, :, lane_block(c)] = 1.0 / total
        return 0

    lax.fori_loop(0, out.shape[0], per_slice, 0)


def update_kernel(shears, grads, slices, scale, out):
    base = pl.program_id(0) * out.shape[0]

    def per_slice(k, _):
        starts = [SH - shears[a, base + k] for a in range(ANGLES)]
        for part in range(2):
            for c in range(COLS):
                total = grads[0, part, c, pl.ds(starts[0], STRIP)]
                for a in range(1, ANGLES):
                    total += grads[a, part, c, pl.ds(starts[a], STRIP)]
                cols = lane_block(c)
                out[k, part, :, cols] = slices[k, part, :, cols] - total * scale[k, :, cols]
        return 0

    lax.fori_loop(0, out.shape[0], per_slice, 0)


def per_device(object_field, shears, positions, measured, probe_field, kappa_field):
    strip_index = lax.axis_index("block").astype(jnp.int32)[None]
    all_shears = lax.all_gather(shears[0], "angle", axis=0)
    all_positions = lax.all_gather(positions[0, 0], ("angle", "block"), axis=0)
    all_positions = all_positions.reshape(ANGLES, FRAMES, 2)
    own_positions = lax.dynamic_index_in_dim(
        all_positions, lax.axis_index("angle"), 0, keepdims=False
    )

    moved = pl.pallas_call(
        measured_kernel,
        out_shape=jax.ShapeDtypeStruct((FRAMES, COLS, ROWS, LANES), F32),
        in_specs=[SMEM, VMEM],
        out_specs=VMEM,
        scratch_shapes=[pltpu.VMEM((COLS, WRAP, LANES), F32)],
        name="measured_rows",
    )(positions[0, 0], measured[0, 0])
    observed = lax.all_to_all(moved, "block", 0, 0)

    step = 4
    partial = pl.pallas_call(
        project_kernel,
        grid=(Z // step,),
        out_shape=jax.ShapeDtypeStruct((2, COLS, RIM_ROWS, LANES), F32),
        in_specs=[SMEM, pl.BlockSpec((step, 2, STRIP, NY), lambda i: (i, 0, 0, 0))],
        out_specs=pl.BlockSpec((2, COLS, RIM_ROWS, LANES), lambda i: (0, 0, 0, 0)),
        name="project",
    )(shears[0], object_field)
    count = FRAMES
    up = [(i, (i + 1) % count) for i in range(count)]
    down = [(j, i) for i, j in up]
    before = lax.ppermute(partial[:, :, RIM_ROWS - SENT :], "block", up)
    after = lax.ppermute(partial[:, :, :SENT], "block", down)

    field = pltpu.VMEM((2, COLS, ROWS + 16, LANES), F32)
    grads = pl.pallas_call(
        frames_kernel,
        out_shape=jax.ShapeDtypeStruct((2, COLS, RIM_ROWS, LANES), F32),
        in_specs=[SMEM, SMEM] + [VMEM] * 6,
        out_specs=VMEM,
        scratch_shapes=[
            pltpu.VMEM((3, COLS, WRAP, LANES), F32),
            pltpu.VMEM((2, COLS, ROWS, LANES), F32),
            pltpu.VMEM((3, COLS, ROWS, LANES), F32),
            field,
            field,
            field,
        ],
        name="frames",
    )(
        strip_index,
        own_positions,
        partial,
        before,
        after,
        observed,
        probe_field,
        kappa_field[0],
    )

    weights = pl.pallas_call(
        weight_kernel,
        out_shape=jax.ShapeDtypeStruct((ANGLES, COLS, RIM_ROWS, LANES), F32),
        in_specs=[SMEM, SMEM, VMEM],
        out_specs=VMEM,
        scratch_shapes=[pltpu.VMEM((COLS, WRAP, LANES), F32)],
        name="weights",
    )(strip_index, all_positions, probe_field)
    slices_spec = pl.BlockSpec((step, STRIP, NY), lambda i: (i, 0, 0))
    scale = pl.pallas_call(
        divisor_kernel,
        grid=(Z // step,),
        out_shape=jax.ShapeDtypeStruct((Z, STRIP, NY), F32),
        in_specs=[SMEM, VMEM],
        out_specs=slices_spec,
        name="divisor",
    )(all_shears, weights)

    all_grads = lax.all_gather(grads, "angle", axis=0)
    object_spec = pl.BlockSpec((step, 2, STRIP, NY), lambda i: (i, 0, 0, 0))
    return pl.pallas_call(
        update_kernel,
        grid=(Z // step,),
        out_shape=jax.ShapeDtypeStruct(object_field.shape, F32),
        in_specs=[SMEM, VMEM, object_spec, slices_spec],
        out_specs=object_spec,
        name="update",
    )(all_shears, all_grads, object_field, scale)


def solution(mesh):
    placed = (
        P(None, None, "block", None),
        P("angle", None),
        P("angle", "block", None),
        P("angle", "block", None, None),
        P(),
        P("angle", None, None),
    )
    return jax.shard_map(
        per_device,
        mesh=mesh,
        in_specs=placed,
        out_specs=P(None, None, "block", None),
        check_vma=False,
    )
```

time: 600 us -> 182 us (0.30); the launches traced: 589 us -> 182 us
  waiting for transfers between devices: 301 us -> 19.7 us
  local copies, waits for them, and re-layouts: 177 us -> 2.95 us
  other arithmetic: 85.6 us -> 0 us
  Pallas kernels: 0 us -> 80.7 us
  blocking collectives: 0 us -> 56.1 us
  between operations: 19.5 us -> 13.4 us
    psum x1 -> x0, waiting for transfers between devices: 182 us -> none  [per_device(): summed = lax.psum(unsheared, 'angle')]
    dynamic_update_slice x1 -> x0, local copies, waits for them, and re-layouts: 96.8 us -> none  [frame_loss(): window = jnp.roll(projected, (-offset[0], -offset[1]), axis=(1, 2))]
    pallas_call x0 -> x6, Pallas kernels: none -> 80.7 us  [the longest x1 30.6 us: per_device(): pl.pallas_call(frames_kernel, out_shape=jax.ShapeDtypeStruct((2, COLS, RI...]
    unnamed x4 -> x1, waiting for transfers between devices: 70.2 us -> 0.02 us
    all_gather x0 -> x2, blocking collectives: none -> 56.1 us  [the longest x1 39.5 us: per_device(): all_positions = lax.all_gather(positions[0, 0], ('angle', 'block'), axis=0)]
    gather x3 -> x0, local copies, waits for them, and re-layouts: 44.2 us -> none  [the longest x2 27.9 us: unshear_rows(): return lax.dynamic_slice_in_dim(rim_block, SH - amount, strip_rows, 1)]
    concatenate x8 -> x0, other arithmetic: 41.3 us -> none  [the longest x2 26.2 us: with_halo(): x = jnp.concatenate([before, x, after], axis=dim)]
    ppermute x4 -> x2, waiting for transfers between devices: 27.1 us -> 0.01 us  [the longest x1 0.01 us: per_device(): after = lax.ppermute(partial[:, :, :SENT], 'block', down)]
  transfers between devices with their start and end apart: 7 -> 4, of which waited for: 6 -> 1; matrix products, arithmetic and copies ran while one was open for 0% -> 1% of each run, Pallas kernels for 0% -> 16%
where the time goes in v1:
time: 182 us
  Pallas kernels  80.7 us (44%)
  blocking collectives  56.1 us (31%)
  waiting for transfers between devices  19.7 us (11%)
  between operations  13.4 us (7%)
  starting transfers between devices  8.57 us (5%)
  local copies, waits for them, and re-layouts  2.95 us (2%)
    all_gather x1, blocking collectives, per_device(): all_positions = lax.all_gather(positions[0, 0], ('angle', 'block'), axis=0)  39.5 us
    pallas_call x1, Pallas kernels, per_device(): pl.pallas_call(frames_kernel, out_shape=jax.ShapeDtypeStruct((2, COLS, RI...  30.6 us
    all_gather x1, waiting for transfers between devices, per_device(): all_grads = lax.all_gather(grads, 'angle', axis=0)  19.7 us
    pallas_call x1, Pallas kernels, per_device(): pl.pallas_call(update_kernel, grid=(Z // step,), out_shape=jax.ShapeDtype...  18.4 us
    all_gather x1, blocking collectives, per_device(): all_shears = lax.all_gather(shears[0], 'angle', axis=0)  16.6 us
    pallas_call x1, Pallas kernels, per_device(): pl.pallas_call(weight_kernel, out_shape=jax.ShapeDtypeStruct((ANGLES, COL...  12 us
    pallas_call x1, Pallas kernels, per_device(): pl.pallas_call(divisor_kernel, grid=(Z // step,), out_shape=jax.ShapeDtyp...  9.9 us
    pallas_call x1, Pallas kernels, per_device(): pl.pallas_call(project_kernel, grid=(Z // step,), out_shape=jax.ShapeDtyp...  6.87 us
  transfers between devices with their start and end apart: 4, of which 1 were waited for; matrix products, arithmetic and copies ran while one was open for 1% of the time, Pallas kernels for 16%

profile of v1, /device:TPU:1, one launch (start us, length us, event | category | flops | bytes accessed | tf_op | source)
XLA Modules:
  0.0 181.5 jit_solution(15572546816635183882)
XLA Ops:
  6.5 2.9 %measured_rows.1 = f32[8,4,112,128]{3,2,1,0:T(8,128)} custom-call(s32[2]{0:T(128)} %bitcast.18, bf16[512,512]{1,0:T(8,128)(2,1)} %bitcast.13), custom_call_target="tpu_custom_call" | custom-call | tf_op jit(solution)/shard_map/measured_rows/pallas_call | solution.py:260
  9.4 6.8 %all-to-all-start = ((f32[8,4,112,128]{3,2,1,0:T(8,128)}), f32[8,4,112,128]{3,2,1,0:T(8,128)S(1)}, u32[]{:S(2)}, u32[]{:S(2)}) async-start(f32[8,4,112,128]{3,2,1,0:T(8,128)} %measured_rows.1), calls=%async_computation | async-start | bytes 3670016 | tf_op jit(solution)/shard_map/all_to_all | solution.py:268
  16.3 0.0 all-gather.5.cloned.1.call-start
  16.3 0.0 copy-start.4
  16.3 6.9 %project.1.partial = f32[2,4,96,128]{3,2,1,0:T(8,128)} custom-call(s32[32]{0:T(128)} %bitcast.19, f32[32,2,64,512]{3,2,1,0:T(8,128)} %slices.3), custom_call_target="tpu_custom_call" | custom-call | tf_op jit(solution)/shard_map/project/pallas_call | solution.py:271
  23.1 1.0 fusion
  24.2 0.1 collective-permute-start.1
  24.2 1.7 collective-permute-start
  25.9 0.0 copy-done.4
  25.9 39.5 %all-gather = s32[128,1,2]{2,1,0:T(1,128)S(1)} all-gather(s32[1,1,2]{2,1,0:T(1,128)S(1)} %copy-done.4), channel_id=2, replica_groups=mesh['angle'=16,'block'=8] {'angle','block'}, dimensions={0}, use_global_device_ids=true | all-gather | bytes 1032 | tf_op jit(solution)/shard_map/all_gather | solution.py:254
  65.4 0.0 copy-start.1
  65.4 0.6 dynamic-slice_bitcast_fusion.positions
  66.0 0.0 collective-permute-done.1.after
  66.0 0.0 copy-start.2
  66.0 0.0 collective-permute-done.before
  66.0 0.0 copy-start.3
  66.0 0.0 all-to-all-done.measured
  66.0 0.0 copy-start
  66.0 0.6 copy-done.2
  66.7 0.1 copy-done.3
  66.7 0.6 copy-done
  67.3 30.6 %frames.1 = f32[2,4,96,128]{3,2,1,0:T(8,128)} custom-call(s32[1]{0:T(128)} %bitcast.2.strip_index, s32[8,2]{1,0:T(8,128)} %dynamic-slice_bitcast_fusion.positions, f32[2,4,96,128]{3,2,1,0:T(8,128)} %project.1.partial, f32[2,4,40,128]{3,2,1,0:T(8,128)} %copy-done.3, f32[2,4,40,128]{3,2,1,0:T(8,128)} %copy-done.2, f32[8,4,112,128]{3,2,1,0:T(8,128)} %copy-done, ...), custom_call_target="tpu_custom_call" | custom-call | tf_op jit(solution)/shard_map/frames/pallas_call | solution.py:286
  98.0 0.0 copy-start.5
  98.0 0.0 all-gather.5.cloned.1.call-update
  98.0 0.0 copy-done.1
  98.0 12.0 %weights.1 = f32[16,4,96,128]{3,2,1,0:T(8,128)} custom-call(s32[1]{0:T(128)} %bitcast.2.strip_index, s32[16,8,2]{2,1,0:T(8,128)} %bitcast.15, f32[2,512,512]{2,1,0:T(8,128)} %probe.3), custom_call_target="tpu_custom_call" | custom-call | tf_op jit(solution)/shard_map/weights/pallas_call | solution.py:311
  110.0 0.0 copy-done.5
  110.0 16.6 %all-gather.2 = s32[16,1,32]{2,1,0:T(1,128)} all-gather(s32[1,1,32]{2,1,0:T(1,128)S(1)} %bitcast.20), channel_id=1, replica_groups=mesh['angle'=16,'block'=8] {'angle'}, dimensions={0}, use_global_device_ids=true | all-gather | bytes 2176 | tf_op jit(solution)/shard_map/all_gather | solution.py:253
  126.6 9.9 %divisor.1.scale = f32[32,64,512]{2,1,0:T(8,128)} custom-call(s32[16,32]{1,0:T(8,128)} %bitcast.16, f32[16,4,96,128]{3,2,1,0:T(8,128)} %weights.1), custom_call_target="tpu_custom_call" | custom-call | tf_op jit(solution)/shard_map/divisor/pallas_call | solution.py:320
  136.5 19.7 %all-gather.5.cloned.1.call-done = f32[32,4,96,128]{3,2,1,0:T(8,128)} async-done(((f32[2,4,96,128]{3,2,1,0:T(8,128)}), f32[32,4,96,128]{3,2,1,0:T(8,128)}) %all-gather.5.cloned.1.call-update) | async-done | bytes 6291472 | tf_op jit(solution)/shard_map/all_gather | solution.py:329
  156.2 18.4 %update.1 = f32[32,2,64,512]{3,2,1,0:T(8,128)} custom-call(s32[16,32]{1,0:T(8,128)} %bitcast.17, f32[16,2,4,96,128]{4,3,2,1,0:T(8,128)} %bitcast.11, f32[32,2,64,512]{3,2,1,0:T(8,128)} %slices.3, f32[32,64,512]{2,1,0:T(8,128)} %divisor.1.scale), custom_call_target="tpu_custom_call" | custom-call | tf_op jit(solution)/shard_map/update/pallas_call | solution.py:331
Async XLA Ops:
  9.4 56.6 %all-to-all-start = ((f32[8,4,112,128]{3,2,1,0:T(8,128)}), f32[8,4,112,128]{3,2,1,0:T(8,128)S(1)}, u32[]{:S(2)}, u32[]{:S(2)}) async-start(f32[8,4,112,128]{3,2,1,0:T(8,128)} %measured_rows.1), calls=%async_computation | async-start | bytes 3670016 | tf_op jit(solution)/shard_map/all_to_all | solution.py:268
  16.3 140.0 %all-gather.5.cloned.1.call-start = ((), (), s32[]{:S(2)}) async-start(), calls=%async_computation.1 | async-start | bytes 6684672 | tf_op jit(solution)/shard_map/all_gather | solution.py:329
  16.3 9.7 %copy-start.4 = (s32[1,1,2]{2,1,0:T(1,128)S(1)}, s32[1,1,2]{2,1,0:T(1,128)}, u32[]{:S(2)}) copy-start(s32[1,1,2]{2,1,0:T(1,128)} %param.8) | copy-start | bytes 28
  24.2 41.8 %collective-permute-start.1 = (f32[2,4,40,128]{3,2,1,0:T(8,128)S(1)}, f32[2,4,40,128]{3,2,1,0:T(8,128)S(1)}, u32[]{:S(2)}, u32[]{:S(2)}) collective-permute-start(f32[2,4,40,128]{3,2,1,0:T(8,128)S(1)} %get-tuple-element.5), channel_id=1, source_target_pairs={{1,0},{2,1},{3,2},{4,3},{5,4},{6,5},{7,6},{0,7},{9,8},{10,9},{11,1... | collective-permute-start | bytes 491528 | tf_op jit(solution)/shard_map/ppermute | solution.py:283
  24.2 41.8 %collective-permute-start = (f32[2,4,40,128]{3,2,1,0:T(8,128)S(1)}, f32[2,4,40,128]{3,2,1,0:T(8,128)S(1)}, u32[]{:S(2)}, u32[]{:S(2)}) collective-permute-start(f32[2,4,40,128]{3,2,1,0:T(8,128)S(1)} %get-tuple-element.6), channel_id=1, source_target_pairs={{0,1},{1,2},{2,3},{3,4},{4,5},{5,6},{6,7},{7,0},{8,9},{9,10},{10,1... | collective-permute-start | bytes 491528 | tf_op jit(solution)/shard_map/ppermute | solution.py:282
  65.4 32.6 %copy-start.1 = (s32[128,1,2]{2,1,0:T(1,128)}, s32[128,1,2]{2,1,0:T(1,128)S(1)}, u32[]{:S(2)}) copy-start(s32[128,1,2]{2,1,0:T(1,128)S(1)} %all-gather) | copy-start | bytes 3076
  66.0 0.7 copy-start.2
  66.0 0.7 copy-start.3
  66.0 1.3 copy-start
  98.0 12.0 %copy-start.5 = (s32[1,32]{1,0:T(1,128)S(1)}, s32[1,32]{1,0:T(1,128)}, u32[]{:S(2)}) copy-start(s32[1,32]{1,0:T(1,128)} %param.7) | copy-start | bytes 388
Sparse Core Ops, SparseCore 0:
  98.1 58.0 all-gather.4

commit v2 on v1

v2 whole, which is shorter than its diff:
```python
import jax
import jax.numpy as jnp
from jax import lax
from jax.experimental import pallas as pl
from jax.experimental.pallas import tpu as pltpu
from jax.sharding import PartitionSpec as P

NX = 512
NY = 512
Z = 32
SH = 16
ANGLES = 16
FRAMES = 8
STRIP = 64
LANES = 128
COLS = NY // LANES
BASE = 8
ROWS = STRIP + 2 * BASE
RIM_ROWS = STRIP + 2 * SH
SENT = BASE + SH
WRAP = NX + RIM_ROWS
F32 = jnp.float32
BF16 = jnp.bfloat16
HOPS = (0, 2, 1, 3)
SIDE = 4
COST_SCALE = 3_000_000

SMEM = pl.BlockSpec(memory_space=pltpu.SMEM)
VMEM = pl.BlockSpec(memory_space=pltpu.VMEM)


def cost(microseconds):
    return pl.CostEstimate(
        flops=0, transcendentals=0, bytes_accessed=microseconds * COST_SCALE
    )


def lane_block(c):
    return slice(c * LANES, (c + 1) * LANES)


def lane_ids(rows):
    return lax.broadcasted_iota(jnp.int32, (rows, LANES), 1)


def load_wrapped(scratch, index, image):
    for c in range(COLS):
        scratch[index + (c, pl.ds(0, NX))] = image[:, lane_block(c)]
        scratch[index + (c, pl.ds(NX, WRAP - NX))] = image[: WRAP - NX, lane_block(c)]


def rolled_blocks(scratch, index, first_row, rows, amount):
    whole, part = amount // LANES, amount % LANES
    turned = [
        pltpu.roll(scratch[index + ((c - whole) & (COLS - 1), pl.ds(first_row, rows))], part, 1)
        for c in range(COLS)
    ]
    keep = lane_ids(rows) >= part
    return [jnp.where(keep, turned[c], turned[c - 1]) for c in range(COLS)]


def interleave(transposed=False):
    old = lax.broadcasted_iota(jnp.int32, (NY, NY), 1 if transposed else 0)
    new = lax.broadcasted_iota(jnp.int32, (NY, NY), 0 if transposed else 1)
    return jnp.where(old == (new % LANES) * COLS + new // LANES, 1.0, 0.0).astype(BF16)


def permuted(image, matrix):
    result = None
    for term in range(3):
        high = image.astype(BF16)
        product = jnp.dot(high, matrix, preferred_element_type=F32)
        result = product if result is None else result + product
        if term < 2:
            image = image - high.astype(F32)
    return result


def interleaved_roll(scratch, index, first_row, rows, amount):
    whole, part = amount // COLS, amount % COLS
    return [
        pltpu.roll(
            scratch[index + ((c - part) & (COLS - 1), pl.ds(first_row, rows))],
            (whole + jnp.where(c < part, 1, 0)) & (LANES - 1),
            1,
        )
        for c in range(COLS)
    ]


def measured_kernel(position, measured, out, wrapped):
    load_wrapped(
        wrapped, (), jnp.dot(measured[...], interleave(), preferred_element_type=F32)
    )
    for strip in range(FRAMES):
        first_row = (strip * STRIP - BASE - position[0]) & (NX - 1)
        for c, block in enumerate(interleaved_roll(wrapped, (), first_row, ROWS, position[1])):
            out[strip, c] = block
        for k in range(2):
            out[strip, 0, k : k + 1] = jnp.full((1, LANES), position[k].astype(F32), F32)


def project_kernel(shears, slices, out):
    step = pl.program_id(0)

    @pl.when(step == 0)
    def _():
        out[...] = jnp.zeros_like(out)

    count = slices.shape[0]
    for k in range(count):
        rows = pl.ds(SH - shears[step * count + k], STRIP)
        for part in range(2):
            for c in range(COLS):
                out[part, c, rows] += slices[k, part, :, lane_block(c)]

    @pl.when(step == pl.num_programs(0) - 1)
    def _():
        matrix = interleave()
        for part in range(2):
            image = jnp.concatenate([out[part, c] for c in range(COLS)], axis=1)
            image = permuted(image, matrix)
            for c in range(COLS):
                out[part, c] = image[:, lane_block(c)]


def fields_kernel(probe, kappa, out):
    matrix = interleave()
    for k in range(3):
        load_wrapped(out, (k,), permuted(probe[k] if k < 2 else kappa[...], matrix))


def frames_kernel(
    strip_index,
    partial,
    before,
    after,
    measured,
    wrapped,
    out,
    window,
    local,
    field_a,
    field_b,
    field_c,
    total,
    positions,
):
    pad = 8
    for frame in range(FRAMES):
        for k in range(2):
            place = jnp.max(measured[frame, 0, k : k + 1])
            positions[frame, k] = place.astype(jnp.int32)
    window[...] = partial[:, :, SH - BASE : SH - BASE + ROWS]
    window[:, :, :SENT] += before[...]
    window[:, :, ROWS - SENT :] += after[...]
    total[...] = jnp.zeros_like(total)
    for field in (field_a, field_b, field_c):
        field[:, :, :pad] = jnp.zeros((2, COLS, pad, LANES), F32)
        field[:, :, pad + ROWS :] = jnp.zeros((2, COLS, pad, LANES), F32)
    tile = 16

    def laplace(field, part, row):
        centre = field[part, :, pl.ds(row, tile)]
        around = field[part, :, pl.ds(row - 1, tile)] + field[part, :, pl.ds(row + 1, tile)]
        left = jnp.concatenate([pltpu.roll(centre[COLS - 1 :], 1, 2), centre[: COLS - 1]], axis=0)
        right = jnp.concatenate([centre[1:], pltpu.roll(centre[:1], LANES - 1, 2)], axis=0)
        return centre, around + left + right - 4.0 * centre

    def per_frame(frame, _):
        first_row = (strip_index[0] * STRIP - BASE - positions[frame, 0]) & (NX - 1)
        for k in range(3):
            for c, block in enumerate(
                interleaved_roll(wrapped, (k,), first_row, ROWS, positions[frame, 1])
            ):
                local[k, c] = block
        tiles = range(0, ROWS, tile)
        for row in tiles:
            rows, padded = pl.ds(row, tile), pl.ds(row + pad, tile)
            probe_re, probe_im = local[0, :, rows], local[1, :, rows]
            re, im = window[0, :, rows], window[1, :, rows]
            field_a[0, :, padded] = probe_re * re - probe_im * im
            field_a[1, :, padded] = probe_re * im + probe_im * re
        for row in tiles:
            rows, padded = pl.ds(row, tile), pl.ds(row + pad, tile)
            re, lap_re = laplace(field_a, 0, row + pad)
            im, lap_im = laplace(field_a, 1, row + pad)
            kappa = local[2, :, rows]
            field_b[0, :, padded] = re - kappa * lap_im
            field_b[1, :, padded] = im + kappa * lap_re
        for row in tiles:
            rows, padded = pl.ds(row, tile), pl.ds(row + pad, tile)
            re, lap_re = laplace(field_b, 0, row + pad)
            im, lap_im = laplace(field_b, 1, row + pad)
            kappa = local[2, :, rows]
            wave_re = re - kappa * lap_im
            wave_im = im + kappa * lap_re
            twice = 2.0 * (wave_re * wave_re + wave_im * wave_im - measured[frame, :, rows])
            grad_re, grad_im = twice * wave_re, twice * wave_im
            field_a[0, :, padded] = grad_re
            field_a[1, :, padded] = grad_im
            field_c[0, :, padded] = kappa * grad_re
            field_c[1, :, padded] = kappa * grad_im
        for row in tiles:
            rows, padded = pl.ds(row, tile), pl.ds(row + pad, tile)
            _, lap_re = laplace(field_c, 0, row + pad)
            _, lap_im = laplace(field_c, 1, row + pad)
            kappa = local[2, :, rows]
            grad_re = field_a[0, :, padded] + lap_im
            grad_im = field_a[1, :, padded] - lap_re
            field_a[0, :, padded] = grad_re
            field_a[1, :, padded] = grad_im
            field_b[0, :, padded] = kappa * grad_re
            field_b[1, :, padded] = kappa * grad_im
        for row in range(0, STRIP, tile):
            rows, padded = pl.ds(row + BASE, tile), pl.ds(row + BASE + pad, tile)
            _, lap_re = laplace(field_b, 0, row + BASE + pad)
            _, lap_im = laplace(field_b, 1, row + BASE + pad)
            grad_re = field_a[0, :, padded] + lap_im
            grad_im = field_a[1, :, padded] - lap_re
            probe_re, probe_im = local[0, :, rows], local[1, :, rows]
            total[0, :, pl.ds(row, tile)] += probe_re * grad_re + probe_im * grad_im
            total[1, :, pl.ds(row, tile)] += probe_re * grad_im - probe_im * grad_re
        return 0

    lax.fori_loop(0, FRAMES, per_frame, 0)
    matrix = interleave(transposed=True)
    for part in range(2):
        image = jnp.concatenate([total[part, c] for c in range(COLS)], axis=1)
        image = permuted(image, matrix)
        for c in range(COLS):
            out[part, c] = image[:, lane_block(c)]


def weight_kernel(strip_index, positions, probe, out, wrapped):
    load_wrapped(wrapped, (), probe[0] * probe[0] + probe[1] * probe[1])
    chunk = 32

    def per_angle(angle, _):
        for row in range(0, RIM_ROWS, chunk):
            total = [jnp.zeros((chunk, LANES), F32)] * COLS
            for frame in range(FRAMES):
                first_row = (strip_index[0] * STRIP - SH - positions[angle, frame, 0]) & (NX - 1)
                blocks = rolled_blocks(
                    wrapped, (), first_row + row, chunk, positions[angle, frame, 1]
                )
                total = [a + b for a, b in zip(total, blocks)]
            for c in range(COLS):
                out[angle, c, row : row + chunk] = total[c]
        return 0

    lax.fori_loop(0, ANGLES, per_angle, 0)


def divisor_kernel(shears, weights, out):
    base = pl.program_id(0) * out.shape[0]

    def per_slice(k, _):
        starts = [SH - shears[a, base + k] for a in range(ANGLES)]
        for c in range(COLS):
            total = jnp.ones((STRIP, LANES), F32)
            for a in range(ANGLES):
                total += weights[a, c, pl.ds(starts[a], STRIP)]
            out[k, :, lane_block(c)] = 1.0 / total
        return 0

    lax.fori_loop(0, out.shape[0], per_slice, 0)


def split(values):
    high = values.astype(BF16)
    return high, (values - high.astype(F32)).astype(BF16)


def core_kernel(shears, own, two, one, three, slices, scale, out, grads):
    @pl.when(pl.program_id(0) == 0)
    def _():
        for k, piece in enumerate((own, two, one, three)):
            for j in range(SIDE):
                grads[SIDE * k + j, :, :, SH : SH + STRIP] = piece[j]
        grads[:, :, :, :SH] = jnp.zeros((ANGLES, 2, COLS, SH, LANES), F32)
        grads[:, :, :, SH + STRIP :] = jnp.zeros((ANGLES, 2, COLS, SH, LANES), F32)

    base = pl.program_id(0) * out.shape[0]

    def per_slice(k, _):
        starts = [SH - shears[a, base + k] for a in range(ANGLES)]
        for part in range(2):
            for c in range(COLS):
                total = grads[0, part, c, pl.ds(starts[0], STRIP)]
                for a in range(1, ANGLES):
                    total += grads[a, part, c, pl.ds(starts[a], STRIP)]
                cols = lane_block(c)
                out[k, part, :, cols] = slices[k, part, :, cols] - total * scale[k, :, cols]
        return 0

    lax.fori_loop(0, out.shape[0], per_slice, 0)


def rim_kernel(shears, before, after, scale, core, out, high, low, shifts):
    side = pl.program_id(0)

    def take(rim):
        for a in range(ANGLES):
            for part in range(2):
                for c in range(COLS):
                    rows, cols = slice(a * SH, (a + 1) * SH), lane_block(part * COLS + c)
                    high[rows, cols], low[rows, cols] = split(rim[a, part, c])

    @pl.when((pl.program_id(1) == 0) & (side == 0))
    def _():
        take(before)

    @pl.when((pl.program_id(1) == 0) & (side == 1))
    def _():
        take(after)

    count = out.shape[0]
    width = ANGLES * SH
    column = lax.broadcasted_iota(jnp.int32, (SH, width), 1) & (SH - 1)
    apart = column - lax.broadcasted_iota(jnp.int32, (SH, width), 0)
    middle = jnp.where(side == 0, SH, -SH)
    for k in range(count):
        chosen = jnp.where(apart == middle - shears[k : k + 1], 1.0, 0.0)
        shifts[k * SH : (k + 1) * SH] = chosen.astype(BF16)
    product = jnp.dot(shifts[...], high[...], preferred_element_type=F32)
    product += jnp.dot(shifts[...], low[...], preferred_element_type=F32)
    for k in range(count):
        for part in range(2):
            total = product[k * SH : (k + 1) * SH, part * NY : (part + 1) * NY]
            out[k, part] = core[k, part] - total * scale[k]


def hop_pairs(hop, stage):
    pairs = []
    for y in range(SIDE):
        for x in range(SIDE):
            for block in range(FRAMES):
                along_x = (block % 2 == 0) == (stage == 0)
                to_y = y if along_x else (y + hop) % SIDE
                to_x = (x + hop) % SIDE if along_x else x
                pairs.append(((y * SIDE + x) * FRAMES + block, (to_y * SIDE + to_x) * FRAMES + block))
    return pairs


def gather_angles(grads, facts):
    axes = ("angle", "block")
    row = [grads] + [lax.ppermute(grads, axes, hop_pairs(hop, 0)) for hop in HOPS[1:]]
    row, facts = lax.optimization_barrier((jnp.stack(row), facts))
    pieces = [row] + [lax.ppermute(row, axes, hop_pairs(hop, 1)) for hop in HOPS[1:]]
    angle = lax.axis_index("angle")
    y, x = angle // SIDE, angle % SIDE
    odd = lax.axis_index("block") % 2
    second, first = (jnp.asarray(HOPS).repeat(SIDE), jnp.asarray(HOPS * SIDE))
    along_x = jnp.where(odd == 1, second, first)
    along_y = jnp.where(odd == 1, first, second)
    order = ((y - along_y) % SIDE) * SIDE + (x - along_x) % SIDE
    return pieces, order.astype(jnp.int32), facts


def per_device(object_field, shears, positions, measured, probe_field, kappa_field):
    strip_index = lax.axis_index("block").astype(jnp.int32)[None]
    moved = pl.pallas_call(
        measured_kernel,
        out_shape=jax.ShapeDtypeStruct((FRAMES, COLS, ROWS, LANES), F32),
        in_specs=[SMEM, VMEM],
        out_specs=VMEM,
        scratch_shapes=[pltpu.VMEM((COLS, WRAP, LANES), F32)],
        cost_estimate=cost(3),
        name="measured_rows",
    )(positions[0, 0], measured[0, 0])
    observed = lax.all_to_all(moved, "block", 0, 0)
    facts = observed[:, 0, :2, 0].reshape(2 * FRAMES).astype(jnp.int32)
    facts = jnp.pad(jnp.concatenate([facts, shears[0]]), (0, LANES - 2 * FRAMES - Z))
    facts = jnp.broadcast_to(facts, (ANGLES, 8, LANES))
    facts, observed = lax.optimization_barrier((facts, observed))

    step = 4
    partial = pl.pallas_call(
        project_kernel,
        grid=(Z // step,),
        out_shape=jax.ShapeDtypeStruct((2, COLS, RIM_ROWS, LANES), F32),
        in_specs=[SMEM, pl.BlockSpec((step, 2, STRIP, NY), lambda i: (i, 0, 0, 0))],
        out_specs=pl.BlockSpec((2, COLS, RIM_ROWS, LANES), lambda i: (0, 0, 0, 0)),
        cost_estimate=cost(7),
        name="project",
    )(shears[0], object_field)
    count = FRAMES
    up = [(i, (i + 1) % count) for i in range(count)]
    down = [(j, i) for i, j in up]
    before = lax.ppermute(partial[:, :, RIM_ROWS - SENT :], "block", up)
    after = lax.ppermute(partial[:, :, :SENT], "block", down)
    wrapped = pl.pallas_call(
        fields_kernel,
        out_shape=jax.ShapeDtypeStruct((3, COLS, WRAP, LANES), F32),
        in_specs=[VMEM, VMEM],
        out_specs=VMEM,
        cost_estimate=cost(6),
        name="fields",
    )(probe_field, kappa_field[0])

    field = pltpu.VMEM((2, COLS, ROWS + 16, LANES), F32)
    grads = pl.pallas_call(
        frames_kernel,
        out_shape=jax.ShapeDtypeStruct((2, COLS, STRIP, LANES), F32),
        in_specs=[SMEM] + [VMEM] * 5,
        out_specs=VMEM,
        scratch_shapes=[
            pltpu.VMEM((2, COLS, ROWS, LANES), F32),
            pltpu.VMEM((3, COLS, ROWS, LANES), F32),
            field,
            field,
            field,
            pltpu.VMEM((2, COLS, STRIP, LANES), F32),
            pltpu.SMEM((FRAMES, 2), jnp.int32),
        ],
        cost_estimate=cost(9),
        name="frames",
    )(strip_index, partial, before, after, observed, wrapped)
    facts, grads = lax.optimization_barrier((facts, grads))
    facts = lax.all_to_all(facts, "angle", 0, 0)
    pieces, order, facts = gather_angles(grads, facts)
    facts = facts[:, 0]
    all_positions = facts[:, : 2 * FRAMES].reshape(ANGLES, FRAMES, 2)
    all_shears = facts[:, 2 * FRAMES : 2 * FRAMES + Z]
    ordered_shears = jnp.take(all_shears, order, axis=0)
    rim_shears = ordered_shears.reshape(SIDE, SIDE, Z).transpose(2, 1, 0).reshape(Z, ANGLES)
    rim_shears = jnp.repeat(rim_shears, SH, axis=1)
    weights = pl.pallas_call(
        weight_kernel,
        out_shape=jax.ShapeDtypeStruct((ANGLES, COLS, RIM_ROWS, LANES), F32),
        in_specs=[SMEM, SMEM, VMEM],
        out_specs=VMEM,
        scratch_shapes=[pltpu.VMEM((COLS, WRAP, LANES), F32)],
        cost_estimate=cost(2),
        name="weights",
    )(strip_index, all_positions, probe_field)
    slices_spec = pl.BlockSpec((step, STRIP, NY), lambda i: (i, 0, 0))
    scale = pl.pallas_call(
        divisor_kernel,
        grid=(Z // step,),
        out_shape=jax.ShapeDtypeStruct((Z, STRIP, NY), F32),
        in_specs=[SMEM, VMEM],
        out_specs=slices_spec,
        cost_estimate=cost(2),
        name="divisor",
    )(all_shears, weights)

    scale, *pieces = lax.optimization_barrier((scale, *pieces))
    rims = [
        jnp.concatenate([piece[..., rows, :] for piece in pieces])
        for rows in (slice(STRIP - SH, STRIP), slice(0, SH))
    ]
    rims = [lax.ppermute(rim, "block", pairs) for rim, pairs in zip(rims, (up, down))]

    object_spec = pl.BlockSpec((step, 2, STRIP, NY), lambda i: (i, 0, 0, 0))
    core = pl.pallas_call(
        core_kernel,
        grid=(Z // step,),
        out_shape=jax.ShapeDtypeStruct(object_field.shape, F32),
        in_specs=[SMEM] + [VMEM] * 4 + [object_spec, slices_spec],
        out_specs=object_spec,
        scratch_shapes=[pltpu.VMEM((ANGLES, 2, COLS, RIM_ROWS, LANES), F32)],
        cost_estimate=cost(17),
        name="core",
    )(ordered_shears, *pieces, object_field, scale)
    many = 16
    edge_spec = pl.BlockSpec((many, 2, SH, NY), lambda j, i: (i, 0, j * (STRIP // SH - 1), 0))
    return pl.pallas_call(
        rim_kernel,
        grid=(2, Z // many),
        out_shape=jax.ShapeDtypeStruct(object_field.shape, F32),
        in_specs=[pl.BlockSpec((many, ANGLES * SH), lambda j, i: (i, 0)), VMEM, VMEM]
        + [pl.BlockSpec((many, SH, NY), lambda j, i: (i, j * (STRIP // SH - 1), 0)), edge_spec],
        out_specs=edge_spec,
        scratch_shapes=[
            pltpu.VMEM((ANGLES * SH, 2 * NY), BF16),
            pltpu.VMEM((ANGLES * SH, 2 * NY), BF16),
            pltpu.VMEM((many * SH, ANGLES * SH), BF16),
        ],
        input_output_aliases={4: 0},
        cost_estimate=cost(9),
        name="rim",
    )(rim_shears, *rims, scale, core)


def solution(mesh):
    placed = (
        P(None, None, "block", None),
        P("angle", None),
        P("angle", "block", None),
        P("angle", "block", None, None),
        P(),
        P("angle", None, None),
    )
    return jax.shard_map(
        per_device,
        mesh=mesh,
        in_specs=placed,
        out_specs=P(None, None, "block", None),
        check_vma=False,
    )
```

time: 182 us -> 122 us (0.67)
  blocking collectives: 56.1 us -> 0 us
  starting transfers between devices: 8.57 us -> 25.3 us
  between operations: 13.4 us -> 0.16 us
  waiting for transfers between devices: 19.7 us -> 9.58 us
  Pallas kernels: 80.7 us -> 72.1 us
  local copies, waits for them, and re-layouts: 2.95 us -> 8.16 us
  other arithmetic: 0 us -> 4.45 us
    all_gather x2 -> x0, blocking collectives: 56.1 us -> none  [the longest x1 39.5 us: per_device(): all_positions = lax.all_gather(positions[0, 0], ('angle', 'block'), axis=0)]
    all_gather x1 -> x0, waiting for transfers between devices: 19.7 us -> none  [per_device(): all_grads = lax.all_gather(grads, 'angle', axis=0)]
    ppermute x0 -> x8, starting transfers between devices: none -> 11.3 us  [the longest x2 4.41 us: per_device(): lax.ppermute(rim, 'block', pairs)]
    pallas_call x2 -> x4, Pallas kernels: 49.1 us -> 40.9 us  [the longest x1 18.2 us: per_device(): pl.pallas_call(core_kernel, grid=(Z // step,), out_shape=jax.ShapeDtypeSt...]
    all_to_all x0 -> x1, starting transfers between devices: none -> 5.46 us  [per_device(): facts = lax.all_to_all(facts, 'angle', 0, 0)]
    ppermute x0 -> x8, waiting for transfers between devices: none -> 5.42 us  [the longest x3 2.77 us: gather_angles(): lax.ppermute(row, axes, hop_pairs(hop, 1))]
    all_to_all x0 -> x1, waiting for transfers between devices: none -> 2.81 us  [per_device(): facts = lax.all_to_all(facts, 'angle', 0, 0)]
    slice x0 -> x4, local copies, waits for them, and re-layouts: none -> 2.36 us  [the longest x2 1.62 us: per_device(): piece[..., rows, :]]
  transfers between devices with their start and end apart: 4 -> 12, of which waited for: 1 -> 4; matrix products, arithmetic and copies ran while one was open for 1% -> 7% of each run, Pallas kernels for 16% -> 44%
where the time goes in v2:
time: 122 us; the launch traced here: 120 us
  Pallas kernels  72.1 us (59%)
  starting transfers between devices  25.3 us (21%)
  waiting for transfers between devices  9.58 us (8%)
  local copies, waits for them, and re-layouts  8.16 us (7%)
  other arithmetic  4.45 us (4%)
    pallas_call x1, Pallas kernels, per_device(): pl.pallas_call(core_kernel, grid=(Z // step,), out_shape=jax.ShapeDtypeSt...  18.2 us
    pallas_call x1, Pallas kernels, per_device(): pl.pallas_call(weight_kernel, out_shape=jax.ShapeDtypeStruct((ANGLES, COL...  11.4 us
    pallas_call x1, Pallas kernels, per_device(): pl.pallas_call(frames_kernel, out_shape=jax.ShapeDtypeStruct((2, COLS, ST...  9.37 us
    pallas_call x1, Pallas kernels, per_device(): pl.pallas_call(divisor_kernel, grid=(Z // step,), out_shape=jax.ShapeDtyp...  9.33 us
    pallas_call x1, Pallas kernels, per_device(): pl.pallas_call(project_kernel, grid=(Z // step,), out_shape=jax.ShapeDtyp...  7.52 us
    pallas_call x1, Pallas kernels, per_device(): pl.pallas_call(rim_kernel, grid=(2, Z // many), out_shape=jax.ShapeDtypeS...  6.93 us
    all_to_all x1, starting transfers between devices, per_device(): observed = lax.all_to_all(moved, 'block', 0, 0)  6.81 us
    pallas_call x1, Pallas kernels, per_device(): pl.pallas_call(fields_kernel, out_shape=jax.ShapeDtypeStruct((3, COLS, WR...  6.35 us
  transfers between devices with their start and end apart: 12, of which 4 were waited for; matrix products, arithmetic and copies ran while one was open for 7% of the time, Pallas kernels for 44%

profile of v2, /device:TPU:1, one launch (start us, length us, event | category | flops | bytes accessed | tf_op | source)
XLA Modules:
  0.0 119.7 jit_solution(3336946807830220876)
XLA Ops:
  0.0 3.0 %measured_rows.1 = f32[8,4,80,128]{3,2,1,0:T(8,128)} custom-call(s32[2]{0:T(128)} %bitcast.31, bf16[512,512]{1,0:T(8,128)(2,1)} %bitcast.21), custom_call_target="tpu_custom_call" | custom-call | bytes 9000000 | tf_op jit(solution)/shard_map/measured_rows/pallas_call | solution.py:363
  3.0 6.8 %all-to-all-start = ((f32[8,4,80,128]{3,2,1,0:T(8,128)}), f32[8,4,80,128]{3,2,1,0:T(8,128)S(1)}, u32[]{:S(2)}, u32[]{:S(2)}) async-start(f32[8,4,80,128]{3,2,1,0:T(8,128)} %measured_rows.1), calls=%async_computation | async-start | bytes 2621440 | tf_op jit(solution)/shard_map/all_to_all | solution.py:372
  9.8 7.5 %project.1.partial = f32[2,4,96,128]{3,2,1,0:T(8,128)} custom-call(s32[32]{0:T(128)} %bitcast.29, f32[32,2,64,512]{3,2,1,0:T(8,128)} %slices.3), custom_call_target="tpu_custom_call" | custom-call | bytes 21000000 | tf_op jit(solution)/shard_map/project/pallas_call | solution.py:379
  17.3 1.0 fusion.9
  18.3 0.0 collective-permute-start.1
  18.3 1.7 %collective-permute-start = (f32[2,4,24,128]{3,2,1,0:T(8,128)S(1)}, f32[2,4,24,128]{3,2,1,0:T(8,128)S(1)}, u32[]{:S(2)}, u32[]{:S(2)}) collective-permute-start(f32[2,4,24,128]{3,2,1,0:T(8,128)S(1)} %get-tuple-element.38), channel_id=1, source_target_pairs={{0,1},{1,2},{2,3},{3,4},{4,5},{5,6},{6,7},{7,0},{8,9},{9,10},{10,1... | collective-permute-start | bytes 294920 | tf_op jit(solution)/shard_map/ppermute | solution.py:391
  20.0 6.3 %fields.1.wrapped = f32[3,4,608,128]{3,2,1,0:T(8,128)} custom-call(f32[2,512,512]{2,1,0:T(8,128)} %probe.3, f32[512,512]{1,0:T(8,128)} %bitcast.18), custom_call_target="tpu_custom_call" | custom-call | bytes 18000000 | tf_op jit(solution)/shard_map/fields/pallas_call | solution.py:393
  26.4 1.4 %all-to-all-done.measured = f32[8,4,80,128]{3,2,1,0:T(8,128)S(1)} async-done(((f32[8,4,80,128]{3,2,1,0:T(8,128)}), f32[8,4,80,128]{3,2,1,0:T(8,128)S(1)}, u32[]{:S(2)}, u32[]{:S(2)}) %all-to-all-start) | async-done | bytes 1310752 | tf_op jit(solution)/shard_map/all_to_all | solution.py:372
  27.7 0.2 fusion
  28.0 0.1 convert_element_type.7
  28.0 0.0 copy-done.9
  28.0 0.1 pad_add_fusion
  28.1 0.7 broadcast_in_dim.33
  28.8 0.0 collective-permute-done.1.after
  28.8 0.0 collective-permute-done.before
  28.8 0.0 copy-start.7
  28.8 0.0 copy-done.1
  28.9 0.6 copy-done.6
  29.5 0.0 copy-done.7
  29.5 9.4 %frames.1 = f32[2,4,64,128]{3,2,1,0:T(8,128)} custom-call(s32[1]{0:T(128)} %bitcast.3.strip_index, f32[2,4,96,128]{3,2,1,0:T(8,128)} %project.1.partial, f32[2,4,24,128]{3,2,1,0:T(8,128)} %copy-done.7, f32[2,4,24,128]{3,2,1,0:T(8,128)} %copy-done.6, f32[8,4,80,128]{3,2,1,0:T(8,128)} %copy-done.1, f32[3,4,608,128]{3,2,1,0:T(8,128)} %fields.1.wrapped), custom_call_target="tpu_custom_call" | custom-call | bytes 27000000 | tf_op jit(solution)/shard_map/frames/pallas_call | solution.py:403
  38.9 2.7 %collective-permute-start.4 = (f32[2,4,64,128]{3,2,1,0:T(8,128)}, f32[2,4,64,128]{3,2,1,0:T(8,128)S(1)}, u32[]{:S(2)}, u32[]{:S(2)}) collective-permute-start(f32[2,4,64,128]{3,2,1,0:T(8,128)} %frames.1), channel_id=1, source_target_pairs={{0,24},{1,97},{2,26},{3,99},{4,28},{5,101},{6,30},{7,103},{8,0},{9... | collective-permute-start | bytes 786440 | tf_op jit(solution)/shard_map/ppermute | solution.py:348
  41.6 0.0 collective-permute-start.3
  41.6 1.6 %collective-permute-start.2 = (f32[2,4,64,128]{3,2,1,0:T(8,128)}, f32[2,4,64,128]{3,2,1,0:T(8,128)S(1)}, u32[]{:S(2)}, u32[]{:S(2)}) collective-permute-start(f32[2,4,64,128]{3,2,1,0:T(8,128)} %frames.1), channel_id=1, source_target_pairs={{0,16},{1,65},{2,18},{3,67},{4,20},{5,69},{6,22},{7,71},{8,24},{9,... | collective-permute-start | bytes 786440 | tf_op jit(solution)/shard_map/ppermute | solution.py:348
  43.3 5.5 %all-to-all-start.1 = ((s32[16,8,128]{2,1,0:T(8,128)}), s32[16,8,128]{2,1,0:T(8,128)S(1)}, u32[]{:S(2)}, u32[]{:S(2)}) async-start(s32[16,8,128]{2,1,0:T(8,128)} %broadcast_in_dim.33), calls=%async_computation.1 | async-start | bytes 131072 | tf_op jit(solution)/shard_map/all_to_all | solution.py:421
  48.7 0.0 collective-permute-done.4
  48.7 2.6 %collective-permute-done.3 = f32[2,4,64,128]{3,2,1,0:T(8,128)S(1)} collective-permute-done((f32[2,4,64,128]{3,2,1,0:T(8,128)}, f32[2,4,64,128]{3,2,1,0:T(8,128)S(1)}, u32[]{:S(2)}, u32[]{:S(2)}) %collective-permute-start.3) | collective-permute-done | bytes 262176 | tf_op jit(solution)/shard_map/ppermute | solution.py:348
  51.4 0.0 collective-permute-done.2
  51.4 1.0 pad_maximum_fusion.own
  52.4 0.0 copy-start
  52.4 2.8 %all-to-all-done.1 = s32[16,8,128]{2,1,0:T(8,128)S(1)} async-done(((s32[16,8,128]{2,1,0:T(8,128)}), s32[16,8,128]{2,1,0:T(8,128)S(1)}, u32[]{:S(2)}, u32[]{:S(2)}) %all-to-all-start.1) | async-done | bytes 65568 | tf_op jit(solution)/shard_map/all_to_all | solution.py:421
  55.2 1.0 collective-permute-start.7
  56.2 0.5 collective-permute-start.6
  56.7 1.0 collective-permute-start.5
  57.8 0.7 slice.62.shears
  58.4 0.1 copy.18
  58.5 0.7 copy.19.positions
  59.2 11.4 %weights.1 = f32[16,4,96,128]{3,2,1,0:T(8,128)} custom-call(s32[1]{0:T(128)} %bitcast.3.strip_index, s32[16,8,2]{2,1,0:T(8,128)} %copy.19.positions, f32[2,512,512]{2,1,0:T(8,128)} %probe.3), custom_call_target="tpu_custom_call" | custom-call | bytes 6000000 | tf_op jit(solution)/shard_map/weights/pallas_call | solution.py:429
  70.6 9.3 %divisor.1.scale = f32[32,64,512]{2,1,0:T(8,128)} custom-call(s32[16,32]{1,0:T(8,128)} %slice.62.shears, f32[16,4,96,128]{3,2,1,0:T(8,128)} %weights.1), custom_call_target="tpu_custom_call" | custom-call | bytes 6000000 | tf_op jit(solution)/shard_map/divisor/pallas_call | solution.py:439
  79.9 0.0 collective-permute-done.7.three
  80.0 0.0 copy-start.2
  80.0 2.8 %collective-permute-done.6.one = f32[4,2,4,64,128]{4,3,2,1,0:T(8,128)S(1)} collective-permute-done((f32[4,2,4,64,128]{4,3,2,1,0:T(8,128)S(1)}, f32[4,2,4,64,128]{4,3,2,1,0:T(8,128)S(1)}, u32[]{:S(2)}, u32[]{:S(2)}) %collective-permute-start.6) | collective-permute-done | bytes 1048608 | tf_op jit(solution)/shard_map/ppermute | solution.py:350
  82.7 0.0 collective-permute-done.5.two
  82.7 1.5 %fusion.5 = (f32[4,2,4,16,128]{4,3,2,1,0:T(8,128)S(1)}, f32[4,2,4,16,128]{4,3,2,1,0:T(8,128)S(1)}, f32[4,2,4,16,128]{4,3,2,1,0:T(8,128)S(1)}, f32[4,2,4,16,128]{4,3,2,1,0:T(8,128)S(1)}) fusion(f32[4,2,4,64,128]{4,3,2,1,0:T(8,128)S(1)} %pad_maximum_fusion.own, f32[4,2,4,64,128]{4,3,2,1,0:T(8,128)} %collective-permute-done.5.two), kind=kLoop, calls=%fused_computation.25 | loop fusion | bytes 2097152 | tf_op jit(solution)/shard_map/slice | solution.py:451
  84.3 0.1 fusion.7
  84.4 1.1 pad_maximum_fusion.1
  85.5 4.2 %collective-permute-start.8 = (f32[16,2,4,16,128]{4,3,2,1,0:T(8,128)}, f32[16,2,4,16,128]{4,3,2,1,0:T(8,128)S(1)}, u32[]{:S(2)}, u32[]{:S(2)}) collective-permute-start(f32[16,2,4,16,128]{4,3,2,1,0:T(8,128)} %pad_maximum_fusion.1), channel_id=1, source_target_pairs={{0,1},{1,2},{2,3},{3,4},{4,5},{5,6},{6,7},{7,0},{8,9},{9,10},{10,1... | collective-permute-start | bytes 3145736 | tf_op jit(solution)/shard_map/ppermute | solution.py:454
  89.7 1.1 pad_maximum_fusion.2
  90.8 0.0 copy-done.3
  90.8 0.2 collective-permute-start.9
  91.1 0.0 copy-done.8
  91.1 0.1 select_subtract_fusion.1
  91.2 0.1 reshape.36
  91.2 0.1 reshape.38
  91.3 0.1 broadcast_in_dim.31
  91.4 0.1 copy.15
  91.6 0.6 gather_fusion
  92.1 0.1 copy_select_fusion
  92.2 0.7 copy.20.shears
  92.9 0.7 broadcast_select_fusion.shears
  93.5 18.2 %core.1 = f32[32,2,64,512]{3,2,1,0:T(8,128)} custom-call(s32[16,32]{1,0:T(8,128)} %broadcast_select_fusion.shears, f32[4,2,4,64,128]{4,3,2,1,0:T(8,128)} %copy-done, f32[4,2,4,64,128]{4,3,2,1,0:T(8,128)} %collective-permute-done.5.two, f32[4,2,4,64,128]{4,3,2,1,0:T(8,128)} %copy-done.3, f32[4,2,4,64,128]{4,3,2,1,0:T(8,128)} %copy-done.2, ...), custom_call_target="tpu_custom_call" | custom-call | bytes 51000000 | tf_op jit(solution)/shard_map/core/pallas_call | solution.py:457
  111.8 0.0 collective-permute-done.8.before
  111.8 0.0 collective-permute-done.9.after
  111.8 1.0 copy-done.4
  112.8 6.9 %rim.1 = f32[32,2,64,512]{3,2,1,0:T(8,128)} custom-call(s32[32,256]{1,0:T(8,128)} %copy.20.shears, f32[16,2,4,16,128]{4,3,2,1,0:T(8,128)} %copy-done.4, f32[16,2,4,16,128]{4,3,2,1,0:T(8,128)} %collective-permute-done.9.after, f32[32,64,512]{2,1,0:T(8,128)} %divisor.1.scale, f32[32,2,64,512]{3,2,1,0:T(8,128)} %core.1), custom_call_target="tpu_custom_call", output_to_operand_aliasing={{}: (4, {})} | custom-call | bytes 27000000 | tf_op jit(solution)/shard_map/rim/pallas_call | solution.py:469
  (18 shorter events, 0.1 us)
Async XLA Ops:
  3.0 24.8 %all-to-all-start = ((f32[8,4,80,128]{3,2,1,0:T(8,128)}), f32[8,4,80,128]{3,2,1,0:T(8,128)S(1)}, u32[]{:S(2)}, u32[]{:S(2)}) async-start(f32[8,4,80,128]{3,2,1,0:T(8,128)} %measured_rows.1), calls=%async_computation | async-start | bytes 2621440 | tf_op jit(solution)/shard_map/all_to_all | solution.py:372
  17.3 10.7 %copy-start.9 = (s32[1,32]{1,0:T(1,128)S(1)}, s32[1,32]{1,0:T(1,128)}, u32[]{:S(2)}) copy-start(s32[1,32]{1,0:T(1,128)} %param.9) | copy-start | bytes 388
  18.3 10.6 %collective-permute-start.1 = (f32[2,4,24,128]{3,2,1,0:T(8,128)S(1)}, f32[2,4,24,128]{3,2,1,0:T(8,128)S(1)}, u32[]{:S(2)}, u32[]{:S(2)}) collective-permute-start(f32[2,4,24,128]{3,2,1,0:T(8,128)S(1)} %get-tuple-element.37), channel_id=1, source_target_pairs={{1,0},{2,1},{3,2},{4,3},{5,4},{6,5},{7,6},{0,7},{9,8},{10,9},{11,1... | collective-permute-start | bytes 294920 | tf_op jit(solution)/shard_map/ppermute | solution.py:392
  18.3 10.5 %collective-permute-start = (f32[2,4,24,128]{3,2,1,0:T(8,128)S(1)}, f32[2,4,24,128]{3,2,1,0:T(8,128)S(1)}, u32[]{:S(2)}, u32[]{:S(2)}) collective-permute-start(f32[2,4,24,128]{3,2,1,0:T(8,128)S(1)} %get-tuple-element.38), channel_id=1, source_target_pairs={{0,1},{1,2},{2,3},{3,4},{4,5},{5,6},{6,7},{7,0},{8,9},{9,10},{10,1... | collective-permute-start | bytes 294920 | tf_op jit(solution)/shard_map/ppermute | solution.py:391
  27.7 1.1 copy-start.1
  28.8 0.6 copy-start.6
  28.8 0.7 copy-start.7
  38.9 9.8 %collective-permute-start.4 = (f32[2,4,64,128]{3,2,1,0:T(8,128)}, f32[2,4,64,128]{3,2,1,0:T(8,128)S(1)}, u32[]{:S(2)}, u32[]{:S(2)}) collective-permute-start(f32[2,4,64,128]{3,2,1,0:T(8,128)} %frames.1), channel_id=1, source_target_pairs={{0,24},{1,97},{2,26},{3,99},{4,28},{5,101},{6,30},{7,103},{8,0},{9... | collective-permute-start | bytes 786440 | tf_op jit(solution)/shard_map/ppermute | solution.py:348
  41.6 9.7 %collective-permute-start.3 = (f32[2,4,64,128]{3,2,1,0:T(8,128)}, f32[2,4,64,128]{3,2,1,0:T(8,128)S(1)}, u32[]{:S(2)}, u32[]{:S(2)}) collective-permute-start(f32[2,4,64,128]{3,2,1,0:T(8,128)} %frames.1), channel_id=1, source_target_pairs={{0,8},{1,33},{2,10},{3,35},{4,12},{5,37},{6,14},{7,39},{8,16},{9,4... | collective-permute-start | bytes 786440 | tf_op jit(solution)/shard_map/ppermute | solution.py:348
  41.6 9.7 %collective-permute-start.2 = (f32[2,4,64,128]{3,2,1,0:T(8,128)}, f32[2,4,64,128]{3,2,1,0:T(8,128)S(1)}, u32[]{:S(2)}, u32[]{:S(2)}) collective-permute-start(f32[2,4,64,128]{3,2,1,0:T(8,128)} %frames.1), channel_id=1, source_target_pairs={{0,16},{1,65},{2,18},{3,67},{4,20},{5,69},{6,22},{7,71},{8,24},{9,... | collective-permute-start | bytes 786440 | tf_op jit(solution)/shard_map/ppermute | solution.py:348
  43.3 12.0 %all-to-all-start.1 = ((s32[16,8,128]{2,1,0:T(8,128)}), s32[16,8,128]{2,1,0:T(8,128)S(1)}, u32[]{:S(2)}, u32[]{:S(2)}) async-start(s32[16,8,128]{2,1,0:T(8,128)} %broadcast_in_dim.33), calls=%async_computation.1 | async-start | bytes 131072 | tf_op jit(solution)/shard_map/all_to_all | solution.py:421
  52.4 30.3 %copy-start = (f32[4,2,4,64,128]{4,3,2,1,0:T(8,128)}, f32[4,2,4,64,128]{4,3,2,1,0:T(8,128)S(1)}, u32[]{:S(2)}) copy-start(f32[4,2,4,64,128]{4,3,2,1,0:T(8,128)S(1)} %pad_maximum_fusion.own) | copy-start | bytes 3145732
  55.2 24.7 %collective-permute-start.7 = (f32[4,2,4,64,128]{4,3,2,1,0:T(8,128)S(1)}, f32[4,2,4,64,128]{4,3,2,1,0:T(8,128)S(1)}, u32[]{:S(2)}, u32[]{:S(2)}) collective-permute-start(f32[4,2,4,64,128]{4,3,2,1,0:T(8,128)S(1)} %pad_maximum_fusion.own), channel_id=1, source_target_pairs={{0,96},{1,25},{2,98},{3,27},{4,100},{5,29},{6,102},{7,31},{8,104},... | collective-permute-start | bytes 3145736 | tf_op jit(solution)/shard_map/ppermute | solution.py:350
  56.2 26.5 %collective-permute-start.6 = (f32[4,2,4,64,128]{4,3,2,1,0:T(8,128)S(1)}, f32[4,2,4,64,128]{4,3,2,1,0:T(8,128)S(1)}, u32[]{:S(2)}, u32[]{:S(2)}) collective-permute-start(f32[4,2,4,64,128]{4,3,2,1,0:T(8,128)S(1)} %pad_maximum_fusion.own), channel_id=1, source_target_pairs={{0,32},{1,9},{2,34},{3,11},{4,36},{5,13},{6,38},{7,15},{8,40},{9,1... | collective-permute-start | bytes 3145736 | tf_op jit(solution)/shard_map/ppermute | solution.py:350
  56.7 26.0 %collective-permute-start.5 = (f32[4,2,4,64,128]{4,3,2,1,0:T(8,128)S(1)}, f32[4,2,4,64,128]{4,3,2,1,0:T(8,128)}, u32[]{:S(2)}, u32[]{:S(2)}) collective-permute-start(f32[4,2,4,64,128]{4,3,2,1,0:T(8,128)S(1)} %pad_maximum_fusion.own), channel_id=1, source_target_pairs={{0,64},{1,17},{2,66},{3,19},{4,68},{5,21},{6,70},{7,23},{8,72},{9,... | collective-permute-start | bytes 3145736 | tf_op jit(solution)/shard_map/ppermute | solution.py:350
  79.9 11.1 %copy-start.8 = (s32[4,4]{1,0:T(4,128)S(1)}, s32[4,4]{1,0:T(4,128)}, u32[]{:S(2)}) copy-start(s32[4,4]{1,0:T(4,128)} %constant.86) | copy-start | bytes 196
  79.9 11.1 %copy-start.10 = (s32[4]{0:T(128)S(1)}, s32[4]{0:T(128)}, u32[]{:S(2)}) copy-start(s32[4]{0:T(128)} %constant.78.clone) | copy-start | bytes 52
  79.9 11.6 %copy-start.5 = (s32[16,32]{1,0:T(8,128)S(1)}, s32[16,32]{1,0:T(8,128)}, u32[]{:S(2)}) copy-start(s32[16,32]{1,0:T(8,128)} %slice.62.shears) | copy-start | bytes 6148
  80.0 10.9 %copy-start.2 = (f32[4,2,4,64,128]{4,3,2,1,0:T(8,128)}, f32[4,2,4,64,128]{4,3,2,1,0:T(8,128)S(1)}, u32[]{:S(2)}) copy-start(f32[4,2,4,64,128]{4,3,2,1,0:T(8,128)S(1)} %collective-permute-done.7.three) | copy-start | bytes 3145732
  82.7 8.1 %copy-start.3 = (f32[4,2,4,64,128]{4,3,2,1,0:T(8,128)}, f32[4,2,4,64,128]{4,3,2,1,0:T(8,128)S(1)}, u32[]{:S(2)}) copy-start(f32[4,2,4,64,128]{4,3,2,1,0:T(8,128)S(1)} %collective-permute-done.6.one) | copy-start | bytes 3145732
  85.5 26.3 %collective-permute-start.8 = (f32[16,2,4,16,128]{4,3,2,1,0:T(8,128)}, f32[16,2,4,16,128]{4,3,2,1,0:T(8,128)S(1)}, u32[]{:S(2)}, u32[]{:S(2)}) collective-permute-start(f32[16,2,4,16,128]{4,3,2,1,0:T(8,128)} %pad_maximum_fusion.1), channel_id=1, source_target_pairs={{0,1},{1,2},{2,3},{3,4},{4,5},{5,6},{6,7},{7,0},{8,9},{9,10},{10,1... | collective-permute-start | bytes 3145736 | tf_op jit(solution)/shard_map/ppermute | solution.py:454
  90.8 21.0 %collective-permute-start.9 = (f32[16,2,4,16,128]{4,3,2,1,0:T(8,128)}, f32[16,2,4,16,128]{4,3,2,1,0:T(8,128)}, u32[]{:S(2)}, u32[]{:S(2)}) collective-permute-start(f32[16,2,4,16,128]{4,3,2,1,0:T(8,128)} %pad_maximum_fusion.2), channel_id=1, source_target_pairs={{1,0},{2,1},{3,2},{4,3},{5,4},{6,5},{7,6},{0,7},{9,8},{10,9},{11,1... | collective-permute-start | bytes 3145736 | tf_op jit(solution)/shard_map/ppermute | solution.py:454
  111.8 1.0 copy-start.4

commit v3 on v2

--- a/solution.py
+++ b/solution.py
@@ -21,8 +21,9 @@
 WRAP = NX + RIM_ROWS
 F32 = jnp.float32
 BF16 = jnp.bfloat16
-HOPS = (0, 2, 1, 3)
+HOPS = (2, 1, 3)
 SIDE = 4
+BLOCKS = 2 * COLS
 COST_SCALE = 3_000_000
 
 SMEM = pl.BlockSpec(memory_space=pltpu.SMEM)
@@ -35,6 +36,10 @@
     )
 
 
+def vmem(mebibytes):
+    return pltpu.CompilerParams(vmem_limit_bytes=mebibytes * 2**20)
+
+
 def lane_block(c):
     return slice(c * LANES, (c + 1) * LANES)
 
@@ -47,16 +52,6 @@
     for c in range(COLS):
         scratch[index + (c, pl.ds(0, NX))] = image[:, lane_block(c)]
         scratch[index + (c, pl.ds(NX, WRAP - NX))] = image[: WRAP - NX, lane_block(c)]
-
-
-def rolled_blocks(scratch, index, first_row, rows, amount):
-    whole, part = amount // LANES, amount % LANES
-    turned = [
-        pltpu.roll(scratch[index + ((c - whole) & (COLS - 1), pl.ds(first_row, rows))], part, 1)
-        for c in range(COLS)
-    ]
-    keep = lane_ids(rows) >= part
-    return [jnp.where(keep, turned[c], turned[c - 1]) for c in range(COLS)]
 
 
 def interleave(transposed=False):
@@ -77,7 +72,7 @@
 
 
 def interleaved_roll(scratch, index, first_row, rows, amount):
-    whole, part = amount // COLS, amount % COLS
+    whole, part = amount >> 2, amount & (COLS - 1)
     return [
         pltpu.roll(
             scratch[index + ((c - part) & (COLS - 1), pl.ds(first_row, rows))],
@@ -137,7 +132,9 @@
     after,
     measured,
     wrapped,
+    facts,
     out,
+    known_out,
     window,
     local,
     field_a,
@@ -147,10 +144,13 @@
     positions,
 ):
     pad = 8
+    known = facts[...]
     for frame in range(FRAMES):
         for k in range(2):
-            place = jnp.max(measured[frame, 0, k : k + 1])
-            positions[frame, k] = place.astype(jnp.int32)
+            place = measured[frame, 0, k : k + 1]
+            positions[frame, k] = jnp.max(place).astype(jnp.int32)
+            known = jnp.where(lane_ids(1) == 2 * frame + k, place, known)
+    known_out[...] = jnp.broadcast_to(known, known_out.shape)
     window[...] = partial[:, :, SH - BASE : SH - BASE + ROWS]
     window[:, :, :SENT] += before[...]
     window[:, :, ROWS - SENT :] += after[...]
@@ -229,22 +229,36 @@
         image = jnp.concatenate([total[part, c] for c in range(COLS)], axis=1)
         image = permuted(image, matrix)
         for c in range(COLS):
-            out[part, c] = image[:, lane_block(c)]
+            rows = pl.ds(part * COLS + c, STRIP, stride=BLOCKS)
+            out[rows, :] = image[:, lane_block(c)]
 
 
 def weight_kernel(strip_index, positions, probe, out, wrapped):
     load_wrapped(wrapped, (), probe[0] * probe[0] + probe[1] * probe[1])
     chunk = 32
 
+    keeps = lane_ids(chunk)
+
     def per_angle(angle, _):
+        firsts, wholes, parts = [], [], []
+        for frame in range(FRAMES):
+            top, amount = positions[angle, 2 * frame], positions[angle, 2 * frame + 1]
+            firsts.append((strip_index[0] * STRIP - SH - top) & (NX - 1))
+            wholes.append(amount >> 7)
+            parts.append(amount & (LANES - 1))
         for row in range(0, RIM_ROWS, chunk):
             total = [jnp.zeros((chunk, LANES), F32)] * COLS
-            for frame in range(FRAMES):
-                first_row = (strip_index[0] * STRIP - SH - positions[angle, frame, 0]) & (NX - 1)
-                blocks = rolled_blocks(
-                    wrapped, (), first_row + row, chunk, positions[angle, frame, 1]
-                )
-                total = [a + b for a, b in zip(total, blocks)]
+            for first, whole, part in zip(firsts, wholes, parts):
+                turned = [
+                    pltpu.roll(
+                        wrapped[(c - whole) & (COLS - 1), pl.ds(first + row, chunk)], part, 1
+                    )
+                    for c in range(COLS)
+                ]
+                keep = keeps >= part
+                total = [
+                    total[c] + jnp.where(keep, turned[c], turned[c - 1]) for c in range(COLS)
+                ]
             for c in range(COLS):
                 out[angle, c, row : row + chunk] = total[c]
         return 0
@@ -272,29 +286,36 @@
     return high, (values - high.astype(F32)).astype(BF16)
 
 
-def core_kernel(shears, own, two, one, three, slices, scale, out, grads):
+def pack_kernel(*refs):
+    lasts, firsts, (last, first) = refs[:SIDE], refs[SIDE : 2 * SIDE], refs[2 * SIDE :]
+    for k in range(SIDE):
+        last[SIDE * k : SIDE * (k + 1)] = lasts[k][...]
+        first[SIDE * k : SIDE * (k + 1)] = firsts[k][...]
+
+
+def core_kernel(shears, own, two, one, three, slices, scale, out, grads, rows):
     @pl.when(pl.program_id(0) == 0)
     def _():
         for k, piece in enumerate((own, two, one, three)):
-            for j in range(SIDE):
-                grads[SIDE * k + j, :, :, SH : SH + STRIP] = piece[j]
-        grads[:, :, :, :SH] = jnp.zeros((ANGLES, 2, COLS, SH, LANES), F32)
-        grads[:, :, :, SH + STRIP :] = jnp.zeros((ANGLES, 2, COLS, SH, LANES), F32)
-
-    base = pl.program_id(0) * out.shape[0]
-
-    def per_slice(k, _):
+            grads[SIDE * k : SIDE * (k + 1), SH : SH + STRIP] = piece[...]
+        grads[:, :SH] = jnp.zeros((ANGLES, SH, BLOCKS, LANES), F32)
+        grads[:, SH + STRIP :] = jnp.zeros((ANGLES, SH, BLOCKS, LANES), F32)
+
+    count = out.shape[0]
+    base = pl.program_id(0) * count
+    chunk = 16
+    for k in range(count):
         starts = [SH - shears[a, base + k] for a in range(ANGLES)]
+        for row in range(0, STRIP, chunk):
+            total = grads[0, pl.ds(starts[0] + row, chunk)]
+            for a in range(1, ANGLES):
+                total += grads[a, pl.ds(starts[a] + row, chunk)]
+            rows[k, row * BLOCKS : (row + chunk) * BLOCKS] = total.reshape(chunk * BLOCKS, LANES)
         for part in range(2):
             for c in range(COLS):
-                total = grads[0, part, c, pl.ds(starts[0], STRIP)]
-                for a in range(1, ANGLES):
-                    total += grads[a, part, c, pl.ds(starts[a], STRIP)]
+                total = rows[k, pl.ds(part * COLS + c, STRIP, stride=BLOCKS), :]
                 cols = lane_block(c)
                 out[k, part, :, cols] = slices[k, part, :, cols] - total * scale[k, :, cols]
-        return 0
-
-    lax.fori_loop(0, out.shape[0], per_slice, 0)
 
 
 def rim_kernel(shears, before, after, scale, core, out, high, low, shifts):
@@ -305,7 +326,9 @@
             for part in range(2):
                 for c in range(COLS):
                     rows, cols = slice(a * SH, (a + 1) * SH), lane_block(part * COLS + c)
-                    high[rows, cols], low[rows, cols] = split(rim[a, part, c])
+                    block = part * COLS + c
+                    picked = pl.ds(a * SH * BLOCKS + block, SH, stride=BLOCKS)
+                    high[rows, cols], low[rows, cols] = split(rim[picked, :])
 
     @pl.when((pl.program_id(1) == 0) & (side == 0))
     def _():
@@ -345,17 +368,17 @@
 
 def gather_angles(grads, facts):
     axes = ("angle", "block")
-    row = [grads] + [lax.ppermute(grads, axes, hop_pairs(hop, 0)) for hop in HOPS[1:]]
-    row, facts = lax.optimization_barrier((jnp.stack(row), facts))
-    pieces = [row] + [lax.ppermute(row, axes, hop_pairs(hop, 1)) for hop in HOPS[1:]]
+    facts = lax.all_to_all(facts, "angle", 0, 0)[:, 0]
+    row = jnp.stack([grads] + [lax.ppermute(grads, axes, hop_pairs(hop, 0)) for hop in HOPS])
+    row, facts = lax.optimization_barrier((row, facts))
+    pieces = [row] + [lax.ppermute(row, axes, hop_pairs(hop, 1)) for hop in HOPS]
     angle = lax.axis_index("angle")
-    y, x = angle // SIDE, angle % SIDE
     odd = lax.axis_index("block") % 2
-    second, first = (jnp.asarray(HOPS).repeat(SIDE), jnp.asarray(HOPS * SIDE))
-    along_x = jnp.where(odd == 1, second, first)
-    along_y = jnp.where(odd == 1, first, second)
-    order = ((y - along_y) % SIDE) * SIDE + (x - along_x) % SIDE
-    return pieces, order.astype(jnp.int32), facts
+    first, second = jnp.asarray((0,) + HOPS), jnp.asarray((0,) + HOPS)
+    along_x = jnp.where(odd == 1, second[:, None], first[None])
+    along_y = jnp.where(odd == 1, first[None], second[:, None])
+    order = ((angle // SIDE - along_y) % SIDE) * SIDE + (angle - along_x) % SIDE
+    return pieces, order.reshape(ANGLES), facts.astype(jnp.int32)
 
 
 def per_device(object_field, shears, positions, measured, probe_field, kappa_field):
@@ -366,15 +389,11 @@
         in_specs=[SMEM, VMEM],
         out_specs=VMEM,
         scratch_shapes=[pltpu.VMEM((COLS, WRAP, LANES), F32)],
+        compiler_params=vmem(60),
         cost_estimate=cost(3),
         name="measured_rows",
     )(positions[0, 0], measured[0, 0])
     observed = lax.all_to_all(moved, "block", 0, 0)
-    facts = observed[:, 0, :2, 0].reshape(2 * FRAMES).astype(jnp.int32)
-    facts = jnp.pad(jnp.concatenate([facts, shears[0]]), (0, LANES - 2 * FRAMES - Z))
-    facts = jnp.broadcast_to(facts, (ANGLES, 8, LANES))
-    facts, observed = lax.optimization_barrier((facts, observed))
-
     step = 4
     partial = pl.pallas_call(
         project_kernel,
@@ -382,6 +401,7 @@
         out_shape=jax.ShapeDtypeStruct((2, COLS, RIM_ROWS, LANES), F32),
         in_specs=[SMEM, pl.BlockSpec((step, 2, STRIP, NY), lambda i: (i, 0, 0, 0))],
         out_specs=pl.BlockSpec((2, COLS, RIM_ROWS, LANES), lambda i: (0, 0, 0, 0)),
+        compiler_params=vmem(60),
         cost_estimate=cost(7),
         name="project",
     )(shears[0], object_field)
@@ -395,16 +415,21 @@
         out_shape=jax.ShapeDtypeStruct((3, COLS, WRAP, LANES), F32),
         in_specs=[VMEM, VMEM],
         out_specs=VMEM,
+        compiler_params=vmem(60),
         cost_estimate=cost(6),
         name="fields",
     )(probe_field, kappa_field[0])
 
+    facts = jnp.pad(shears.astype(F32), ((0, 0), (2 * FRAMES, LANES - 2 * FRAMES - Z)))
     field = pltpu.VMEM((2, COLS, ROWS + 16, LANES), F32)
-    grads = pl.pallas_call(
+    grads, facts = pl.pallas_call(
         frames_kernel,
-        out_shape=jax.ShapeDtypeStruct((2, COLS, STRIP, LANES), F32),
-        in_specs=[SMEM] + [VMEM] * 5,
-        out_specs=VMEM,
+        out_shape=[
+            jax.ShapeDtypeStruct((STRIP * BLOCKS, LANES), F32),
+            jax.ShapeDtypeStruct((ANGLES * 8, LANES), F32),
+        ],
+        in_specs=[SMEM] + [VMEM] * 6,
+        out_specs=[VMEM, VMEM],
         scratch_shapes=[
             pltpu.VMEM((2, COLS, ROWS, LANES), F32),
             pltpu.VMEM((3, COLS, ROWS, LANES), F32),
@@ -414,24 +439,26 @@
             pltpu.VMEM((2, COLS, STRIP, LANES), F32),
             pltpu.SMEM((FRAMES, 2), jnp.int32),
         ],
+        compiler_params=vmem(15),
         cost_estimate=cost(9),
         name="frames",
-    )(strip_index, partial, before, after, observed, wrapped)
-    facts, grads = lax.optimization_barrier((facts, grads))
-    facts = lax.all_to_all(facts, "angle", 0, 0)
-    pieces, order, facts = gather_angles(grads, facts)
-    facts = facts[:, 0]
-    all_positions = facts[:, : 2 * FRAMES].reshape(ANGLES, FRAMES, 2)
+    )(strip_index, partial, before, after, observed, wrapped, facts)
+    pieces, order, facts = gather_angles(
+        grads.reshape(STRIP, BLOCKS, LANES), facts.reshape(ANGLES, 8, LANES)
+    )
+    facts = jnp.take(facts, order, axis=0)
+    all_positions = facts[:, : 2 * FRAMES]
     all_shears = facts[:, 2 * FRAMES : 2 * FRAMES + Z]
-    ordered_shears = jnp.take(all_shears, order, axis=0)
-    rim_shears = ordered_shears.reshape(SIDE, SIDE, Z).transpose(2, 1, 0).reshape(Z, ANGLES)
+    rim_shears = all_shears.reshape(SIDE, SIDE, Z).transpose(2, 1, 0).reshape(Z, ANGLES)
     rim_shears = jnp.repeat(rim_shears, SH, axis=1)
+
     weights = pl.pallas_call(
         weight_kernel,
         out_shape=jax.ShapeDtypeStruct((ANGLES, COLS, RIM_ROWS, LANES), F32),
         in_specs=[SMEM, SMEM, VMEM],
         out_specs=VMEM,
         scratch_shapes=[pltpu.VMEM((COLS, WRAP, LANES), F32)],
+        compiler_params=vmem(12),
         cost_estimate=cost(2),
         name="weights",
     )(strip_index, all_positions, probe_field)
@@ -442,16 +469,28 @@
         out_shape=jax.ShapeDtypeStruct((Z, STRIP, NY), F32),
         in_specs=[SMEM, VMEM],
         out_specs=slices_spec,
+        compiler_params=vmem(8),
         cost_estimate=cost(2),
         name="divisor",
     )(all_shears, weights)
 
-    scale, *pieces = lax.optimization_barrier((scale, *pieces))
+    scale, rim_shears, *pieces = lax.optimization_barrier((scale, rim_shears, *pieces))
+    edge = (SIDE, SH, BLOCKS, LANES)
+    rims = pl.pallas_call(
+        pack_kernel,
+        grid=(1,),
+        out_shape=[jax.ShapeDtypeStruct((ANGLES, SH, BLOCKS, LANES), F32)] * 2,
+        in_specs=[pl.BlockSpec(edge, lambda i: (0, STRIP // SH - 1, 0, 0))] * SIDE
+        + [pl.BlockSpec(edge, lambda i: (0, 0, 0, 0))] * SIDE,
+        out_specs=[pl.BlockSpec((ANGLES, SH, BLOCKS, LANES), lambda i: (0, 0, 0, 0))] * 2,
+        compiler_params=vmem(12),
+        cost_estimate=cost(2),
+        name="pack",
+    )(*pieces, *pieces)
     rims = [
-        jnp.concatenate([piece[..., rows, :] for piece in pieces])
-        for rows in (slice(STRIP - SH, STRIP), slice(0, SH))
+        lax.ppermute(rim, "block", pairs).reshape(ANGLES * SH * BLOCKS, LANES)
+        for rim, pairs in zip(rims, (up, down))
     ]
-    rims = [lax.ppermute(rim, "block", pairs) for rim, pairs in zip(rims, (up, down))]
 
     object_spec = pl.BlockSpec((step, 2, STRIP, NY), lambda i: (i, 0, 0, 0))
     core = pl.pallas_call(
@@ -460,10 +499,14 @@
         out_shape=jax.ShapeDtypeStruct(object_field.shape, F32),
         in_specs=[SMEM] + [VMEM] * 4 + [object_spec, slices_spec],
         out_specs=object_spec,
-        scratch_shapes=[pltpu.VMEM((ANGLES, 2, COLS, RIM_ROWS, LANES), F32)],
+        scratch_shapes=[
+            pltpu.VMEM((ANGLES, RIM_ROWS, BLOCKS, LANES), F32),
+            pltpu.VMEM((step, STRIP * BLOCKS, LANES), F32),
+        ],
+        compiler_params=vmem(50),
         cost_estimate=cost(17),
         name="core",
-    )(ordered_shears, *pieces, object_field, scale)
+    )(all_shears, *pieces, object_field, scale)
     many = 16
     edge_spec = pl.BlockSpec((many, 2, SH, NY), lambda j, i: (i, 0, j * (STRIP // SH - 1), 0))
     return pl.pallas_call(
@@ -479,6 +522,7 @@
             pltpu.VMEM((many * SH, ANGLES * SH), BF16),
         ],
         input_output_aliases={4: 0},
+        compiler_params=vmem(50),
         cost_estimate=cost(9),
         name="rim",
     )(rim_shears, *rims, scale, core)

time: 122 us -> 111 us (0.910)
  blocking collectives: 0 us -> 12.1 us
  Pallas kernels: 72.1 us -> 63.2 us
  starting transfers between devices: 25.3 us -> 19.9 us
  other arithmetic: 4.45 us -> 0.26 us
  waiting for transfers between devices: 9.58 us -> 5.61 us
    all_to_all x0 -> x1, blocking collectives: none -> 12.1 us  [gather_angles(): facts = lax.all_to_all(facts, 'angle', 0, 0)[:, 0]]
    all_to_all x1 -> x0, starting transfers between devices: 5.46 us -> none  [per_device(): facts = lax.all_to_all(facts, 'angle', 0, 0)]
    unnamed x22 -> x14, local copies, waits for them, and re-layouts: 1.68 us -> 5.59 us
    pallas_call x1, Pallas kernels: 18.2 us -> 15 us  [per_device(): pl.pallas_call(core_kernel, grid=(Z // step,), out_shape=jax.ShapeDtypeSt...]
    all_to_all x1 -> x0, waiting for transfers between devices: 2.81 us -> none  [per_device(): facts = lax.all_to_all(facts, 'angle', 0, 0)]
    pallas_call x1, Pallas kernels: 11.4 us -> 8.7 us  [per_device(): pl.pallas_call(weight_kernel, out_shape=jax.ShapeDtypeStruct((ANGLES, COL...]
    ppermute x3, waiting for transfers between devices: 2.64 us -> 0.01 us  [gather_angles(): lax.ppermute(grads, axes, hop_pairs(hop, 0))]
    concatenate x3 -> x0, other arithmetic: 2.36 us -> none  [the longest x2 2.28 us: per_device(): jnp.concatenate([piece[..., rows, :] for piece in pieces])]
  transfers between devices with their start and end apart: 12 -> 11, of which waited for: 4 -> 2; matrix products, arithmetic and copies ran while one was open for 7% -> 2% of each run, Pallas kernels for 44% -> 41%
where the time goes in v3:
time: 111 us; the launch traced here: 109 us
  Pallas kernels  63.2 us (57%)
  starting transfers between devices  19.9 us (18%)
  blocking collectives  12.1 us (11%)
  local copies, waits for them, and re-layouts  7.73 us (7%)
  waiting for transfers between devices  5.61 us (5%)
    pallas_call x1, Pallas kernels, per_device(): pl.pallas_call(core_kernel, grid=(Z // step,), out_shape=jax.ShapeDtypeSt...  15 us
    all_to_all x1, blocking collectives, gather_angles(): facts = lax.all_to_all(facts, 'angle', 0, 0)[:, 0]  12.1 us
    pallas_call x1, Pallas kernels, per_device(): pl.pallas_call(weight_kernel, out_shape=jax.ShapeDtypeStruct((ANGLES, COL...  8.7 us
    pallas_call x1, Pallas kernels, per_device(): pl.pallas_call(project_kernel, grid=(Z // step,), out_shape=jax.ShapeDtyp...  7.55 us
    pallas_call x1, Pallas kernels, per_device(): pl.pallas_call(divisor_kernel, grid=(Z // step,), out_shape=jax.ShapeDtyp...  7.42 us
    all_to_all x1, starting transfers between devices, per_device(): observed = lax.all_to_all(moved, 'block', 0, 0)  6.81 us
    pallas_call x1, Pallas kernels, per_device(): pl.pallas_call(rim_kernel, grid=(2, Z // many), out_shape=jax.ShapeDtypeS...  6.8 us
    pallas_call x1, Pallas kernels, per_device(): pl.pallas_call(fields_kernel, out_shape=jax.ShapeDtypeStruct((3, COLS, WR...  6.35 us
  transfers between devices with their start and end apart: 11, of which 2 were waited for; matrix products, arithmetic and copies ran while one was open for 2% of the time, Pallas kernels for 41%

profile of v3, /device:TPU:1, one launch (start us, length us, event | category | flops | bytes accessed | tf_op | source)
XLA Modules:
  0.0 109.0 jit_solution(4553997952908456452)
XLA Ops:
  0.0 3.0 %measured_rows.1 = f32[8,4,80,128]{3,2,1,0:T(8,128)} custom-call(s32[2]{0:T(128)} %bitcast.41, bf16[512,512]{1,0:T(8,128)(2,1)} %bitcast.34), custom_call_target="tpu_custom_call" | custom-call | bytes 9000000 | tf_op jit(solution)/shard_map/measured_rows/pallas_call | solution.py:386
  3.0 6.8 %all-to-all-start = ((f32[8,4,80,128]{3,2,1,0:T(8,128)}), f32[8,4,80,128]{3,2,1,0:T(8,128)S(1)}, u32[]{:S(2)}, u32[]{:S(2)}) async-start(f32[8,4,80,128]{3,2,1,0:T(8,128)} %measured_rows.1), calls=%async_computation | async-start | bytes 2621440 | tf_op jit(solution)/shard_map/all_to_all | solution.py:396
  9.8 0.0 copy-start.6
  9.8 7.5 %project.1.partial = f32[2,4,96,128]{3,2,1,0:T(8,128)} custom-call(s32[32]{0:T(128)} %bitcast.40, f32[32,2,64,512]{3,2,1,0:T(8,128)} %slices.3), custom_call_target="tpu_custom_call" | custom-call | bytes 21000000 | tf_op jit(solution)/shard_map/project/pallas_call | solution.py:398
  17.3 0.0 copy-start.4
  17.3 1.0 fusion.9
  18.3 0.0 collective-permute-start.1
  18.4 1.7 %collective-permute-start = (f32[2,4,24,128]{3,2,1,0:T(8,128)S(1)}, f32[2,4,24,128]{3,2,1,0:T(8,128)S(1)}, u32[]{:S(2)}, u32[]{:S(2)}) collective-permute-start(f32[2,4,24,128]{3,2,1,0:T(8,128)S(1)} %get-tuple-element.30), channel_id=1, source_target_pairs={{0,1},{1,2},{2,3},{3,4},{4,5},{5,6},{6,7},{7,0},{8,9},{9,10},{10,1... | collective-permute-start | bytes 294920 | tf_op jit(solution)/shard_map/ppermute | solution.py:411
  20.1 0.0 copy-done.6
  20.1 0.1 pad.4.facts
  20.2 6.4 %fields.1.wrapped = f32[3,4,608,128]{3,2,1,0:T(8,128)} custom-call(f32[2,512,512]{2,1,0:T(8,128)} %probe.3, f32[512,512]{1,0:T(8,128)} %bitcast.32), custom_call_target="tpu_custom_call" | custom-call | bytes 18000000 | tf_op jit(solution)/shard_map/fields/pallas_call | solution.py:413
  26.5 1.2 %collective-permute-done.1.after = f32[2,4,24,128]{3,2,1,0:T(8,128)S(1)} collective-permute-done((f32[2,4,24,128]{3,2,1,0:T(8,128)S(1)}, f32[2,4,24,128]{3,2,1,0:T(8,128)S(1)}, u32[]{:S(2)}, u32[]{:S(2)}) %collective-permute-start.1) | collective-permute-done | bytes 98336 | tf_op jit(solution)/shard_map/ppermute | solution.py:412
  27.8 0.0 collective-permute-done.before
  27.8 0.0 all-to-all-done.measured
  27.8 0.0 copy-done.4
  27.8 0.0 copy-start.1
  27.8 2.0 %copy-done.1 = f32[3,4,608,128]{3,2,1,0:T(8,128)S(1)} copy-done((f32[3,4,608,128]{3,2,1,0:T(8,128)S(1)}, f32[3,4,608,128]{3,2,1,0:T(8,128)}, u32[]{:S(2)}) %copy-start.1) | copy-done | bytes 3735576
  29.8 0.0 copy-start.5
  29.8 5.9 %frames.1 = (f32[512,128]{1,0:T(8,128)S(1)}, f32[128,128]{1,0:T(8,128)S(1)}) custom-call(s32[1]{0:T(128)} %bitcast.strip_index, f32[2,4,96,128]{3,2,1,0:T(8,128)S(1)} %copy-done.4, f32[2,4,24,128]{3,2,1,0:T(8,128)S(1)} %collective-permute-done.before, f32[2,4,24,128]{3,2,1,0:T(8,128)S(1)} %collective-permute-done.1.after, ...), custom_call_target="tpu_custom_call" | custom-call | bytes 27000000 | tf_op jit(solution)/shard_map/frames/pallas_call | solution.py:425
  35.7 2.8 %collective-permute-start.4 = (f32[64,8,128]{2,1,0:T(8,128)S(1)}, f32[64,8,128]{2,1,0:T(8,128)S(1)}, u32[]{:S(2)}, u32[]{:S(2)}) collective-permute-start(f32[64,8,128]{2,1,0:T(8,128)S(1)} %bitcast.25), channel_id=1, source_target_pairs={{0,24},{1,97},{2,26},{3,99},{4,28},{5,101},{6,30},{7,103},{8,0},{9... | collective-permute-start | bytes 786440 | tf_op jit(solution)/shard_map/ppermute | solution.py:372
  38.5 0.0 collective-permute-start.3
  38.5 1.6 %collective-permute-start.2 = (f32[64,8,128]{2,1,0:T(8,128)S(1)}, f32[64,8,128]{2,1,0:T(8,128)S(1)}, u32[]{:S(2)}, u32[]{:S(2)}) collective-permute-start(f32[64,8,128]{2,1,0:T(8,128)S(1)} %bitcast.27), channel_id=1, source_target_pairs={{0,16},{1,65},{2,18},{3,67},{4,20},{5,69},{6,22},{7,71},{8,24},{9,... | collective-permute-start | bytes 786440 | tf_op jit(solution)/shard_map/ppermute | solution.py:372
  40.2 12.1 %all_to_all.10 = f32[16,8,128]{2,1,0:T(8,128)S(1)} all-to-all(f32[16,8,128]{2,1,0:T(8,128)S(1)} %bitcast.31), channel_id=1, replica_groups=mesh['angle'=16,'block'=8] {'angle'}, dimensions={0} | all-to-all | bytes 131072 | tf_op jit(solution)/shard_map/all_to_all | solution.py:371
  52.3 0.0 collective-permute-done.4
  52.3 0.0 collective-permute-done.3
  52.3 0.0 collective-permute-done.2
  52.3 0.1 pad_maximum_fusion.refs_0_.refs_4_.own
  52.4 1.1 collective-permute-start.7
  53.5 0.5 collective-permute-start.6
  54.0 0.8 collective-permute-start.5
  54.8 0.0 copy-done.5
  54.8 0.1 select_subtract_fusion.1
  54.8 0.1 sub.55
  54.9 0.1 sub.51
  55.0 0.1 sub.56
  55.1 0.1 sub.54
  55.2 0.6 gather_fusion
  55.8 0.1 broadcast_select_fusion
  55.9 0.1 slice.25.shears
  56.0 0.0 copy-start.3
  56.0 1.6 %copy-done.3 = f32[2,512,512]{2,1,0:T(8,128)S(1)} copy-done((f32[2,512,512]{2,1,0:T(8,128)S(1)}, f32[2,512,512]{2,1,0:T(8,128)}, u32[]{:S(2)}) %copy-start.3) | copy-done | bytes 2097176
  57.6 8.7 %weights.1 = f32[16,4,96,128]{3,2,1,0:T(8,128)S(1)} custom-call(s32[1]{0:T(128)} %bitcast.strip_index, s32[16,16]{1,0:T(8,128)S(1)} %bitcast.30, f32[2,512,512]{2,1,0:T(8,128)S(1)} %copy-done.3), custom_call_target="tpu_custom_call" | custom-call | bytes 6000000 | tf_op jit(solution)/shard_map/weights/pallas_call | solution.py:455
  66.3 7.4 %divisor.1.scale = f32[32,64,512]{2,1,0:T(8,128)S(1)} custom-call(s32[16,32]{1,0:T(8,128)S(1)} %slice.25.shears, f32[16,4,96,128]{3,2,1,0:T(8,128)S(1)} %weights.1), custom_call_target="tpu_custom_call" | custom-call | bytes 6000000 | tf_op jit(solution)/shard_map/divisor/pallas_call | solution.py:466
  73.7 0.0 copy-start
  73.7 1.9 %copy-done = f32[32,64,512]{2,1,0:T(8,128)} copy-done((f32[32,64,512]{2,1,0:T(8,128)}, f32[32,64,512]{2,1,0:T(8,128)S(1)}, u32[]{:S(2)}) %copy-start) | copy-done | bytes 4194328
  75.6 0.0 collective-permute-done.7.refs_3_.refs_7_.three
  75.6 0.0 copy-start.2
  75.6 4.4 %collective-permute-done.6.refs_2_.refs_6_.one = f32[4,64,8,128]{3,2,1,0:T(8,128)S(1)} collective-permute-done((f32[4,64,8,128]{3,2,1,0:T(8,128)S(1)}, f32[4,64,8,128]{3,2,1,0:T(8,128)S(1)}, u32[]{:S(2)}, u32[]{:S(2)}) %collective-permute-start.6) | collective-permute-done | bytes 1048608 | tf_op jit(solution)/shard_map/ppermute | solution.py:374
  80.0 0.0 collective-permute-done.5.refs_1_.refs_5_.two
  80.0 2.5 %pack.1 = (f32[16,16,8,128]{3,2,1,0:T(8,128)}, f32[16,16,8,128]{3,2,1,0:T(8,128)}) custom-call(f32[4,64,8,128]{3,2,1,0:T(8,128)S(1)} %pad_maximum_fusion.refs_0_.refs_4_.own, f32[4,64,8,128]{3,2,1,0:T(8,128)} %collective-permute-done.5.refs_1_.refs_5_.two, f32[4,64,8,128]{3,2,1,0:T(8,128)S(1)} %collective-permute-done.6.refs_2_.refs_6_.one, ...), custom_call_target="tpu_custom_call" | custom-call | bytes 6000000 | tf_op jit(solution)/shard_map/pack/pallas_call | solution.py:479
  82.6 0.0 copy-done.2
  82.6 3.7 %collective-permute-start.8 = (f32[16,16,8,128]{3,2,1,0:T(8,128)}, f32[16,16,8,128]{3,2,1,0:T(8,128)S(1)}, u32[]{:S(2)}, u32[]{:S(2)}) collective-permute-start(f32[16,16,8,128]{3,2,1,0:T(8,128)} %get-tuple-element.26), channel_id=1, source_target_pairs={{0,1},{1,2},{2,3},{3,4},{4,5},{5,6},{6,7},{7,0},{8,9},{9,10},{10,1... | collective-permute-start | bytes 3145736 | tf_op jit(solution)/shard_map/ppermute | solution.py:491
  86.3 0.8 collective-permute-start.9
  87.1 0.1 copy.16.shears
  87.1 15.0 %core.1 = f32[32,2,64,512]{3,2,1,0:T(8,128)} custom-call(s32[16,32]{1,0:T(8,128)S(1)} %slice.25.shears, f32[4,64,8,128]{3,2,1,0:T(8,128)S(1)} %pad_maximum_fusion.refs_0_.refs_4_.own, f32[4,64,8,128]{3,2,1,0:T(8,128)} %collective-permute-done.5.refs_1_.refs_5_.two, f32[4,64,8,128]{3,2,1,0:T(8,128)S(1)} %collective-permute-done.6.refs_2_.refs_6_.one, ...), custom_call_target="tpu_custom_call" | custom-call | bytes 51000000 | tf_op jit(solution)/shard_map/core/pallas_call | solution.py:496
  102.1 0.0 collective-permute-done.8
  102.1 0.0 collective-permute-done.9
  102.2 6.8 %rim.1 = f32[32,2,64,512]{3,2,1,0:T(8,128)} custom-call(s32[32,256]{1,0:T(8,128)S(1)} %copy.16.shears, f32[2048,128]{1,0:T(8,128)S(1)} %bitcast.24, f32[2048,128]{1,0:T(8,128)} %bitcast.18.after, f32[32,64,512]{2,1,0:T(8,128)} %copy-done, f32[32,2,64,512]{3,2,1,0:T(8,128)} %core.1), custom_call_target="tpu_custom_call", output_to_operand_aliasing={{}: (4, {})} | custom-call | bytes 27000000 | tf_op jit(solution)/shard_map/rim/pallas_call | solution.py:512
  (8 shorter events, 0.1 us)
Async XLA Ops:
  3.0 24.8 %all-to-all-start = ((f32[8,4,80,128]{3,2,1,0:T(8,128)}), f32[8,4,80,128]{3,2,1,0:T(8,128)S(1)}, u32[]{:S(2)}, u32[]{:S(2)}) async-start(f32[8,4,80,128]{3,2,1,0:T(8,128)} %measured_rows.1), calls=%async_computation | async-start | bytes 2621440 | tf_op jit(solution)/shard_map/all_to_all | solution.py:396
  9.8 10.3 %copy-start.6 = (s32[1,32]{1,0:T(1,128)S(1)}, s32[1,32]{1,0:T(1,128)}, u32[]{:S(2)}) copy-start(s32[1,32]{1,0:T(1,128)} %param.9) | copy-start | bytes 388
  17.3 10.4 %copy-start.4 = (f32[2,4,96,128]{3,2,1,0:T(8,128)S(1)}, f32[2,4,96,128]{3,2,1,0:T(8,128)}, u32[]{:S(2)}) copy-start(f32[2,4,96,128]{3,2,1,0:T(8,128)} %project.1.partial) | copy-start | bytes 1179652
  18.3 9.4 %collective-permute-start.1 = (f32[2,4,24,128]{3,2,1,0:T(8,128)S(1)}, f32[2,4,24,128]{3,2,1,0:T(8,128)S(1)}, u32[]{:S(2)}, u32[]{:S(2)}) collective-permute-start(f32[2,4,24,128]{3,2,1,0:T(8,128)S(1)} %get-tuple-element.29), channel_id=1, source_target_pairs={{1,0},{2,1},{3,2},{4,3},{5,4},{6,5},{7,6},{0,7},{9,8},{10,9},{11,1... | collective-permute-start | bytes 294920 | tf_op jit(solution)/shard_map/ppermute | solution.py:412
  18.4 9.4 %collective-permute-start = (f32[2,4,24,128]{3,2,1,0:T(8,128)S(1)}, f32[2,4,24,128]{3,2,1,0:T(8,128)S(1)}, u32[]{:S(2)}, u32[]{:S(2)}) collective-permute-start(f32[2,4,24,128]{3,2,1,0:T(8,128)S(1)} %get-tuple-element.30), channel_id=1, source_target_pairs={{0,1},{1,2},{2,3},{3,4},{4,5},{5,6},{6,7},{7,0},{8,9},{9,10},{10,1... | collective-permute-start | bytes 294920 | tf_op jit(solution)/shard_map/ppermute | solution.py:411
  27.8 2.1 %copy-start.1 = (f32[3,4,608,128]{3,2,1,0:T(8,128)S(1)}, f32[3,4,608,128]{3,2,1,0:T(8,128)}, u32[]{:S(2)}) copy-start(f32[3,4,608,128]{3,2,1,0:T(8,128)} %fields.1.wrapped) | copy-start | bytes 11206660
  29.8 24.9 %copy-start.5 = (s32[4]{0:T(128)S(1)}, s32[4]{0:T(128)}, u32[]{:S(2)}) copy-start(s32[4]{0:T(128)} %constant.78.clone) | copy-start | bytes 52
  35.7 16.6 %collective-permute-start.4 = (f32[64,8,128]{2,1,0:T(8,128)S(1)}, f32[64,8,128]{2,1,0:T(8,128)S(1)}, u32[]{:S(2)}, u32[]{:S(2)}) collective-permute-start(f32[64,8,128]{2,1,0:T(8,128)S(1)} %bitcast.25), channel_id=1, source_target_pairs={{0,24},{1,97},{2,26},{3,99},{4,28},{5,101},{6,30},{7,103},{8,0},{9... | collective-permute-start | bytes 786440 | tf_op jit(solution)/shard_map/ppermute | solution.py:372
  38.5 13.8 %collective-permute-start.3 = (f32[64,8,128]{2,1,0:T(8,128)S(1)}, f32[64,8,128]{2,1,0:T(8,128)S(1)}, u32[]{:S(2)}, u32[]{:S(2)}) collective-permute-start(f32[64,8,128]{2,1,0:T(8,128)S(1)} %bitcast.26), channel_id=1, source_target_pairs={{0,8},{1,33},{2,10},{3,35},{4,12},{5,37},{6,14},{7,39},{8,16},{9,4... | collective-permute-start | bytes 786440 | tf_op jit(solution)/shard_map/ppermute | solution.py:372
  38.5 13.8 %collective-permute-start.2 = (f32[64,8,128]{2,1,0:T(8,128)S(1)}, f32[64,8,128]{2,1,0:T(8,128)S(1)}, u32[]{:S(2)}, u32[]{:S(2)}) collective-permute-start(f32[64,8,128]{2,1,0:T(8,128)S(1)} %bitcast.27), channel_id=1, source_target_pairs={{0,16},{1,65},{2,18},{3,67},{4,20},{5,69},{6,22},{7,71},{8,24},{9,... | collective-permute-start | bytes 786440 | tf_op jit(solution)/shard_map/ppermute | solution.py:372
  52.4 23.2 %collective-permute-start.7 = (f32[4,64,8,128]{3,2,1,0:T(8,128)S(1)}, f32[4,64,8,128]{3,2,1,0:T(8,128)S(1)}, u32[]{:S(2)}, u32[]{:S(2)}) collective-permute-start(f32[4,64,8,128]{3,2,1,0:T(8,128)S(1)} %pad_maximum_fusion.refs_0_.refs_4_.own), channel_id=1, source_target_pairs={{0,96},{1,25},{2,98},{3,27},{4,100},{5,29},{6,102},{7,31},{8,104},... | collective-permute-start | bytes 3145736 | tf_op jit(solution)/shard_map/ppermute | solution.py:374
  53.5 26.5 %collective-permute-start.6 = (f32[4,64,8,128]{3,2,1,0:T(8,128)S(1)}, f32[4,64,8,128]{3,2,1,0:T(8,128)S(1)}, u32[]{:S(2)}, u32[]{:S(2)}) collective-permute-start(f32[4,64,8,128]{3,2,1,0:T(8,128)S(1)} %pad_maximum_fusion.refs_0_.refs_4_.own), channel_id=1, source_target_pairs={{0,32},{1,9},{2,34},{3,11},{4,36},{5,13},{6,38},{7,15},{8,40},{9,1... | collective-permute-start | bytes 3145736 | tf_op jit(solution)/shard_map/ppermute | solution.py:374
  54.0 26.0 %collective-permute-start.5 = (f32[4,64,8,128]{3,2,1,0:T(8,128)S(1)}, f32[4,64,8,128]{3,2,1,0:T(8,128)}, u32[]{:S(2)}, u32[]{:S(2)}) collective-permute-start(f32[4,64,8,128]{3,2,1,0:T(8,128)S(1)} %pad_maximum_fusion.refs_0_.refs_4_.own), channel_id=1, source_target_pairs={{0,64},{1,17},{2,66},{3,19},{4,68},{5,21},{6,70},{7,23},{8,72},{9,... | collective-permute-start | bytes 3145736 | tf_op jit(solution)/shard_map/ppermute | solution.py:374
  56.0 1.6 %copy-start.3 = (f32[2,512,512]{2,1,0:T(8,128)S(1)}, f32[2,512,512]{2,1,0:T(8,128)}, u32[]{:S(2)}) copy-start(f32[2,512,512]{2,1,0:T(8,128)} %probe.3) | copy-start | bytes 6291460
  73.7 1.9 %copy-start = (f32[32,64,512]{2,1,0:T(8,128)}, f32[32,64,512]{2,1,0:T(8,128)S(1)}, u32[]{:S(2)}) copy-start(f32[32,64,512]{2,1,0:T(8,128)S(1)} %divisor.1.scale) | copy-start | bytes 12582916
  75.6 6.9 %copy-start.2 = (f32[4,64,8,128]{3,2,1,0:T(8,128)}, f32[4,64,8,128]{3,2,1,0:T(8,128)S(1)}, u32[]{:S(2)}) copy-start(f32[4,64,8,128]{3,2,1,0:T(8,128)S(1)} %collective-permute-done.7.refs_3_.refs_7_.three) | copy-start | bytes 3145732
  82.6 19.6 %collective-permute-start.8 = (f32[16,16,8,128]{3,2,1,0:T(8,128)}, f32[16,16,8,128]{3,2,1,0:T(8,128)S(1)}, u32[]{:S(2)}, u32[]{:S(2)}) collective-permute-start(f32[16,16,8,128]{3,2,1,0:T(8,128)} %get-tuple-element.26), channel_id=1, source_target_pairs={{0,1},{1,2},{2,3},{3,4},{4,5},{5,6},{6,7},{7,0},{8,9},{9,10},{10,1... | collective-permute-start | bytes 3145736 | tf_op jit(solution)/shard_map/ppermute | solution.py:491
  86.3 15.9 %collective-permute-start.9 = (f32[16,16,8,128]{3,2,1,0:T(8,128)}, f32[16,16,8,128]{3,2,1,0:T(8,128)}, u32[]{:S(2)}, u32[]{:S(2)}) collective-permute-start(f32[16,16,8,128]{3,2,1,0:T(8,128)} %get-tuple-element.27), channel_id=1, source_target_pairs={{1,0},{2,1},{3,2},{4,3},{5,4},{6,5},{7,6},{0,7},{9,8},{10,9},{11,1... | collective-permute-start | bytes 3145736 | tf_op jit(solution)/shard_map/ppermute | solution.py:491

commit v4 on v3

--- a/solution.py
+++ b/solution.py
@@ -23,6 +23,7 @@
 BF16 = jnp.bfloat16
 HOPS = (2, 1, 3)
 SIDE = 4
+SPARE = 16
 BLOCKS = 2 * COLS
 COST_SCALE = 3_000_000
 
@@ -131,10 +132,12 @@
     before,
     after,
     measured,
-    wrapped,
+    fields,
     facts,
     out,
     known_out,
+    wrapped,
+    arrival,
     window,
     local,
     field_a,
@@ -144,6 +147,8 @@
     positions,
 ):
     pad = 8
+    copy = pltpu.make_async_copy(fields.at[pl.ds(0, 3)], wrapped, arrival)
+    copy.start()
     known = facts[...]
     for frame in range(FRAMES):
         for k in range(2):
@@ -223,6 +228,7 @@
             total[1, :, pl.ds(row, tile)] += probe_re * grad_im - probe_im * grad_re
         return 0
 
+    copy.wait()
     lax.fori_loop(0, FRAMES, per_frame, 0)
     matrix = interleave(transposed=True)
     for part in range(2):
@@ -233,7 +239,7 @@
             out[rows, :] = image[:, lane_block(c)]
 
 
-def weight_kernel(strip_index, positions, probe, out, wrapped):
+def gather_weights(strip_index, positions, probe, out, wrapped):
     load_wrapped(wrapped, (), probe[0] * probe[0] + probe[1] * probe[1])
     chunk = 32
 
@@ -266,7 +272,25 @@
     lax.fori_loop(0, ANGLES, per_angle, 0)
 
 
-def divisor_kernel(shears, weights, out):
+def divisor_kernel(
+    strip_index,
+    positions,
+    shears,
+    probe,
+    own,
+    slices,
+    out,
+    rest,
+    weights,
+    wrapped,
+    grads,
+    rows,
+):
+    @pl.when(pl.program_id(0) == 0)
+    def _():
+        gather_weights(strip_index, positions, probe, weights, wrapped)
+        fill_grads(grads, (own,))
+
     base = pl.program_id(0) * out.shape[0]
 
     def per_slice(k, _):
@@ -276,6 +300,7 @@
             for a in range(ANGLES):
                 total += weights[a, c, pl.ds(starts[a], STRIP)]
             out[k, :, lane_block(c)] = 1.0 / total
+        take_grads(starts[:SIDE], grads, rows, slices.at[k], out.at[k], rest.at[k])
         return 0
 
     lax.fori_loop(0, out.shape[0], per_slice, 0)
@@ -287,35 +312,69 @@
 
 
 def pack_kernel(*refs):
-    lasts, firsts, (last, first) = refs[:SIDE], refs[SIDE : 2 * SIDE], refs[2 * SIDE :]
-    for k in range(SIDE):
-        last[SIDE * k : SIDE * (k + 1)] = lasts[k][...]
-        first[SIDE * k : SIDE * (k + 1)] = firsts[k][...]
-
-
-def core_kernel(shears, own, two, one, three, slices, scale, out, grads, rows):
+    last, first = refs[-2:]
+    for k in range(2):
+
+        @pl.when(pl.program_id(0) == k)
+        def _():
+            last[...] = refs[2 * k][...]
+            first[...] = refs[2 * k + 1][...]
+
+
+def pack(pieces, places, rims):
+    edge = (SIDE, SH, BLOCKS, LANES)
+    ends = [
+        pl.BlockSpec(edge, lambda i: (0, STRIP // SH - 1, 0, 0)),
+        pl.BlockSpec(edge, lambda i: (0, 0, 0, 0)),
+    ]
+    start, stride = places[0], places[1] - places[0]
+    return pl.pallas_call(
+        pack_kernel,
+        grid=(2,),
+        out_shape=[jax.ShapeDtypeStruct((ANGLES, SH, BLOCKS, LANES), F32)] * 2,
+        in_specs=ends * 2 + [pl.BlockSpec(memory_space=pl.ANY)] * len(rims),
+        out_specs=[pl.BlockSpec(edge, lambda i: (start + i * stride, 0, 0, 0))] * 2,
+        input_output_aliases={4 + k: k for k in range(len(rims))},
+        compiler_params=vmem(12),
+        cost_estimate=cost(1),
+        name="pack",
+    )(pieces[0], pieces[0], pieces[1], pieces[1], *rims)
+
+
+def fill_grads(grads, pieces):
+    for k, piece in enumerate(pieces):
+        grads[SIDE * k : SIDE * (k + 1), SH : SH + STRIP] = piece[...]
+    count = SIDE * len(pieces)
+    grads[:, :SH] = jnp.zeros((count, SH, BLOCKS, LANES), F32)
+    grads[:, SH + STRIP :] = jnp.zeros((count, SH, BLOCKS, LANES), F32)
+
+
+def take_grads(starts, grads, rows, slices, scale, out):
+    chunk = 8
+    for row in range(0, STRIP, chunk):
+        total = grads[0, pl.ds(starts[0] + row, chunk)]
+        for a in range(1, len(starts)):
+            total += grads[a, pl.ds(starts[a] + row, chunk)]
+        rows[row * BLOCKS : (row + chunk) * BLOCKS] = total.reshape(chunk * BLOCKS, LANES)
+    for part in range(2):
+        for c in range(COLS):
+            total = rows[pl.ds(part * COLS + c, STRIP, stride=BLOCKS), :]
+            cols = lane_block(c)
+            out[part, :, cols] = slices[part, :, cols] - total * scale[:, cols]
+
+
+def core_kernel(shears, two, one, three, slices, scale, out, grads, rows):
     @pl.when(pl.program_id(0) == 0)
     def _():
-        for k, piece in enumerate((own, two, one, three)):
-            grads[SIDE * k : SIDE * (k + 1), SH : SH + STRIP] = piece[...]
-        grads[:, :SH] = jnp.zeros((ANGLES, SH, BLOCKS, LANES), F32)
-        grads[:, SH + STRIP :] = jnp.zeros((ANGLES, SH, BLOCKS, LANES), F32)
+        fill_grads(grads, (two, one, three))
 
     count = out.shape[0]
     base = pl.program_id(0) * count
-    chunk = 16
     for k in range(count):
-        starts = [SH - shears[a, base + k] for a in range(ANGLES)]
-        for row in range(0, STRIP, chunk):
-            total = grads[0, pl.ds(starts[0] + row, chunk)]
-            for a in range(1, ANGLES):
-                total += grads[a, pl.ds(starts[a] + row, chunk)]
-            rows[k, row * BLOCKS : (row + chunk) * BLOCKS] = total.reshape(chunk * BLOCKS, LANES)
-        for part in range(2):
-            for c in range(COLS):
-                total = rows[k, pl.ds(part * COLS + c, STRIP, stride=BLOCKS), :]
-                cols = lane_block(c)
-                out[k, part, :, cols] = slices[k, part, :, cols] - total * scale[k, :, cols]
+        starts = [SH - shears[a, base + k] for a in range(SIDE, ANGLES)]
+        take_grads(
+            starts, grads, rows.at[k], slices.at[k], scale.at[k], out.at[k]
+        )
 
 
 def rim_kernel(shears, before, after, scale, core, out, high, low, shifts):
@@ -412,9 +471,10 @@
     after = lax.ppermute(partial[:, :, :SENT], "block", down)
     wrapped = pl.pallas_call(
         fields_kernel,
-        out_shape=jax.ShapeDtypeStruct((3, COLS, WRAP, LANES), F32),
+        grid=(1,),
+        out_shape=jax.ShapeDtypeStruct((3 * SPARE, COLS, WRAP, LANES), F32),
         in_specs=[VMEM, VMEM],
-        out_specs=VMEM,
+        out_specs=pl.BlockSpec((3, COLS, WRAP, LANES), lambda i: (0, 0, 0, 0)),
         compiler_params=vmem(60),
         cost_estimate=cost(6),
         name="fields",
@@ -428,9 +488,11 @@
             jax.ShapeDtypeStruct((STRIP * BLOCKS, LANES), F32),
             jax.ShapeDtypeStruct((ANGLES * 8, LANES), F32),
         ],
-        in_specs=[SMEM] + [VMEM] * 6,
+        in_specs=[SMEM] + [VMEM] * 4 + [pl.BlockSpec(memory_space=pltpu.HBM), VMEM],
         out_specs=[VMEM, VMEM],
         scratch_shapes=[
+            pltpu.VMEM((3, COLS, WRAP, LANES), F32),
+            pltpu.SemaphoreType.DMA,
             pltpu.VMEM((2, COLS, ROWS, LANES), F32),
             pltpu.VMEM((3, COLS, ROWS, LANES), F32),
             field,
@@ -452,62 +514,56 @@
     rim_shears = all_shears.reshape(SIDE, SIDE, Z).transpose(2, 1, 0).reshape(Z, ANGLES)
     rim_shears = jnp.repeat(rim_shears, SH, axis=1)
 
-    weights = pl.pallas_call(
-        weight_kernel,
-        out_shape=jax.ShapeDtypeStruct((ANGLES, COLS, RIM_ROWS, LANES), F32),
-        in_specs=[SMEM, SMEM, VMEM],
-        out_specs=VMEM,
-        scratch_shapes=[pltpu.VMEM((COLS, WRAP, LANES), F32)],
-        compiler_params=vmem(12),
-        cost_estimate=cost(2),
-        name="weights",
-    )(strip_index, all_positions, probe_field)
     slices_spec = pl.BlockSpec((step, STRIP, NY), lambda i: (i, 0, 0))
-    scale = pl.pallas_call(
+    own, two, one, three = pieces
+    object_spec = pl.BlockSpec((step, 2, STRIP, NY), lambda i: (i, 0, 0, 0))
+    scale, rest = pl.pallas_call(
         divisor_kernel,
         grid=(Z // step,),
-        out_shape=jax.ShapeDtypeStruct((Z, STRIP, NY), F32),
-        in_specs=[SMEM, VMEM],
-        out_specs=slices_spec,
-        compiler_params=vmem(8),
+        out_shape=[
+            jax.ShapeDtypeStruct((Z, STRIP, NY), F32),
+            jax.ShapeDtypeStruct(object_field.shape, F32),
+        ],
+        in_specs=[SMEM, SMEM, SMEM, VMEM, VMEM, object_spec],
+        out_specs=[slices_spec, object_spec],
+        scratch_shapes=[
+            pltpu.VMEM((ANGLES, COLS, RIM_ROWS, LANES), F32),
+            pltpu.VMEM((COLS, WRAP, LANES), F32),
+            pltpu.VMEM((SIDE, RIM_ROWS, BLOCKS, LANES), F32),
+            pltpu.VMEM((STRIP * BLOCKS, LANES), F32),
+        ],
+        compiler_params=vmem(60),
         cost_estimate=cost(2),
         name="divisor",
-    )(all_shears, weights)
-
-    scale, rim_shears, *pieces = lax.optimization_barrier((scale, rim_shears, *pieces))
-    edge = (SIDE, SH, BLOCKS, LANES)
-    rims = pl.pallas_call(
-        pack_kernel,
-        grid=(1,),
-        out_shape=[jax.ShapeDtypeStruct((ANGLES, SH, BLOCKS, LANES), F32)] * 2,
-        in_specs=[pl.BlockSpec(edge, lambda i: (0, STRIP // SH - 1, 0, 0))] * SIDE
-        + [pl.BlockSpec(edge, lambda i: (0, 0, 0, 0))] * SIDE,
-        out_specs=[pl.BlockSpec((ANGLES, SH, BLOCKS, LANES), lambda i: (0, 0, 0, 0))] * 2,
-        compiler_params=vmem(12),
-        cost_estimate=cost(2),
-        name="pack",
-    )(*pieces, *pieces)
+    )(strip_index, all_positions, all_shears, probe_field, own, object_field)
+
+    scale, rim_shears, own, three = lax.optimization_barrier((scale, rim_shears, own, three))
+    rims = pack((own, three), (0, 3), ())
+    rims = pack((two, one), (1, 2), rims)
+    pieces = (two, one, three)
     rims = [
         lax.ppermute(rim, "block", pairs).reshape(ANGLES * SH * BLOCKS, LANES)
         for rim, pairs in zip(rims, (up, down))
     ]
 
+    step = 8
+    slices_spec = pl.BlockSpec((step, STRIP, NY), lambda i: (i, 0, 0))
     object_spec = pl.BlockSpec((step, 2, STRIP, NY), lambda i: (i, 0, 0, 0))
     core = pl.pallas_call(
         core_kernel,
         grid=(Z // step,),
         out_shape=jax.ShapeDtypeStruct(object_field.shape, F32),
-        in_specs=[SMEM] + [VMEM] * 4 + [object_spec, slices_spec],
+        in_specs=[SMEM] + [VMEM] * 3 + [object_spec, slices_spec],
         out_specs=object_spec,
         scratch_shapes=[
-            pltpu.VMEM((ANGLES, RIM_ROWS, BLOCKS, LANES), F32),
+            pltpu.VMEM((ANGLES - SIDE, RIM_ROWS, BLOCKS, LANES), F32),
             pltpu.VMEM((step, STRIP * BLOCKS, LANES), F32),
         ],
         compiler_params=vmem(50),
         cost_estimate=cost(17),
         name="core",
-    )(all_shears, *pieces, object_field, scale)
-    many = 16
+    )(all_shears, *pieces, rest, scale)
+    many = 32
     edge_spec = pl.BlockSpec((many, 2, SH, NY), lambda j, i: (i, 0, j * (STRIP // SH - 1), 0))
     return pl.pallas_call(
         rim_kernel,

time: 111 us -> 108 us (0.973)
  Pallas kernels: 63.2 us -> 68 us
  local copies, waits for them, and re-layouts: 7.73 us -> 3.91 us
  waiting for transfers between devices: 5.61 us -> 3.24 us
    pallas_call x4, Pallas kernels: 25 us -> 31.9 us  [the longest x1 22.3 us: per_device(): pl.pallas_call(divisor_kernel, grid=(Z // step,), out_shape=[jax.ShapeDty...]
    ppermute x3, waiting for transfers between devices: 4.37 us -> 0.01 us  [gather_angles(): lax.ppermute(row, axes, hop_pairs(hop, 1))]
    unnamed x14, local copies, waits for them, and re-layouts: 5.59 us -> 1.25 us
    pallas_call x1, Pallas kernels: 15 us -> 12.3 us  [per_device(): pl.pallas_call(core_kernel, grid=(Z // step,), out_shape=jax.ShapeDtypeSt...]
    pallas_call x1, Pallas kernels: 5.89 us -> 7.82 us  [per_device(): pl.pallas_call(frames_kernel, out_shape=[jax.ShapeDtypeStruct((STRIP * BL...]
    ppermute x2, waiting for transfers between devices: 0.01 us -> 1.86 us  [per_device(): lax.ppermute(rim, 'block', pairs).reshape(ANGLES * SH * BLOCKS, LANES)]
    pallas_call x1, Pallas kernels: 6.8 us -> 5.51 us  [per_device(): pl.pallas_call(rim_kernel, grid=(2, Z // many), out_shape=jax.ShapeDtypeS...]
  transfers between devices with their start and end apart: 11 -> 11, of which waited for: 2 -> 2; matrix products, arithmetic and copies ran while one was open for 2% -> 3% of each run, Pallas kernels for 41% -> 46%
where the time goes in v4:
time: 108 us; the launch traced here: 107 us
  Pallas kernels  68 us (63%)
  starting transfers between devices  19.3 us (18%)
  blocking collectives  11.8 us (11%)
  local copies, waits for them, and re-layouts  3.91 us (4%)
  waiting for transfers between devices  3.24 us (3%)
    pallas_call x1, Pallas kernels, per_device(): pl.pallas_call(divisor_kernel, grid=(Z // step,), out_shape=[jax.ShapeDty...  22.3 us
    pallas_call x1, Pallas kernels, per_device(): pl.pallas_call(core_kernel, grid=(Z // step,), out_shape=jax.ShapeDtypeSt...  12.3 us
    all_to_all x1, blocking collectives, gather_angles(): facts = lax.all_to_all(facts, 'angle', 0, 0)[:, 0]  11.8 us
    pallas_call x1, Pallas kernels, per_device(): pl.pallas_call(frames_kernel, out_shape=[jax.ShapeDtypeStruct((STRIP * BL...  7.82 us
    pallas_call x1, Pallas kernels, per_device(): pl.pallas_call(project_kernel, grid=(Z // step,), out_shape=jax.ShapeDtyp...  7.57 us
    all_to_all x1, starting transfers between devices, per_device(): observed = lax.all_to_all(moved, 'block', 0, 0)  6.81 us
    pallas_call x1, Pallas kernels, per_device(): pl.pallas_call(fields_kernel, grid=(1,), out_shape=jax.ShapeDtypeStruct((...  6.34 us
    pallas_call x1, Pallas kernels, per_device(): pl.pallas_call(rim_kernel, grid=(2, Z // many), out_shape=jax.ShapeDtypeS...  5.51 us
  transfers between devices with their start and end apart: 11, of which 2 were waited for; matrix products, arithmetic and copies ran while one was open for 3% of the time, Pallas kernels for 46%

profile of v4, /device:TPU:1, one launch (start us, length us, event | category | flops | bytes accessed | tf_op | source)
XLA Modules:
  0.0 106.7 jit_solution(18199227234421381813)
XLA Ops:
  0.0 0.0 copy-start.6
  0.0 3.0 %measured_rows.1 = f32[8,4,80,128]{3,2,1,0:T(8,128)} custom-call(s32[2]{0:T(128)} %bitcast.41, bf16[512,512]{1,0:T(8,128)(2,1)} %bitcast.33), custom_call_target="tpu_custom_call" | custom-call | bytes 9000000 | tf_op jit(solution)/shard_map/measured_rows/pallas_call | solution.py:445
  3.0 6.8 %all-to-all-start = ((f32[8,4,80,128]{3,2,1,0:T(8,128)}), f32[8,4,80,128]{3,2,1,0:T(8,128)S(1)}, u32[]{:S(2)}, u32[]{:S(2)}) async-start(f32[8,4,80,128]{3,2,1,0:T(8,128)} %measured_rows.1), calls=%async_computation | async-start | bytes 2621440 | tf_op jit(solution)/shard_map/all_to_all | solution.py:455
  9.8 7.6 %project.1.partial = f32[2,4,96,128]{3,2,1,0:T(8,128)} custom-call(s32[32]{0:T(128)} %bitcast.40, f32[32,2,64,512]{3,2,1,0:T(8,128)} %slices.3), custom_call_target="tpu_custom_call" | custom-call | bytes 21000000 | tf_op jit(solution)/shard_map/project/pallas_call | solution.py:457
  17.4 1.0 fusion.9
  18.3 1.6 %collective-permute-start = (f32[2,4,24,128]{3,2,1,0:T(8,128)S(1)}, f32[2,4,24,128]{3,2,1,0:T(8,128)S(1)}, u32[]{:S(2)}, u32[]{:S(2)}) collective-permute-start(f32[2,4,24,128]{3,2,1,0:T(8,128)S(1)} %get-tuple-element.34), channel_id=1, source_target_pairs={{0,1},{1,2},{2,3},{3,4},{4,5},{5,6},{6,7},{7,0},{8,9},{9,10},{10,1... | collective-permute-start | bytes 294920 | tf_op jit(solution)/shard_map/ppermute | solution.py:470
  20.0 0.0 collective-permute-start.1
  20.0 0.0 copy-done.6
  20.0 0.0 copy-start.2
  20.0 6.3 %fields.1 = f32[48,4,608,128]{3,2,1,0:T(8,128)} custom-call(f32[2,512,512]{2,1,0:T(8,128)} %probe.3, f32[512,512]{1,0:T(8,128)} %bitcast.31), custom_call_target="tpu_custom_call" | custom-call | bytes 18000000 | tf_op jit(solution)/shard_map/fields/pallas_call | solution.py:472
  26.3 0.1 pad.4.facts
  26.4 0.0 collective-permute-done.before
  26.4 1.4 %collective-permute-done.1.after = f32[2,4,24,128]{3,2,1,0:T(8,128)S(1)} collective-permute-done((f32[2,4,24,128]{3,2,1,0:T(8,128)S(1)}, f32[2,4,24,128]{3,2,1,0:T(8,128)S(1)}, u32[]{:S(2)}, u32[]{:S(2)}) %collective-permute-start.1) | collective-permute-done | bytes 98336 | tf_op jit(solution)/shard_map/ppermute | solution.py:471
  27.8 0.0 all-to-all-done.measured
  27.8 0.0 copy-done.2
  27.8 0.0 copy-start.5
  27.8 7.8 %frames.1 = (f32[512,128]{1,0:T(8,128)S(1)}, f32[128,128]{1,0:T(8,128)S(1)}) custom-call(s32[1]{0:T(128)} %bitcast.strip_index, f32[2,4,96,128]{3,2,1,0:T(8,128)S(1)} %copy-done.2, f32[2,4,24,128]{3,2,1,0:T(8,128)S(1)} %collective-permute-done.before, f32[2,4,24,128]{3,2,1,0:T(8,128)S(1)} %collective-permute-done.1.after, ...), custom_call_target="tpu_custom_call" | custom-call | bytes 27000000 | tf_op jit(solution)/shard_map/frames/pallas_call | solution.py:485
  35.6 2.8 %collective-permute-start.4 = (f32[64,8,128]{2,1,0:T(8,128)S(1)}, f32[64,8,128]{2,1,0:T(8,128)S(1)}, u32[]{:S(2)}, u32[]{:S(2)}) collective-permute-start(f32[64,8,128]{2,1,0:T(8,128)S(1)} %bitcast.25), channel_id=1, source_target_pairs={{0,24},{1,97},{2,26},{3,99},{4,28},{5,101},{6,30},{7,103},{8,0},{9... | collective-permute-start | bytes 786440 | tf_op jit(solution)/shard_map/ppermute | solution.py:431
  38.4 0.0 collective-permute-start.3
  38.4 1.6 %collective-permute-start.2 = (f32[64,8,128]{2,1,0:T(8,128)S(1)}, f32[64,8,128]{2,1,0:T(8,128)S(1)}, u32[]{:S(2)}, u32[]{:S(2)}) collective-permute-start(f32[64,8,128]{2,1,0:T(8,128)S(1)} %bitcast.27), channel_id=1, source_target_pairs={{0,16},{1,65},{2,18},{3,67},{4,20},{5,69},{6,22},{7,71},{8,24},{9,... | collective-permute-start | bytes 786440 | tf_op jit(solution)/shard_map/ppermute | solution.py:431
  40.1 11.8 %all_to_all.10 = f32[16,8,128]{2,1,0:T(8,128)S(1)} all-to-all(f32[16,8,128]{2,1,0:T(8,128)S(1)} %bitcast.30), channel_id=1, replica_groups=mesh['angle'=16,'block'=8] {'angle'}, dimensions={0} | all-to-all | bytes 131072 | tf_op jit(solution)/shard_map/all_to_all | solution.py:430
  51.9 0.0 collective-permute-done.4
  51.9 0.0 collective-permute-done.3
  51.9 0.0 collective-permute-done.2
  51.9 0.1 pad_maximum_fusion.own.refs_0_.refs_1_
  52.0 0.0 copy-start
  52.0 1.3 %collective-permute-start.5 = (f32[4,64,8,128]{3,2,1,0:T(8,128)S(1)}, f32[4,64,8,128]{3,2,1,0:T(8,128)S(1)}, u32[]{:S(2)}, u32[]{:S(2)}) collective-permute-start(f32[4,64,8,128]{3,2,1,0:T(8,128)S(1)} %pad_maximum_fusion.own.refs_0_.refs_1_), channel_id=1, source_target_pairs={{0,96},{1,25},{2,98},{3,27},{4,100},{5,29},{6,102},{7,31},{8,104},... | collective-permute-start | bytes 3145736 | tf_op jit(solution)/shard_map/ppermute | solution.py:433
  53.2 0.8 collective-permute-start.6
  54.1 0.0 collective-permute-start.7
  54.1 0.0 copy-done.5
  54.1 0.1 select_subtract_fusion.1
  54.1 0.1 sub.56
  54.2 0.1 sub.54
  54.3 0.1 sub.55
  54.4 0.1 sub.51
  54.5 0.6 gather_fusion
  55.1 0.1 broadcast_select_fusion
  55.2 0.0 copy-start.4
  55.2 0.7 slice.26.shears
  55.9 0.0 copy-start.3
  55.9 0.0 copy-done
  55.9 0.0 copy-done.4
  55.9 22.3 %divisor.1 = (f32[32,64,512]{2,1,0:T(8,128)}, f32[32,2,64,512]{3,2,1,0:T(8,128)}) custom-call(s32[1]{0:T(128)} %bitcast.strip_index, s32[16,16]{1,0:T(8,128)} %bitcast.37, s32[16,32]{1,0:T(8,128)} %slice.26.shears, f32[2,512,512]{2,1,0:T(8,128)} %probe.3, f32[4,64,8,128]{3,2,1,0:T(8,128)} %copy-done, f32[32,2,64,512]{3,2,1,0:T(8,128)} %slices.3), custom_call_target="tpu_custom_call" | custom-call | bytes 6000000 | tf_op jit(solution)/shard_map/divisor/pallas_call | solution.py:520
  78.1 0.0 copy-done.3
  78.1 0.0 collective-permute-done.5.refs_2_.refs_3_.three
  78.2 0.0 copy-start.1
  78.2 1.2 %copy-done.1 = f32[4,64,8,128]{3,2,1,0:T(8,128)S(1)} copy-done((f32[4,64,8,128]{3,2,1,0:T(8,128)S(1)}, f32[4,64,8,128]{3,2,1,0:T(8,128)}, u32[]{:S(2)}) %copy-start.1) | copy-done | bytes 1048600
  79.4 1.1 %pack.2 = (f32[16,16,8,128]{3,2,1,0:T(8,128)}, f32[16,16,8,128]{3,2,1,0:T(8,128)}) custom-call(f32[4,64,8,128]{3,2,1,0:T(8,128)S(1)} %copy-done.1, f32[4,64,8,128]{3,2,1,0:T(8,128)S(1)} %copy-done.1, f32[4,64,8,128]{3,2,1,0:T(8,128)S(1)} %collective-permute-done.5.refs_2_.refs_3_.three, f32[4,64,8,128]{3,2,1,0:T(8,128)S(1)} %collective-permute-done.5.refs_2_.refs_3_.three), custom_call_target="tpu_custom_call" | custom-call | bytes 3000000 | tf_op jit(solution)/shard_map/pack/pallas_call | solution.py:331
  80.5 0.0 collective-permute-done.6.refs_0_.refs_1_.two
  80.5 0.0 collective-permute-done.7.refs_2_.refs_3_.one
  80.5 2.1 %pack.3 = (f32[16,16,8,128]{3,2,1,0:T(8,128)}, f32[16,16,8,128]{3,2,1,0:T(8,128)}) custom-call(f32[4,64,8,128]{3,2,1,0:T(8,128)S(1)} %collective-permute-done.6.refs_0_.refs_1_.two, f32[4,64,8,128]{3,2,1,0:T(8,128)S(1)} %collective-permute-done.6.refs_0_.refs_1_.two, ...), custom_call_target="tpu_custom_call", output_to_operand_aliasing={{0}: (4, {}), {1}: (5, {})} | custom-call | bytes 3000000 | tf_op jit(solution)/shard_map/pack/pallas_call | solution.py:331
  82.6 3.8 %collective-permute-start.8 = (f32[16,16,8,128]{3,2,1,0:T(8,128)}, f32[16,16,8,128]{3,2,1,0:T(8,128)S(1)}, u32[]{:S(2)}, u32[]{:S(2)}) collective-permute-start(f32[16,16,8,128]{3,2,1,0:T(8,128)} %get-tuple-element.29), channel_id=1, source_target_pairs={{0,1},{1,2},{2,3},{3,4},{4,5},{5,6},{6,7},{7,0},{8,9},{9,10},{10,1... | collective-permute-start | bytes 3145736 | tf_op jit(solution)/shard_map/ppermute | solution.py:545
  86.4 0.5 collective-permute-start.9
  86.9 0.1 copy.18.shears
  87.0 12.3 %core.1 = f32[32,2,64,512]{3,2,1,0:T(8,128)} custom-call(s32[16,32]{1,0:T(8,128)S(1)} %copy-done.3, f32[4,64,8,128]{3,2,1,0:T(8,128)S(1)} %collective-permute-done.6.refs_0_.refs_1_.two, f32[4,64,8,128]{3,2,1,0:T(8,128)} %collective-permute-done.7.refs_2_.refs_3_.one, f32[4,64,8,128]{3,2,1,0:T(8,128)S(1)} %collective-permute-done.5.refs_2_.refs_3_.three, ...), custom_call_target="tpu_custom_call" | custom-call | bytes 51000000 | tf_op jit(solution)/shard_map/core/pallas_call | solution.py:552
  99.3 0.0 collective-permute-done.8
  99.3 1.9 %collective-permute-done.9 = f32[16,16,8,128]{3,2,1,0:T(8,128)} collective-permute-done((f32[16,16,8,128]{3,2,1,0:T(8,128)}, f32[16,16,8,128]{3,2,1,0:T(8,128)}, u32[]{:S(2)}, u32[]{:S(2)}) %collective-permute-start.9) | collective-permute-done | bytes 1048608 | tf_op jit(solution)/shard_map/ppermute | solution.py:545
  101.1 5.5 %rim.1 = f32[32,2,64,512]{3,2,1,0:T(8,128)} custom-call(s32[32,256]{1,0:T(8,128)S(1)} %copy.18.shears, f32[2048,128]{1,0:T(8,128)S(1)} %bitcast.24, f32[2048,128]{1,0:T(8,128)} %bitcast.18.after, f32[32,64,512]{2,1,0:T(8,128)} %get-tuple-element.31.scale, f32[32,2,64,512]{3,2,1,0:T(8,128)} %core.1), custom_call_target="tpu_custom_call", output_to_operand_aliasing={{}: (4, {})} | custom-call | bytes 27000000 | tf_op jit(solution)/shard_map/rim/pallas_call | solution.py:568
  (8 shorter events, 0.1 us)
Async XLA Ops:
  0.0 20.0 %copy-start.6 = (s32[1,32]{1,0:T(1,128)S(1)}, s32[1,32]{1,0:T(1,128)}, u32[]{:S(2)}) copy-start(s32[1,32]{1,0:T(1,128)} %param.9) | copy-start | bytes 388
  3.0 24.8 %all-to-all-start = ((f32[8,4,80,128]{3,2,1,0:T(8,128)}), f32[8,4,80,128]{3,2,1,0:T(8,128)S(1)}, u32[]{:S(2)}, u32[]{:S(2)}) async-start(f32[8,4,80,128]{3,2,1,0:T(8,128)} %measured_rows.1), calls=%async_computation | async-start | bytes 2621440 | tf_op jit(solution)/shard_map/all_to_all | solution.py:455
  18.3 8.1 %collective-permute-start = (f32[2,4,24,128]{3,2,1,0:T(8,128)S(1)}, f32[2,4,24,128]{3,2,1,0:T(8,128)S(1)}, u32[]{:S(2)}, u32[]{:S(2)}) collective-permute-start(f32[2,4,24,128]{3,2,1,0:T(8,128)S(1)} %get-tuple-element.34), channel_id=1, source_target_pairs={{0,1},{1,2},{2,3},{3,4},{4,5},{5,6},{6,7},{7,0},{8,9},{9,10},{10,1... | collective-permute-start | bytes 294920 | tf_op jit(solution)/shard_map/ppermute | solution.py:470
  20.0 7.8 %collective-permute-start.1 = (f32[2,4,24,128]{3,2,1,0:T(8,128)S(1)}, f32[2,4,24,128]{3,2,1,0:T(8,128)S(1)}, u32[]{:S(2)}, u32[]{:S(2)}) collective-permute-start(f32[2,4,24,128]{3,2,1,0:T(8,128)S(1)} %get-tuple-element.33), channel_id=1, source_target_pairs={{1,0},{2,1},{3,2},{4,3},{5,4},{6,5},{7,6},{0,7},{9,8},{10,9},{11,1... | collective-permute-start | bytes 294920 | tf_op jit(solution)/shard_map/ppermute | solution.py:471
  20.0 7.8 %copy-start.2 = (f32[2,4,96,128]{3,2,1,0:T(8,128)S(1)}, f32[2,4,96,128]{3,2,1,0:T(8,128)}, u32[]{:S(2)}) copy-start(f32[2,4,96,128]{3,2,1,0:T(8,128)} %project.1.partial) | copy-start | bytes 1179652
  27.8 26.3 %copy-start.5 = (s32[4]{0:T(128)S(1)}, s32[4]{0:T(128)}, u32[]{:S(2)}) copy-start(s32[4]{0:T(128)} %constant.78.clone) | copy-start | bytes 52
  35.6 16.3 %collective-permute-start.4 = (f32[64,8,128]{2,1,0:T(8,128)S(1)}, f32[64,8,128]{2,1,0:T(8,128)S(1)}, u32[]{:S(2)}, u32[]{:S(2)}) collective-permute-start(f32[64,8,128]{2,1,0:T(8,128)S(1)} %bitcast.25), channel_id=1, source_target_pairs={{0,24},{1,97},{2,26},{3,99},{4,28},{5,101},{6,30},{7,103},{8,0},{9... | collective-permute-start | bytes 786440 | tf_op jit(solution)/shard_map/ppermute | solution.py:431
  38.4 13.5 %collective-permute-start.3 = (f32[64,8,128]{2,1,0:T(8,128)S(1)}, f32[64,8,128]{2,1,0:T(8,128)S(1)}, u32[]{:S(2)}, u32[]{:S(2)}) collective-permute-start(f32[64,8,128]{2,1,0:T(8,128)S(1)} %bitcast.26), channel_id=1, source_target_pairs={{0,8},{1,33},{2,10},{3,35},{4,12},{5,37},{6,14},{7,39},{8,16},{9,4... | collective-permute-start | bytes 786440 | tf_op jit(solution)/shard_map/ppermute | solution.py:431
  38.4 13.5 %collective-permute-start.2 = (f32[64,8,128]{2,1,0:T(8,128)S(1)}, f32[64,8,128]{2,1,0:T(8,128)S(1)}, u32[]{:S(2)}, u32[]{:S(2)}) collective-permute-start(f32[64,8,128]{2,1,0:T(8,128)S(1)} %bitcast.27), channel_id=1, source_target_pairs={{0,16},{1,65},{2,18},{3,67},{4,20},{5,69},{6,22},{7,71},{8,24},{9,... | collective-permute-start | bytes 786440 | tf_op jit(solution)/shard_map/ppermute | solution.py:431
  52.0 3.9 %copy-start = (f32[4,64,8,128]{3,2,1,0:T(8,128)}, f32[4,64,8,128]{3,2,1,0:T(8,128)S(1)}, u32[]{:S(2)}) copy-start(f32[4,64,8,128]{3,2,1,0:T(8,128)S(1)} %pad_maximum_fusion.own.refs_0_.refs_1_) | copy-start | bytes 3145732
  52.0 26.2 %collective-permute-start.5 = (f32[4,64,8,128]{3,2,1,0:T(8,128)S(1)}, f32[4,64,8,128]{3,2,1,0:T(8,128)S(1)}, u32[]{:S(2)}, u32[]{:S(2)}) collective-permute-start(f32[4,64,8,128]{3,2,1,0:T(8,128)S(1)} %pad_maximum_fusion.own.refs_0_.refs_1_), channel_id=1, source_target_pairs={{0,96},{1,25},{2,98},{3,27},{4,100},{5,29},{6,102},{7,31},{8,104},... | collective-permute-start | bytes 3145736 | tf_op jit(solution)/shard_map/ppermute | solution.py:433
  53.2 27.3 %collective-permute-start.6 = (f32[4,64,8,128]{3,2,1,0:T(8,128)S(1)}, f32[4,64,8,128]{3,2,1,0:T(8,128)S(1)}, u32[]{:S(2)}, u32[]{:S(2)}) collective-permute-start(f32[4,64,8,128]{3,2,1,0:T(8,128)S(1)} %pad_maximum_fusion.own.refs_0_.refs_1_), channel_id=1, source_target_pairs={{0,64},{1,17},{2,66},{3,19},{4,68},{5,21},{6,70},{7,23},{8,72},{9,... | collective-permute-start | bytes 3145736 | tf_op jit(solution)/shard_map/ppermute | solution.py:433
  54.1 26.4 %collective-permute-start.7 = (f32[4,64,8,128]{3,2,1,0:T(8,128)S(1)}, f32[4,64,8,128]{3,2,1,0:T(8,128)}, u32[]{:S(2)}, u32[]{:S(2)}) collective-permute-start(f32[4,64,8,128]{3,2,1,0:T(8,128)S(1)} %pad_maximum_fusion.own.refs_0_.refs_1_), channel_id=1, source_target_pairs={{0,32},{1,9},{2,34},{3,11},{4,36},{5,13},{6,38},{7,15},{8,40},{9,1... | collective-permute-start | bytes 3145736 | tf_op jit(solution)/shard_map/ppermute | solution.py:433
  55.2 0.7 copy-start.4
  55.9 22.3 %copy-start.3 = (s32[16,32]{1,0:T(8,128)S(1)}, s32[16,32]{1,0:T(8,128)}, u32[]{:S(2)}) copy-start(s32[16,32]{1,0:T(8,128)} %slice.26.shears) | copy-start | bytes 6148
  78.2 1.2 %copy-start.1 = (f32[4,64,8,128]{3,2,1,0:T(8,128)S(1)}, f32[4,64,8,128]{3,2,1,0:T(8,128)}, u32[]{:S(2)}) copy-start(f32[4,64,8,128]{3,2,1,0:T(8,128)} %copy-done) | copy-start | bytes 3145732
  82.6 16.6 %collective-permute-start.8 = (f32[16,16,8,128]{3,2,1,0:T(8,128)}, f32[16,16,8,128]{3,2,1,0:T(8,128)S(1)}, u32[]{:S(2)}, u32[]{:S(2)}) collective-permute-start(f32[16,16,8,128]{3,2,1,0:T(8,128)} %get-tuple-element.29), channel_id=1, source_target_pairs={{0,1},{1,2},{2,3},{3,4},{4,5},{5,6},{6,7},{7,0},{8,9},{9,10},{10,1... | collective-permute-start | bytes 3145736 | tf_op jit(solution)/shard_map/ppermute | solution.py:545
  86.4 14.7 %collective-permute-start.9 = (f32[16,16,8,128]{3,2,1,0:T(8,128)}, f32[16,16,8,128]{3,2,1,0:T(8,128)}, u32[]{:S(2)}, u32[]{:S(2)}) collective-permute-start(f32[16,16,8,128]{3,2,1,0:T(8,128)} %get-tuple-element.30), channel_id=1, source_target_pairs={{1,0},{2,1},{3,2},{4,3},{5,4},{6,5},{7,6},{0,7},{9,8},{10,9},{11,1... | collective-permute-start | bytes 3145736 | tf_op jit(solution)/shard_map/ppermute | solution.py:545

commit v5 on v4

--- a/solution.py
+++ b/solution.py
@@ -16,6 +16,8 @@
 COLS = NY // LANES
 BASE = 8
 ROWS = STRIP + 2 * BASE
+SEEN_BASE = 4
+SEEN_ROWS = STRIP + 2 * SEEN_BASE
 RIM_ROWS = STRIP + 2 * SH
 SENT = BASE + SH
 WRAP = NX + RIM_ROWS
@@ -89,8 +91,8 @@
         wrapped, (), jnp.dot(measured[...], interleave(), preferred_element_type=F32)
     )
     for strip in range(FRAMES):
-        first_row = (strip * STRIP - BASE - position[0]) & (NX - 1)
-        for c, block in enumerate(interleaved_roll(wrapped, (), first_row, ROWS, position[1])):
+        first_row = (strip * STRIP - SEEN_BASE - position[0]) & (NX - 1)
+        for c, block in enumerate(interleaved_roll(wrapped, (), first_row, SEEN_ROWS, position[1])):
             out[strip, c] = block
         for k in range(2):
             out[strip, 0, k : k + 1] = jnp.full((1, LANES), position[k].astype(F32), F32)
@@ -120,10 +122,20 @@
                 out[part, c] = image[:, lane_block(c)]
 
 
-def fields_kernel(probe, kappa, out):
-    matrix = interleave()
-    for k in range(3):
-        load_wrapped(out, (k,), permuted(probe[k] if k < 2 else kappa[...], matrix))
+def fields_kernel(probe, kappa, out, matrix):
+    step = pl.program_id(0)
+
+    @pl.when(step == 0)
+    def _():
+        matrix[...] = interleave()
+
+    @pl.when(step < 2)
+    def _():
+        load_wrapped(out, (0,), permuted(probe[0], matrix[...]))
+
+    @pl.when(step == 2)
+    def _():
+        load_wrapped(out, (0,), permuted(kappa[...], matrix[...]))
 
 
 def frames_kernel(
@@ -165,7 +177,7 @@
         field[:, :, pad + ROWS :] = jnp.zeros((2, COLS, pad, LANES), F32)
     tile = 16
 
-    def laplace(field, part, row):
+    def laplace(field, part, row, tile=tile):
         centre = field[part, :, pl.ds(row, tile)]
         around = field[part, :, pl.ds(row - 1, tile)] + field[part, :, pl.ds(row + 1, tile)]
         left = jnp.concatenate([pltpu.roll(centre[COLS - 1 :], 1, 2), centre[: COLS - 1]], axis=0)
@@ -193,14 +205,15 @@
             kappa = local[2, :, rows]
             field_b[0, :, padded] = re - kappa * lap_im
             field_b[1, :, padded] = im + kappa * lap_re
-        for row in tiles:
-            rows, padded = pl.ds(row, tile), pl.ds(row + pad, tile)
-            re, lap_re = laplace(field_b, 0, row + pad)
-            im, lap_im = laplace(field_b, 1, row + pad)
+        for seen in range(0, SEEN_ROWS, 8):
+            row = seen + BASE - SEEN_BASE
+            rows, padded = pl.ds(row, 8), pl.ds(row + pad, 8)
+            re, lap_re = laplace(field_b, 0, row + pad, 8)
+            im, lap_im = laplace(field_b, 1, row + pad, 8)
             kappa = local[2, :, rows]
             wave_re = re - kappa * lap_im
             wave_im = im + kappa * lap_re
-            twice = 2.0 * (wave_re * wave_re + wave_im * wave_im - measured[frame, :, rows])
+            twice = 2.0 * (wave_re * wave_re + wave_im * wave_im - measured[frame, :, pl.ds(seen, 8)])
             grad_re, grad_im = twice * wave_re, twice * wave_im
             field_a[0, :, padded] = grad_re
             field_a[1, :, padded] = grad_im
@@ -444,7 +457,7 @@
     strip_index = lax.axis_index("block").astype(jnp.int32)[None]
     moved = pl.pallas_call(
         measured_kernel,
-        out_shape=jax.ShapeDtypeStruct((FRAMES, COLS, ROWS, LANES), F32),
+        out_shape=jax.ShapeDtypeStruct((FRAMES, COLS, SEEN_ROWS, LANES), F32),
         in_specs=[SMEM, VMEM],
         out_specs=VMEM,
         scratch_shapes=[pltpu.VMEM((COLS, WRAP, LANES), F32)],
@@ -453,7 +466,7 @@
         name="measured_rows",
     )(positions[0, 0], measured[0, 0])
     observed = lax.all_to_all(moved, "block", 0, 0)
-    step = 4
+    step = 8
     partial = pl.pallas_call(
         project_kernel,
         grid=(Z // step,),
@@ -464,6 +477,7 @@
         cost_estimate=cost(7),
         name="project",
     )(shears[0], object_field)
+    step = 4
     count = FRAMES
     up = [(i, (i + 1) % count) for i in range(count)]
     down = [(j, i) for i, j in up]
@@ -471,10 +485,14 @@
     after = lax.ppermute(partial[:, :, :SENT], "block", down)
     wrapped = pl.pallas_call(
         fields_kernel,
-        grid=(1,),
+        grid=(3,),
         out_shape=jax.ShapeDtypeStruct((3 * SPARE, COLS, WRAP, LANES), F32),
-        in_specs=[VMEM, VMEM],
-        out_specs=pl.BlockSpec((3, COLS, WRAP, LANES), lambda i: (0, 0, 0, 0)),
+        in_specs=[
+            pl.BlockSpec((1, NX, NY), lambda i: (jnp.minimum(i, 1), 0, 0)),
+            pl.BlockSpec((NX, NY), lambda i: (0, 0)),
+        ],
+        out_specs=pl.BlockSpec((1, COLS, WRAP, LANES), lambda i: (i, 0, 0, 0)),
+        scratch_shapes=[pltpu.VMEM((NY, NY), BF16)],
         compiler_params=vmem(60),
         cost_estimate=cost(6),
         name="fields",

time: 108 us -> 106 us (0.981)
  Pallas kernels: 68 us -> 65.8 us
    pallas_call x1, Pallas kernels: 7.57 us -> 6.01 us  [per_device(): pl.pallas_call(project_kernel, grid=(Z // step,), out_shape=jax.ShapeDtyp...]
  transfers between devices with their start and end apart: 11 -> 11, of which waited for: 2 -> 2; matrix products, arithmetic and copies ran while one was open for 3% -> 3% of each run, Pallas kernels for 46% -> 45%
where the time goes in v5:
time: 106 us; the launch traced here: 105 us
  Pallas kernels  65.8 us (62%)
  starting transfers between devices  19.3 us (18%)
  blocking collectives  11.8 us (11%)
  waiting for transfers between devices  3.95 us (4%)
  local copies, waits for them, and re-layouts  3.91 us (4%)
    pallas_call x1, Pallas kernels, per_device(): pl.pallas_call(divisor_kernel, grid=(Z // step,), out_shape=[jax.ShapeDty...  22.3 us
    pallas_call x1, Pallas kernels, per_device(): pl.pallas_call(core_kernel, grid=(Z // step,), out_shape=jax.ShapeDtypeSt...  12.3 us
    all_to_all x1, blocking collectives, gather_angles(): facts = lax.all_to_all(facts, 'angle', 0, 0)[:, 0]  11.8 us
    pallas_call x1, Pallas kernels, per_device(): pl.pallas_call(frames_kernel, out_shape=[jax.ShapeDtypeStruct((STRIP * BL...  7.81 us
    all_to_all x1, starting transfers between devices, per_device(): observed = lax.all_to_all(moved, 'block', 0, 0)  6.81 us
    pallas_call x1, Pallas kernels, per_device(): pl.pallas_call(project_kernel, grid=(Z // step,), out_shape=jax.ShapeDtyp...  6.01 us
    pallas_call x1, Pallas kernels, per_device(): pl.pallas_call(fields_kernel, grid=(3,), out_shape=jax.ShapeDtypeStruct((...  5.79 us
    pallas_call x1, Pallas kernels, per_device(): pl.pallas_call(rim_kernel, grid=(2, Z // many), out_shape=jax.ShapeDtypeS...  5.51 us
  transfers between devices with their start and end apart: 11, of which 2 were waited for; matrix products, arithmetic and copies ran while one was open for 3% of the time, Pallas kernels for 45%

profile of v5, /device:TPU:1, one launch (start us, length us, event | category | flops | bytes accessed | tf_op | source)
XLA Modules:
  0.0 105.2 jit_solution(12528346778095856657)
XLA Ops:
  0.0 0.0 copy-start.6
  0.0 2.9 %measured_rows.1 = f32[8,4,72,128]{3,2,1,0:T(8,128)} custom-call(s32[2]{0:T(128)} %bitcast.40, bf16[512,512]{1,0:T(8,128)(2,1)} %bitcast.33), custom_call_target="tpu_custom_call" | custom-call | bytes 9000000 | tf_op jit(solution)/shard_map/measured_rows/pallas_call | solution.py:458
  2.9 6.8 %all-to-all-start = ((f32[8,4,72,128]{3,2,1,0:T(8,128)}), f32[8,4,72,128]{3,2,1,0:T(8,128)S(1)}, u32[]{:S(2)}, u32[]{:S(2)}) async-start(f32[8,4,72,128]{3,2,1,0:T(8,128)} %measured_rows.1), calls=%async_computation | async-start | bytes 2359296 | tf_op jit(solution)/shard_map/all_to_all | solution.py:468
  9.7 6.0 %project.1.partial = f32[2,4,96,128]{3,2,1,0:T(8,128)} custom-call(s32[32]{0:T(128)} %bitcast.41, f32[32,2,64,512]{3,2,1,0:T(8,128)} %slices.3), custom_call_target="tpu_custom_call" | custom-call | bytes 21000000 | tf_op jit(solution)/shard_map/project/pallas_call | solution.py:470
  15.7 1.0 fusion.9
  16.7 1.6 %collective-permute-start = (f32[2,4,24,128]{3,2,1,0:T(8,128)S(1)}, f32[2,4,24,128]{3,2,1,0:T(8,128)S(1)}, u32[]{:S(2)}, u32[]{:S(2)}) collective-permute-start(f32[2,4,24,128]{3,2,1,0:T(8,128)S(1)} %get-tuple-element.34), channel_id=1, source_target_pairs={{0,1},{1,2},{2,3},{3,4},{4,5},{5,6},{6,7},{7,0},{8,9},{9,10},{10,1... | collective-permute-start | bytes 294920 | tf_op jit(solution)/shard_map/ppermute | solution.py:484
  18.3 0.0 collective-permute-start.1
  18.3 0.0 copy-done.6
  18.3 0.0 copy-start.2
  18.3 5.8 %fields.1 = f32[48,4,608,128]{3,2,1,0:T(8,128)} custom-call(f32[2,512,512]{2,1,0:T(8,128)} %probe.3, f32[512,512]{1,0:T(8,128)} %bitcast.31), custom_call_target="tpu_custom_call" | custom-call | bytes 18000000 | tf_op jit(solution)/shard_map/fields/pallas_call | solution.py:486
  24.1 0.1 pad.4.facts
  24.2 0.0 collective-permute-done.before
  24.2 2.1 %collective-permute-done.1.after = f32[2,4,24,128]{3,2,1,0:T(8,128)S(1)} collective-permute-done((f32[2,4,24,128]{3,2,1,0:T(8,128)S(1)}, f32[2,4,24,128]{3,2,1,0:T(8,128)S(1)}, u32[]{:S(2)}, u32[]{:S(2)}) %collective-permute-start.1) | collective-permute-done | bytes 98336 | tf_op jit(solution)/shard_map/ppermute | solution.py:485
  26.3 0.0 all-to-all-done.measured
  26.3 0.0 copy-done.2
  26.3 0.0 copy-start.5
  26.3 7.8 %frames.1 = (f32[512,128]{1,0:T(8,128)S(1)}, f32[128,128]{1,0:T(8,128)S(1)}) custom-call(s32[1]{0:T(128)} %bitcast.strip_index, f32[2,4,96,128]{3,2,1,0:T(8,128)S(1)} %copy-done.2, f32[2,4,24,128]{3,2,1,0:T(8,128)S(1)} %collective-permute-done.before, f32[2,4,24,128]{3,2,1,0:T(8,128)S(1)} %collective-permute-done.1.after, ...), custom_call_target="tpu_custom_call" | custom-call | bytes 27000000 | tf_op jit(solution)/shard_map/frames/pallas_call | solution.py:503
  34.1 2.8 %collective-permute-start.4 = (f32[64,8,128]{2,1,0:T(8,128)S(1)}, f32[64,8,128]{2,1,0:T(8,128)S(1)}, u32[]{:S(2)}, u32[]{:S(2)}) collective-permute-start(f32[64,8,128]{2,1,0:T(8,128)S(1)} %bitcast.25), channel_id=1, source_target_pairs={{0,24},{1,97},{2,26},{3,99},{4,28},{5,101},{6,30},{7,103},{8,0},{9... | collective-permute-start | bytes 786440 | tf_op jit(solution)/shard_map/ppermute | solution.py:444
  36.9 0.0 collective-permute-start.3
  36.9 1.6 %collective-permute-start.2 = (f32[64,8,128]{2,1,0:T(8,128)S(1)}, f32[64,8,128]{2,1,0:T(8,128)S(1)}, u32[]{:S(2)}, u32[]{:S(2)}) collective-permute-start(f32[64,8,128]{2,1,0:T(8,128)S(1)} %bitcast.27), channel_id=1, source_target_pairs={{0,16},{1,65},{2,18},{3,67},{4,20},{5,69},{6,22},{7,71},{8,24},{9,... | collective-permute-start | bytes 786440 | tf_op jit(solution)/shard_map/ppermute | solution.py:444
  38.6 11.8 %all_to_all.10 = f32[16,8,128]{2,1,0:T(8,128)S(1)} all-to-all(f32[16,8,128]{2,1,0:T(8,128)S(1)} %bitcast.30), channel_id=1, replica_groups=mesh['angle'=16,'block'=8] {'angle'}, dimensions={0} | all-to-all | bytes 131072 | tf_op jit(solution)/shard_map/all_to_all | solution.py:443
  50.4 0.0 collective-permute-done.4
  50.4 0.0 collective-permute-done.3
  50.4 0.0 collective-permute-done.2
  50.4 0.1 pad_maximum_fusion.own.refs_0_.refs_1_
  50.5 0.0 copy-start
  50.5 1.3 %collective-permute-start.5 = (f32[4,64,8,128]{3,2,1,0:T(8,128)S(1)}, f32[4,64,8,128]{3,2,1,0:T(8,128)S(1)}, u32[]{:S(2)}, u32[]{:S(2)}) collective-permute-start(f32[4,64,8,128]{3,2,1,0:T(8,128)S(1)} %pad_maximum_fusion.own.refs_0_.refs_1_), channel_id=1, source_target_pairs={{0,96},{1,25},{2,98},{3,27},{4,100},{5,29},{6,102},{7,31},{8,104},... | collective-permute-start | bytes 3145736 | tf_op jit(solution)/shard_map/ppermute | solution.py:446
  51.8 0.8 collective-permute-start.6
  52.6 0.0 collective-permute-start.7
  52.6 0.0 copy-done.5
  52.6 0.1 select_subtract_fusion.1
  52.7 0.1 sub.56
  52.7 0.1 sub.54
  52.8 0.1 sub.55
  52.9 0.1 sub.51
  53.1 0.6 gather_fusion
  53.6 0.1 broadcast_select_fusion
  53.7 0.0 copy-start.4
  53.7 0.7 slice.26.shears
  54.4 0.0 copy-start.3
  54.4 0.0 copy-done
  54.4 0.0 copy-done.4
  54.4 22.3 %divisor.1 = (f32[32,64,512]{2,1,0:T(8,128)}, f32[32,2,64,512]{3,2,1,0:T(8,128)}) custom-call(s32[1]{0:T(128)} %bitcast.strip_index, s32[16,16]{1,0:T(8,128)} %bitcast.37, s32[16,32]{1,0:T(8,128)} %slice.26.shears, f32[2,512,512]{2,1,0:T(8,128)} %probe.3, f32[4,64,8,128]{3,2,1,0:T(8,128)} %copy-done, f32[32,2,64,512]{3,2,1,0:T(8,128)} %slices.3), custom_call_target="tpu_custom_call" | custom-call | bytes 6000000 | tf_op jit(solution)/shard_map/divisor/pallas_call | solution.py:538
  76.6 0.0 copy-done.3
  76.7 0.0 collective-permute-done.5.refs_2_.refs_3_.three
  76.7 0.0 copy-start.1
  76.7 1.2 %copy-done.1 = f32[4,64,8,128]{3,2,1,0:T(8,128)S(1)} copy-done((f32[4,64,8,128]{3,2,1,0:T(8,128)S(1)}, f32[4,64,8,128]{3,2,1,0:T(8,128)}, u32[]{:S(2)}) %copy-start.1) | copy-done | bytes 1048600
  77.9 1.1 %pack.2 = (f32[16,16,8,128]{3,2,1,0:T(8,128)}, f32[16,16,8,128]{3,2,1,0:T(8,128)}) custom-call(f32[4,64,8,128]{3,2,1,0:T(8,128)S(1)} %copy-done.1, f32[4,64,8,128]{3,2,1,0:T(8,128)S(1)} %copy-done.1, f32[4,64,8,128]{3,2,1,0:T(8,128)S(1)} %collective-permute-done.5.refs_2_.refs_3_.three, f32[4,64,8,128]{3,2,1,0:T(8,128)S(1)} %collective-permute-done.5.refs_2_.refs_3_.three), custom_call_target="tpu_custom_call" | custom-call | bytes 3000000 | tf_op jit(solution)/shard_map/pack/pallas_call | solution.py:344
  79.0 0.0 collective-permute-done.6.refs_0_.refs_1_.two
  79.0 0.0 collective-permute-done.7.refs_2_.refs_3_.one
  79.0 2.1 %pack.3 = (f32[16,16,8,128]{3,2,1,0:T(8,128)}, f32[16,16,8,128]{3,2,1,0:T(8,128)}) custom-call(f32[4,64,8,128]{3,2,1,0:T(8,128)S(1)} %collective-permute-done.6.refs_0_.refs_1_.two, f32[4,64,8,128]{3,2,1,0:T(8,128)S(1)} %collective-permute-done.6.refs_0_.refs_1_.two, ...), custom_call_target="tpu_custom_call", output_to_operand_aliasing={{0}: (4, {}), {1}: (5, {})} | custom-call | bytes 3000000 | tf_op jit(solution)/shard_map/pack/pallas_call | solution.py:344
  81.2 3.8 %collective-permute-start.8 = (f32[16,16,8,128]{3,2,1,0:T(8,128)}, f32[16,16,8,128]{3,2,1,0:T(8,128)S(1)}, u32[]{:S(2)}, u32[]{:S(2)}) collective-permute-start(f32[16,16,8,128]{3,2,1,0:T(8,128)} %get-tuple-element.29), channel_id=1, source_target_pairs={{0,1},{1,2},{2,3},{3,4},{4,5},{5,6},{6,7},{7,0},{8,9},{9,10},{10,1... | collective-permute-start | bytes 3145736 | tf_op jit(solution)/shard_map/ppermute | solution.py:563
  84.9 0.5 collective-permute-start.9
  85.5 0.1 copy.18.shears
  85.5 12.3 %core.1 = f32[32,2,64,512]{3,2,1,0:T(8,128)} custom-call(s32[16,32]{1,0:T(8,128)S(1)} %copy-done.3, f32[4,64,8,128]{3,2,1,0:T(8,128)S(1)} %collective-permute-done.6.refs_0_.refs_1_.two, f32[4,64,8,128]{3,2,1,0:T(8,128)} %collective-permute-done.7.refs_2_.refs_3_.one, f32[4,64,8,128]{3,2,1,0:T(8,128)S(1)} %collective-permute-done.5.refs_2_.refs_3_.three, ...), custom_call_target="tpu_custom_call" | custom-call | bytes 51000000 | tf_op jit(solution)/shard_map/core/pallas_call | solution.py:570
  97.8 0.0 collective-permute-done.8
  97.8 1.9 %collective-permute-done.9 = f32[16,16,8,128]{3,2,1,0:T(8,128)} collective-permute-done((f32[16,16,8,128]{3,2,1,0:T(8,128)}, f32[16,16,8,128]{3,2,1,0:T(8,128)}, u32[]{:S(2)}, u32[]{:S(2)}) %collective-permute-start.9) | collective-permute-done | bytes 1048608 | tf_op jit(solution)/shard_map/ppermute | solution.py:563
  99.7 5.5 %rim.1 = f32[32,2,64,512]{3,2,1,0:T(8,128)} custom-call(s32[32,256]{1,0:T(8,128)S(1)} %copy.18.shears, f32[2048,128]{1,0:T(8,128)S(1)} %bitcast.24, f32[2048,128]{1,0:T(8,128)} %bitcast.18.after, f32[32,64,512]{2,1,0:T(8,128)} %get-tuple-element.31.scale, f32[32,2,64,512]{3,2,1,0:T(8,128)} %core.1), custom_call_target="tpu_custom_call", output_to_operand_aliasing={{}: (4, {})} | custom-call | bytes 27000000 | tf_op jit(solution)/shard_map/rim/pallas_call | solution.py:586
  (8 shorter events, 0.1 us)
Async XLA Ops:
  0.0 18.3 %copy-start.6 = (s32[1,32]{1,0:T(1,128)S(1)}, s32[1,32]{1,0:T(1,128)}, u32[]{:S(2)}) copy-start(s32[1,32]{1,0:T(1,128)} %param.9) | copy-start | bytes 388
  2.9 23.4 %all-to-all-start = ((f32[8,4,72,128]{3,2,1,0:T(8,128)}), f32[8,4,72,128]{3,2,1,0:T(8,128)S(1)}, u32[]{:S(2)}, u32[]{:S(2)}) async-start(f32[8,4,72,128]{3,2,1,0:T(8,128)} %measured_rows.1), calls=%async_computation | async-start | bytes 2359296 | tf_op jit(solution)/shard_map/all_to_all | solution.py:468
  16.7 7.5 %collective-permute-start = (f32[2,4,24,128]{3,2,1,0:T(8,128)S(1)}, f32[2,4,24,128]{3,2,1,0:T(8,128)S(1)}, u32[]{:S(2)}, u32[]{:S(2)}) collective-permute-start(f32[2,4,24,128]{3,2,1,0:T(8,128)S(1)} %get-tuple-element.34), channel_id=1, source_target_pairs={{0,1},{1,2},{2,3},{3,4},{4,5},{5,6},{6,7},{7,0},{8,9},{9,10},{10,1... | collective-permute-start | bytes 294920 | tf_op jit(solution)/shard_map/ppermute | solution.py:484
  18.3 8.0 %collective-permute-start.1 = (f32[2,4,24,128]{3,2,1,0:T(8,128)S(1)}, f32[2,4,24,128]{3,2,1,0:T(8,128)S(1)}, u32[]{:S(2)}, u32[]{:S(2)}) collective-permute-start(f32[2,4,24,128]{3,2,1,0:T(8,128)S(1)} %get-tuple-element.33), channel_id=1, source_target_pairs={{1,0},{2,1},{3,2},{4,3},{5,4},{6,5},{7,6},{0,7},{9,8},{10,9},{11,1... | collective-permute-start | bytes 294920 | tf_op jit(solution)/shard_map/ppermute | solution.py:485
  18.3 7.9 %copy-start.2 = (f32[2,4,96,128]{3,2,1,0:T(8,128)S(1)}, f32[2,4,96,128]{3,2,1,0:T(8,128)}, u32[]{:S(2)}) copy-start(f32[2,4,96,128]{3,2,1,0:T(8,128)} %project.1.partial) | copy-start | bytes 1179652
  26.3 26.3 %copy-start.5 = (s32[4]{0:T(128)S(1)}, s32[4]{0:T(128)}, u32[]{:S(2)}) copy-start(s32[4]{0:T(128)} %constant.78.clone) | copy-start | bytes 52
  34.1 16.3 %collective-permute-start.4 = (f32[64,8,128]{2,1,0:T(8,128)S(1)}, f32[64,8,128]{2,1,0:T(8,128)S(1)}, u32[]{:S(2)}, u32[]{:S(2)}) collective-permute-start(f32[64,8,128]{2,1,0:T(8,128)S(1)} %bitcast.25), channel_id=1, source_target_pairs={{0,24},{1,97},{2,26},{3,99},{4,28},{5,101},{6,30},{7,103},{8,0},{9... | collective-permute-start | bytes 786440 | tf_op jit(solution)/shard_map/ppermute | solution.py:444
  36.9 13.5 %collective-permute-start.3 = (f32[64,8,128]{2,1,0:T(8,128)S(1)}, f32[64,8,128]{2,1,0:T(8,128)S(1)}, u32[]{:S(2)}, u32[]{:S(2)}) collective-permute-start(f32[64,8,128]{2,1,0:T(8,128)S(1)} %bitcast.26), channel_id=1, source_target_pairs={{0,8},{1,33},{2,10},{3,35},{4,12},{5,37},{6,14},{7,39},{8,16},{9,4... | collective-permute-start | bytes 786440 | tf_op jit(solution)/shard_map/ppermute | solution.py:444
  36.9 13.5 %collective-permute-start.2 = (f32[64,8,128]{2,1,0:T(8,128)S(1)}, f32[64,8,128]{2,1,0:T(8,128)S(1)}, u32[]{:S(2)}, u32[]{:S(2)}) collective-permute-start(f32[64,8,128]{2,1,0:T(8,128)S(1)} %bitcast.27), channel_id=1, source_target_pairs={{0,16},{1,65},{2,18},{3,67},{4,20},{5,69},{6,22},{7,71},{8,24},{9,... | collective-permute-start | bytes 786440 | tf_op jit(solution)/shard_map/ppermute | solution.py:444
  50.5 3.9 %copy-start = (f32[4,64,8,128]{3,2,1,0:T(8,128)}, f32[4,64,8,128]{3,2,1,0:T(8,128)S(1)}, u32[]{:S(2)}) copy-start(f32[4,64,8,128]{3,2,1,0:T(8,128)S(1)} %pad_maximum_fusion.own.refs_0_.refs_1_) | copy-start | bytes 3145732
  50.5 26.2 %collective-permute-start.5 = (f32[4,64,8,128]{3,2,1,0:T(8,128)S(1)}, f32[4,64,8,128]{3,2,1,0:T(8,128)S(1)}, u32[]{:S(2)}, u32[]{:S(2)}) collective-permute-start(f32[4,64,8,128]{3,2,1,0:T(8,128)S(1)} %pad_maximum_fusion.own.refs_0_.refs_1_), channel_id=1, source_target_pairs={{0,96},{1,25},{2,98},{3,27},{4,100},{5,29},{6,102},{7,31},{8,104},... | collective-permute-start | bytes 3145736 | tf_op jit(solution)/shard_map/ppermute | solution.py:446
  51.8 27.3 %collective-permute-start.6 = (f32[4,64,8,128]{3,2,1,0:T(8,128)S(1)}, f32[4,64,8,128]{3,2,1,0:T(8,128)S(1)}, u32[]{:S(2)}, u32[]{:S(2)}) collective-permute-start(f32[4,64,8,128]{3,2,1,0:T(8,128)S(1)} %pad_maximum_fusion.own.refs_0_.refs_1_), channel_id=1, source_target_pairs={{0,64},{1,17},{2,66},{3,19},{4,68},{5,21},{6,70},{7,23},{8,72},{9,... | collective-permute-start | bytes 3145736 | tf_op jit(solution)/shard_map/ppermute | solution.py:446
  52.6 26.4 %collective-permute-start.7 = (f32[4,64,8,128]{3,2,1,0:T(8,128)S(1)}, f32[4,64,8,128]{3,2,1,0:T(8,128)}, u32[]{:S(2)}, u32[]{:S(2)}) collective-permute-start(f32[4,64,8,128]{3,2,1,0:T(8,128)S(1)} %pad_maximum_fusion.own.refs_0_.refs_1_), channel_id=1, source_target_pairs={{0,32},{1,9},{2,34},{3,11},{4,36},{5,13},{6,38},{7,15},{8,40},{9,1... | collective-permute-start | bytes 3145736 | tf_op jit(solution)/shard_map/ppermute | solution.py:446
  53.7 0.7 copy-start.4
  54.4 22.3 %copy-start.3 = (s32[16,32]{1,0:T(8,128)S(1)}, s32[16,32]{1,0:T(8,128)}, u32[]{:S(2)}) copy-start(s32[16,32]{1,0:T(8,128)} %slice.26.shears) | copy-start | bytes 6148
  76.7 1.2 %copy-start.1 = (f32[4,64,8,128]{3,2,1,0:T(8,128)S(1)}, f32[4,64,8,128]{3,2,1,0:T(8,128)}, u32[]{:S(2)}) copy-start(f32[4,64,8,128]{3,2,1,0:T(8,128)} %copy-done) | copy-start | bytes 3145732
  81.2 16.7 %collective-permute-start.8 = (f32[16,16,8,128]{3,2,1,0:T(8,128)}, f32[16,16,8,128]{3,2,1,0:T(8,128)S(1)}, u32[]{:S(2)}, u32[]{:S(2)}) collective-permute-start(f32[16,16,8,128]{3,2,1,0:T(8,128)} %get-tuple-element.29), channel_id=1, source_target_pairs={{0,1},{1,2},{2,3},{3,4},{4,5},{5,6},{6,7},{7,0},{8,9},{9,10},{10,1... | collective-permute-start | bytes 3145736 | tf_op jit(solution)/shard_map/ppermute | solution.py:563
  84.9 14.7 %collective-permute-start.9 = (f32[16,16,8,128]{3,2,1,0:T(8,128)}, f32[16,16,8,128]{3,2,1,0:T(8,128)}, u32[]{:S(2)}, u32[]{:S(2)}) collective-permute-start(f32[16,16,8,128]{3,2,1,0:T(8,128)} %get-tuple-element.30), channel_id=1, source_target_pairs={{1,0},{2,1},{3,2},{4,3},{5,4},{6,5},{7,6},{0,7},{9,8},{10,9},{11,1... | collective-permute-start | bytes 3145736 | tf_op jit(solution)/shard_map/ppermute | solution.py:563

commit v6 on v5

--- a/solution.py
+++ b/solution.py
@@ -477,7 +477,7 @@
         cost_estimate=cost(7),
         name="project",
     )(shears[0], object_field)
-    step = 4
+    step = 8
     count = FRAMES
     up = [(i, (i + 1) % count) for i in range(count)]
     down = [(j, i) for i, j in up]

time: 106 us -> 105 us (level)
  transfers between devices with their start and end apart: 11 -> 11, of which waited for: 2 -> 3; matrix products, arithmetic and copies ran while one was open for 3% -> 3% of each run, Pallas kernels for 45% -> 44%
where the time goes in v6:
time: 105 us
  Pallas kernels  64.8 us (62%)
  starting transfers between devices  19.5 us (19%)
  blocking collectives  11.8 us (11%)
  waiting for transfers between devices  4.44 us (4%)
  local copies, waits for them, and re-layouts  3.91 us (4%)
    pallas_call x1, Pallas kernels, per_device(): pl.pallas_call(divisor_kernel, grid=(Z // step,), out_shape=[jax.ShapeDty...  21.3 us
    pallas_call x1, Pallas kernels, per_device(): pl.pallas_call(core_kernel, grid=(Z // step,), out_shape=jax.ShapeDtypeSt...  12.3 us
    all_to_all x1, blocking collectives, gather_angles(): facts = lax.all_to_all(facts, 'angle', 0, 0)[:, 0]  11.8 us
    pallas_call x1, Pallas kernels, per_device(): pl.pallas_call(frames_kernel, out_shape=[jax.ShapeDtypeStruct((STRIP * BL...  7.81 us
    all_to_all x1, starting transfers between devices, per_device(): observed = lax.all_to_all(moved, 'block', 0, 0)  6.82 us
    pallas_call x1, Pallas kernels, per_device(): pl.pallas_call(project_kernel, grid=(Z // step,), out_shape=jax.ShapeDtyp...  6.02 us
    pallas_call x1, Pallas kernels, per_device(): pl.pallas_call(fields_kernel, grid=(3,), out_shape=jax.ShapeDtypeStruct((...  5.78 us
    pallas_call x1, Pallas kernels, per_device(): pl.pallas_call(rim_kernel, grid=(2, Z // many), out_shape=jax.ShapeDtypeS...  5.51 us
  transfers between devices with their start and end apart: 11, of which 3 were waited for; matrix products, arithmetic and copies ran while one was open for 3% of the time, Pallas kernels for 44%

profile of v6, /device:TPU:1, one launch (start us, length us, event | category | flops | bytes accessed | tf_op | source)
XLA Modules:
  0.0 104.9 jit_solution(17939392875293600927)
XLA Ops:
  0.0 0.0 copy-start.6
  0.0 2.9 %measured_rows.1 = f32[8,4,72,128]{3,2,1,0:T(8,128)} custom-call(s32[2]{0:T(128)} %bitcast.40, bf16[512,512]{1,0:T(8,128)(2,1)} %bitcast.33), custom_call_target="tpu_custom_call" | custom-call | bytes 9000000 | tf_op jit(solution)/shard_map/measured_rows/pallas_call | solution.py:458
  2.9 6.8 %all-to-all-start = ((f32[8,4,72,128]{3,2,1,0:T(8,128)}), f32[8,4,72,128]{3,2,1,0:T(8,128)S(1)}, u32[]{:S(2)}, u32[]{:S(2)}) async-start(f32[8,4,72,128]{3,2,1,0:T(8,128)} %measured_rows.1), calls=%async_computation | async-start | bytes 2359296 | tf_op jit(solution)/shard_map/all_to_all | solution.py:468
  9.7 6.0 %project.1.partial = f32[2,4,96,128]{3,2,1,0:T(8,128)} custom-call(s32[32]{0:T(128)} %bitcast.41, f32[32,2,64,512]{3,2,1,0:T(8,128)} %slices.3), custom_call_target="tpu_custom_call" | custom-call | bytes 21000000 | tf_op jit(solution)/shard_map/project/pallas_call | solution.py:470
  15.7 1.0 fusion.9
  16.7 1.6 %collective-permute-start = (f32[2,4,24,128]{3,2,1,0:T(8,128)S(1)}, f32[2,4,24,128]{3,2,1,0:T(8,128)S(1)}, u32[]{:S(2)}, u32[]{:S(2)}) collective-permute-start(f32[2,4,24,128]{3,2,1,0:T(8,128)S(1)} %get-tuple-element.34), channel_id=1, source_target_pairs={{0,1},{1,2},{2,3},{3,4},{4,5},{5,6},{6,7},{7,0},{8,9},{9,10},{10,1... | collective-permute-start | bytes 294920 | tf_op jit(solution)/shard_map/ppermute | solution.py:484
  18.3 0.0 collective-permute-start.1
  18.3 0.0 copy-done.6
  18.3 0.0 copy-start.2
  18.4 5.8 %fields.1 = f32[48,4,608,128]{3,2,1,0:T(8,128)} custom-call(f32[2,512,512]{2,1,0:T(8,128)} %probe.3, f32[512,512]{1,0:T(8,128)} %bitcast.31), custom_call_target="tpu_custom_call" | custom-call | bytes 18000000 | tf_op jit(solution)/shard_map/fields/pallas_call | solution.py:486
  24.1 0.1 pad.4.facts
  24.2 0.0 collective-permute-done.before
  24.2 2.1 %collective-permute-done.1.after = f32[2,4,24,128]{3,2,1,0:T(8,128)S(1)} collective-permute-done((f32[2,4,24,128]{3,2,1,0:T(8,128)S(1)}, f32[2,4,24,128]{3,2,1,0:T(8,128)S(1)}, u32[]{:S(2)}, u32[]{:S(2)}) %collective-permute-start.1) | collective-permute-done | bytes 98336 | tf_op jit(solution)/shard_map/ppermute | solution.py:485
  26.3 0.0 all-to-all-done.measured
  26.3 0.0 copy-done.2
  26.3 0.0 copy-start.5
  26.3 7.8 %frames.1 = (f32[512,128]{1,0:T(8,128)S(1)}, f32[128,128]{1,0:T(8,128)S(1)}) custom-call(s32[1]{0:T(128)} %bitcast.strip_index, f32[2,4,96,128]{3,2,1,0:T(8,128)S(1)} %copy-done.2, f32[2,4,24,128]{3,2,1,0:T(8,128)S(1)} %collective-permute-done.before, f32[2,4,24,128]{3,2,1,0:T(8,128)S(1)} %collective-permute-done.1.after, ...), custom_call_target="tpu_custom_call" | custom-call | bytes 27000000 | tf_op jit(solution)/shard_map/frames/pallas_call | solution.py:503
  34.1 2.8 %collective-permute-start.4 = (f32[64,8,128]{2,1,0:T(8,128)S(1)}, f32[64,8,128]{2,1,0:T(8,128)S(1)}, u32[]{:S(2)}, u32[]{:S(2)}) collective-permute-start(f32[64,8,128]{2,1,0:T(8,128)S(1)} %bitcast.25), channel_id=1, source_target_pairs={{0,24},{1,97},{2,26},{3,99},{4,28},{5,101},{6,30},{7,103},{8,0},{9... | collective-permute-start | bytes 786440 | tf_op jit(solution)/shard_map/ppermute | solution.py:444
  36.9 0.0 collective-permute-start.3
  36.9 1.6 %collective-permute-start.2 = (f32[64,8,128]{2,1,0:T(8,128)S(1)}, f32[64,8,128]{2,1,0:T(8,128)S(1)}, u32[]{:S(2)}, u32[]{:S(2)}) collective-permute-start(f32[64,8,128]{2,1,0:T(8,128)S(1)} %bitcast.27), channel_id=1, source_target_pairs={{0,16},{1,65},{2,18},{3,67},{4,20},{5,69},{6,22},{7,71},{8,24},{9,... | collective-permute-start | bytes 786440 | tf_op jit(solution)/shard_map/ppermute | solution.py:444
  38.6 11.8 %all_to_all.10 = f32[16,8,128]{2,1,0:T(8,128)S(1)} all-to-all(f32[16,8,128]{2,1,0:T(8,128)S(1)} %bitcast.30), channel_id=1, replica_groups=mesh['angle'=16,'block'=8] {'angle'}, dimensions={0} | all-to-all | bytes 131072 | tf_op jit(solution)/shard_map/all_to_all | solution.py:443
  50.4 0.0 collective-permute-done.4
  50.4 0.0 collective-permute-done.3
  50.4 0.0 collective-permute-done.2
  50.4 0.1 pad_maximum_fusion.own.refs_0_.refs_1_
  50.5 0.0 copy-start
  50.5 1.3 %collective-permute-start.5 = (f32[4,64,8,128]{3,2,1,0:T(8,128)S(1)}, f32[4,64,8,128]{3,2,1,0:T(8,128)S(1)}, u32[]{:S(2)}, u32[]{:S(2)}) collective-permute-start(f32[4,64,8,128]{3,2,1,0:T(8,128)S(1)} %pad_maximum_fusion.own.refs_0_.refs_1_), channel_id=1, source_target_pairs={{0,96},{1,25},{2,98},{3,27},{4,100},{5,29},{6,102},{7,31},{8,104},... | collective-permute-start | bytes 3145736 | tf_op jit(solution)/shard_map/ppermute | solution.py:446
  51.8 0.8 collective-permute-start.6
  52.6 0.0 collective-permute-start.7
  52.6 0.0 copy-done.5
  52.6 0.1 select_subtract_fusion.1
  52.7 0.1 sub.56
  52.7 0.1 sub.54
  52.8 0.1 sub.55
  52.9 0.1 sub.51
  53.1 0.6 gather_fusion
  53.6 0.1 broadcast_select_fusion
  53.7 0.0 copy-start.4
  53.7 0.7 slice.26.shears
  54.4 0.0 copy-start.3
  54.4 0.0 copy-done
  54.4 0.0 copy-done.4
  54.4 21.3 %divisor.1 = (f32[32,64,512]{2,1,0:T(8,128)}, f32[32,2,64,512]{3,2,1,0:T(8,128)}) custom-call(s32[1]{0:T(128)} %bitcast.strip_index, s32[16,16]{1,0:T(8,128)} %bitcast.37, s32[16,32]{1,0:T(8,128)} %slice.26.shears, f32[2,512,512]{2,1,0:T(8,128)} %probe.3, f32[4,64,8,128]{3,2,1,0:T(8,128)} %copy-done, f32[32,2,64,512]{3,2,1,0:T(8,128)} %slices.3), custom_call_target="tpu_custom_call" | custom-call | bytes 6000000 | tf_op jit(solution)/shard_map/divisor/pallas_call | solution.py:538
  75.7 0.0 copy-done.3
  75.7 0.0 collective-permute-done.5.refs_2_.refs_3_.three
  75.7 0.0 copy-start.1
  75.7 1.2 %copy-done.1 = f32[4,64,8,128]{3,2,1,0:T(8,128)S(1)} copy-done((f32[4,64,8,128]{3,2,1,0:T(8,128)S(1)}, f32[4,64,8,128]{3,2,1,0:T(8,128)}, u32[]{:S(2)}) %copy-start.1) | copy-done | bytes 1048600
  76.9 1.1 %pack.2 = (f32[16,16,8,128]{3,2,1,0:T(8,128)}, f32[16,16,8,128]{3,2,1,0:T(8,128)}) custom-call(f32[4,64,8,128]{3,2,1,0:T(8,128)S(1)} %copy-done.1, f32[4,64,8,128]{3,2,1,0:T(8,128)S(1)} %copy-done.1, f32[4,64,8,128]{3,2,1,0:T(8,128)S(1)} %collective-permute-done.5.refs_2_.refs_3_.three, f32[4,64,8,128]{3,2,1,0:T(8,128)S(1)} %collective-permute-done.5.refs_2_.refs_3_.three), custom_call_target="tpu_custom_call" | custom-call | bytes 3000000 | tf_op jit(solution)/shard_map/pack/pallas_call | solution.py:344
  78.0 0.0 collective-permute-done.6.refs_0_.refs_1_.two
  78.0 0.5 collective-permute-done.7.refs_2_.refs_3_.one
  78.5 2.1 %pack.3 = (f32[16,16,8,128]{3,2,1,0:T(8,128)}, f32[16,16,8,128]{3,2,1,0:T(8,128)}) custom-call(f32[4,64,8,128]{3,2,1,0:T(8,128)S(1)} %collective-permute-done.6.refs_0_.refs_1_.two, f32[4,64,8,128]{3,2,1,0:T(8,128)S(1)} %collective-permute-done.6.refs_0_.refs_1_.two, ...), custom_call_target="tpu_custom_call", output_to_operand_aliasing={{0}: (4, {}), {1}: (5, {})} | custom-call | bytes 3000000 | tf_op jit(solution)/shard_map/pack/pallas_call | solution.py:344
  80.6 4.0 %collective-permute-start.8 = (f32[16,16,8,128]{3,2,1,0:T(8,128)}, f32[16,16,8,128]{3,2,1,0:T(8,128)S(1)}, u32[]{:S(2)}, u32[]{:S(2)}) collective-permute-start(f32[16,16,8,128]{3,2,1,0:T(8,128)} %get-tuple-element.29), channel_id=1, source_target_pairs={{0,1},{1,2},{2,3},{3,4},{4,5},{5,6},{6,7},{7,0},{8,9},{9,10},{10,1... | collective-permute-start | bytes 3145736 | tf_op jit(solution)/shard_map/ppermute | solution.py:563
  84.6 0.5 collective-permute-start.9
  85.1 0.1 copy.18.shears
  85.2 12.3 %core.1 = f32[32,2,64,512]{3,2,1,0:T(8,128)} custom-call(s32[16,32]{1,0:T(8,128)S(1)} %copy-done.3, f32[4,64,8,128]{3,2,1,0:T(8,128)S(1)} %collective-permute-done.6.refs_0_.refs_1_.two, f32[4,64,8,128]{3,2,1,0:T(8,128)} %collective-permute-done.7.refs_2_.refs_3_.one, f32[4,64,8,128]{3,2,1,0:T(8,128)S(1)} %collective-permute-done.5.refs_2_.refs_3_.three, ...), custom_call_target="tpu_custom_call" | custom-call | bytes 51000000 | tf_op jit(solution)/shard_map/core/pallas_call | solution.py:570
  97.5 0.0 collective-permute-done.8
  97.5 1.8 %collective-permute-done.9 = f32[16,16,8,128]{3,2,1,0:T(8,128)} collective-permute-done((f32[16,16,8,128]{3,2,1,0:T(8,128)}, f32[16,16,8,128]{3,2,1,0:T(8,128)}, u32[]{:S(2)}, u32[]{:S(2)}) %collective-permute-start.9) | collective-permute-done | bytes 1048608 | tf_op jit(solution)/shard_map/ppermute | solution.py:563
  99.4 5.5 %rim.1 = f32[32,2,64,512]{3,2,1,0:T(8,128)} custom-call(s32[32,256]{1,0:T(8,128)S(1)} %copy.18.shears, f32[2048,128]{1,0:T(8,128)S(1)} %bitcast.24, f32[2048,128]{1,0:T(8,128)} %bitcast.18.after, f32[32,64,512]{2,1,0:T(8,128)} %get-tuple-element.31.scale, f32[32,2,64,512]{3,2,1,0:T(8,128)} %core.1), custom_call_target="tpu_custom_call", output_to_operand_aliasing={{}: (4, {})} | custom-call | bytes 27000000 | tf_op jit(solution)/shard_map/rim/pallas_call | solution.py:586
  (8 shorter events, 0.1 us)
Async XLA Ops:
  0.0 18.3 %copy-start.6 = (s32[1,32]{1,0:T(1,128)S(1)}, s32[1,32]{1,0:T(1,128)}, u32[]{:S(2)}) copy-start(s32[1,32]{1,0:T(1,128)} %param.9) | copy-start | bytes 388
  2.9 23.4 %all-to-all-start = ((f32[8,4,72,128]{3,2,1,0:T(8,128)}), f32[8,4,72,128]{3,2,1,0:T(8,128)S(1)}, u32[]{:S(2)}, u32[]{:S(2)}) async-start(f32[8,4,72,128]{3,2,1,0:T(8,128)} %measured_rows.1), calls=%async_computation | async-start | bytes 2359296 | tf_op jit(solution)/shard_map/all_to_all | solution.py:468
  16.7 7.5 %collective-permute-start = (f32[2,4,24,128]{3,2,1,0:T(8,128)S(1)}, f32[2,4,24,128]{3,2,1,0:T(8,128)S(1)}, u32[]{:S(2)}, u32[]{:S(2)}) collective-permute-start(f32[2,4,24,128]{3,2,1,0:T(8,128)S(1)} %get-tuple-element.34), channel_id=1, source_target_pairs={{0,1},{1,2},{2,3},{3,4},{4,5},{5,6},{6,7},{7,0},{8,9},{9,10},{10,1... | collective-permute-start | bytes 294920 | tf_op jit(solution)/shard_map/ppermute | solution.py:484
  18.3 8.0 %collective-permute-start.1 = (f32[2,4,24,128]{3,2,1,0:T(8,128)S(1)}, f32[2,4,24,128]{3,2,1,0:T(8,128)S(1)}, u32[]{:S(2)}, u32[]{:S(2)}) collective-permute-start(f32[2,4,24,128]{3,2,1,0:T(8,128)S(1)} %get-tuple-element.33), channel_id=1, source_target_pairs={{1,0},{2,1},{3,2},{4,3},{5,4},{6,5},{7,6},{0,7},{9,8},{10,9},{11,1... | collective-permute-start | bytes 294920 | tf_op jit(solution)/shard_map/ppermute | solution.py:485
  18.3 7.9 %copy-start.2 = (f32[2,4,96,128]{3,2,1,0:T(8,128)S(1)}, f32[2,4,96,128]{3,2,1,0:T(8,128)}, u32[]{:S(2)}) copy-start(f32[2,4,96,128]{3,2,1,0:T(8,128)} %project.1.partial) | copy-start | bytes 1179652
  26.3 26.3 %copy-start.5 = (s32[4]{0:T(128)S(1)}, s32[4]{0:T(128)}, u32[]{:S(2)}) copy-start(s32[4]{0:T(128)} %constant.78.clone) | copy-start | bytes 52
  34.1 16.3 %collective-permute-start.4 = (f32[64,8,128]{2,1,0:T(8,128)S(1)}, f32[64,8,128]{2,1,0:T(8,128)S(1)}, u32[]{:S(2)}, u32[]{:S(2)}) collective-permute-start(f32[64,8,128]{2,1,0:T(8,128)S(1)} %bitcast.25), channel_id=1, source_target_pairs={{0,24},{1,97},{2,26},{3,99},{4,28},{5,101},{6,30},{7,103},{8,0},{9... | collective-permute-start | bytes 786440 | tf_op jit(solution)/shard_map/ppermute | solution.py:444
  36.9 13.5 %collective-permute-start.3 = (f32[64,8,128]{2,1,0:T(8,128)S(1)}, f32[64,8,128]{2,1,0:T(8,128)S(1)}, u32[]{:S(2)}, u32[]{:S(2)}) collective-permute-start(f32[64,8,128]{2,1,0:T(8,128)S(1)} %bitcast.26), channel_id=1, source_target_pairs={{0,8},{1,33},{2,10},{3,35},{4,12},{5,37},{6,14},{7,39},{8,16},{9,4... | collective-permute-start | bytes 786440 | tf_op jit(solution)/shard_map/ppermute | solution.py:444
  36.9 13.5 %collective-permute-start.2 = (f32[64,8,128]{2,1,0:T(8,128)S(1)}, f32[64,8,128]{2,1,0:T(8,128)S(1)}, u32[]{:S(2)}, u32[]{:S(2)}) collective-permute-start(f32[64,8,128]{2,1,0:T(8,128)S(1)} %bitcast.27), channel_id=1, source_target_pairs={{0,16},{1,65},{2,18},{3,67},{4,20},{5,69},{6,22},{7,71},{8,24},{9,... | collective-permute-start | bytes 786440 | tf_op jit(solution)/shard_map/ppermute | solution.py:444
  50.5 3.9 %copy-start = (f32[4,64,8,128]{3,2,1,0:T(8,128)}, f32[4,64,8,128]{3,2,1,0:T(8,128)S(1)}, u32[]{:S(2)}) copy-start(f32[4,64,8,128]{3,2,1,0:T(8,128)S(1)} %pad_maximum_fusion.own.refs_0_.refs_1_) | copy-start | bytes 3145732
  50.5 25.2 %collective-permute-start.5 = (f32[4,64,8,128]{3,2,1,0:T(8,128)S(1)}, f32[4,64,8,128]{3,2,1,0:T(8,128)S(1)}, u32[]{:S(2)}, u32[]{:S(2)}) collective-permute-start(f32[4,64,8,128]{3,2,1,0:T(8,128)S(1)} %pad_maximum_fusion.own.refs_0_.refs_1_), channel_id=1, source_target_pairs={{0,96},{1,25},{2,98},{3,27},{4,100},{5,29},{6,102},{7,31},{8,104},... | collective-permute-start | bytes 3145736 | tf_op jit(solution)/shard_map/ppermute | solution.py:446
  51.8 26.3 %collective-permute-start.6 = (f32[4,64,8,128]{3,2,1,0:T(8,128)S(1)}, f32[4,64,8,128]{3,2,1,0:T(8,128)S(1)}, u32[]{:S(2)}, u32[]{:S(2)}) collective-permute-start(f32[4,64,8,128]{3,2,1,0:T(8,128)S(1)} %pad_maximum_fusion.own.refs_0_.refs_1_), channel_id=1, source_target_pairs={{0,64},{1,17},{2,66},{3,19},{4,68},{5,21},{6,70},{7,23},{8,72},{9,... | collective-permute-start | bytes 3145736 | tf_op jit(solution)/shard_map/ppermute | solution.py:446
  52.6 26.0 %collective-permute-start.7 = (f32[4,64,8,128]{3,2,1,0:T(8,128)S(1)}, f32[4,64,8,128]{3,2,1,0:T(8,128)}, u32[]{:S(2)}, u32[]{:S(2)}) collective-permute-start(f32[4,64,8,128]{3,2,1,0:T(8,128)S(1)} %pad_maximum_fusion.own.refs_0_.refs_1_), channel_id=1, source_target_pairs={{0,32},{1,9},{2,34},{3,11},{4,36},{5,13},{6,38},{7,15},{8,40},{9,1... | collective-permute-start | bytes 3145736 | tf_op jit(solution)/shard_map/ppermute | solution.py:446
  53.7 0.7 copy-start.4
  54.4 21.3 %copy-start.3 = (s32[16,32]{1,0:T(8,128)S(1)}, s32[16,32]{1,0:T(8,128)}, u32[]{:S(2)}) copy-start(s32[16,32]{1,0:T(8,128)} %slice.26.shears) | copy-start | bytes 6148
  75.7 1.2 %copy-start.1 = (f32[4,64,8,128]{3,2,1,0:T(8,128)S(1)}, f32[4,64,8,128]{3,2,1,0:T(8,128)}, u32[]{:S(2)}) copy-start(f32[4,64,8,128]{3,2,1,0:T(8,128)} %copy-done) | copy-start | bytes 3145732
  80.6 16.9 %collective-permute-start.8 = (f32[16,16,8,128]{3,2,1,0:T(8,128)}, f32[16,16,8,128]{3,2,1,0:T(8,128)S(1)}, u32[]{:S(2)}, u32[]{:S(2)}) collective-permute-start(f32[16,16,8,128]{3,2,1,0:T(8,128)} %get-tuple-element.29), channel_id=1, source_target_pairs={{0,1},{1,2},{2,3},{3,4},{4,5},{5,6},{6,7},{7,0},{8,9},{9,10},{10,1... | collective-permute-start | bytes 3145736 | tf_op jit(solution)/shard_map/ppermute | solution.py:563
  84.6 14.7 %collective-permute-start.9 = (f32[16,16,8,128]{3,2,1,0:T(8,128)}, f32[16,16,8,128]{3,2,1,0:T(8,128)}, u32[]{:S(2)}, u32[]{:S(2)}) collective-permute-start(f32[16,16,8,128]{3,2,1,0:T(8,128)} %get-tuple-element.30), channel_id=1, source_target_pairs={{1,0},{2,1},{3,2},{4,3},{5,4},{6,5},{7,6},{0,7},{9,8},{10,9},{11,1... | collective-permute-start | bytes 3145736 | tf_op jit(solution)/shard_map/ppermute | solution.py:563
